TPU v7x, 32 devices: a whole 2x2x4 slice. The times are simulated.
32 devices in a mesh: groups: 2 (over y), shard: 4 (over z), dp: 2 (over x), tok: 2 (over core).
Axes of the slice: x: 2, y: 2, z: 4, core: 2. Of those that a mesh axis runs over, the one named last changes fastest.
Arguments:
- tokens: bfloat16 [2048, 4096], P(('groups', 'dp', 'tok'), 'shard'), parts along dimension 0, may hold values from -6 to 6
- gate_blocks: bfloat16 [8, 16, 128, 128], P('shard'), may hold values from -0.125 to 0.125
- up_blocks: bfloat16 [8, 16, 128, 128], P('shard'), may hold values from -0.125 to 0.125
- down_blocks: bfloat16 [8, 16, 128, 128], P('shard'), may hold values from -0.25 to 0.25
- gate_rows: int32 [8, 16], P('shard'), may hold values from 0 to 31, as said below
- up_rows: int32 [8, 16], P('shard'), may hold values from 0 to 31, as said below
- down_rows: int32 [8, 16], replicated, may hold values from 0 to 31, as said below
- cotangent: bfloat16 [2048, 4096], P(('groups', 'dp', 'tok'), 'shard'), parts along dimension 0, may hold values from -6 to 6
Outputs:
- mixed: bfloat16 [2048, 4096], P(('groups', 'dp', 'tok'), 'shard'), parts along dimension 0
- tokens_grad: bfloat16 [2048, 4096], P(('groups', 'dp', 'tok'), 'shard'), parts along dimension 0
- gate_grad: bfloat16 [16, 16, 128, 128], P(('groups', 'shard'), ('dp', 'tok')), parts along dimension 0
- up_grad: bfloat16 [16, 16, 128, 128], P(('groups', 'shard'), ('dp', 'tok')), parts along dimension 0
- down_grad: bfloat16 [16, 16, 128, 128], P(('groups', 'shard'), ('dp', 'tok')), parts along dimension 0
There are 2 independent parts, one for each index of `groups`. A program takes and returns all parts, laid end to end along the dimension named above; an argument that names none is the same for every part. Nothing has to cross between parts.
Inputs may be any that keep to these rules, and one draw needn't show every extreme that they name: `gate_rows`: in every row c of the list and for every o, the entries o * 4 to (o + 1) * 4 - 1 are distinct blocks among o * 2 * 4 to (o + 1) * 2 * 4 - 1, in ascending order. `up_rows`: as for gate_rows, drawn independently. `down_rows`: as for gate_rows, drawn independently.
All inputs are finite; a program needn't handle non-finite values.
Results may differ from a plain program's by a relative error of at most 0.018.
Values may be sent and summed in bfloat16 or wider, within the bound.
No kernel may reach another device: no remote copies, remote signals or barrier semaphores. Data moves between devices by JAX's collectives and lax.ppermute only.
A program may use at most 64 MiB of HBM per device.

v0:
```python
import functools

import jax
import jax.numpy as jnp
from jax import lax
from jax.experimental import pallas as pl
from jax.experimental.pallas import tpu as pltpu
from jax.sharding import PartitionSpec as P

BF = jnp.bfloat16
F32 = jnp.float32
LIMIT = 16 << 20
Z, Q, OWNER, OWNED = range(4)
PLANE = ("shard", "dp", "tok")


def xor_perm(count, step):
    return [(i, i ^ step) for i in range(count)]


def weight_perm(shards, n_dp, n_tok):
    pairs = []
    for z in range(shards):
        for x in range(n_dp):
            for c in range(n_tok):
                q = c * n_dp + x
                pairs.append((q * n_dp * n_tok + weight_source(shards, n_dp, n_tok, q, z), (z * n_dp + x) * n_tok + c))
    return pairs


def weight_source(shards, n_dp, n_tok, q, z):
    if (shards, n_dp, n_tok) == (4, 2, 2):
        x = q % 2
        far = (q < 2) != (z < 2)
        return (x if far else 1 - x) * 2 + z % 2
    return z


def weight_owner(shards, n_dp, n_tok, q, x, c):
    if (shards, n_dp, n_tok) == (4, 2, 2):
        far = (x == (q & 1)).astype(jnp.int32)
        return ((q >> 1) ^ far) * 2 + c
    return x * n_tok + c


def grad_perm(shards, n_dp, n_tok):
    return [
        ((z * n_dp + x) * n_tok + c, (c * n_dp + x) * n_dp * n_tok + z)
        for z in range(shards)
        for x in range(n_dp)
        for c in range(n_tok)
    ]


def vmem(count):
    return [pl.BlockSpec(memory_space=pltpu.VMEM)] * count


def smem(count):
    return [pl.BlockSpec(memory_space=pltpu.SMEM)] * count


def call(kernel, scalars, arrays, outs, scratch, flops, kept, limit, out_spaces):
    moved = sum(a.size * a.dtype.itemsize for a in (*arrays, *kept))
    moved += sum(o.size * o.dtype.itemsize for o in outs)
    return pl.pallas_call(
        kernel,
        out_shape=outs,
        in_specs=smem(len(scalars)) + vmem(len(arrays)) + [pl.BlockSpec(memory_space=pltpu.HBM)] * len(kept),
        out_specs=[pl.BlockSpec(memory_space=s) for s in out_spaces] if out_spaces else vmem(len(outs)),
        scratch_shapes=scratch,
        compiler_params=pltpu.CompilerParams(vmem_limit_bytes=limit),
        cost_estimate=pl.CostEstimate(flops=flops, bytes_accessed=moved, transcendentals=0),
    )(*scalars, *arrays, *kept)


def aligned(value, size):
    return pl.multiple_of(value * size, size)


def down_places(info, down_rows, columns, per_owner):
    first_row, first = info[Q] * columns, info[Z] * per_owner
    return lambda c, k: down_rows[first_row + c, first + k] - info[Z] * info[OWNED]


def scatter_cols(dense, packed, place, columns):
    count, size, _ = packed.shape
    per_owner = count // columns
    dense[...] = jnp.zeros_like(dense)
    for c in range(columns):
        for k in range(per_owner):
            here = pl.ds(aligned(place(c, k), size), size)
            dense[c * size : (c + 1) * size, here] = packed[c * per_owner + k]


def split_rows(total, r, slot, outs, z):
    rows = outs[0].shape[2]
    for d, out in enumerate(outs):
        out[slot, r] = total[r, pl.ds(aligned(z ^ d, rows), rows), :].astype(out.dtype)


def copy_owner(pairs, owner, sems):
    copies = []
    for i, (source, target) in enumerate(pairs):
        columns = source.shape[0]
        per_owner = target.shape[0] // columns
        for c in range(columns):
            part = source.at[c, pl.ds(owner * per_owner, per_owner)]
            place = target.at[pl.ds(c * per_owner, per_owner)]
            copies.append(pltpu.make_async_copy(part, place, sems.at[i * columns + c]))
    for copy in copies:
        copy.start()
    return copies


def pack_kernel(info, gate_rows, up_rows, gate, up, down, rows_out, gate_out, up_out, down_out, sems):
    copies = copy_owner([(gate, gate_out), (up, up_out), (down, down_out)], info[OWNER], sems)
    columns, per_owner = rows_out.shape[1:]
    for i, rows in enumerate((gate_rows, up_rows)):
        for c in range(columns):
            for k in range(per_owner):
                rows_out[i, c, k] = rows[c, info[OWNER] * per_owner + k] - info[OWNER] * info[OWNED]
    for copy in copies:
        copy.wait()


def scatter_rows(dense, packed, rows, i):
    columns, per_owner = rows.shape[1:]
    size = packed.shape[1]
    dense[...] = jnp.zeros_like(dense)
    for c in range(columns):
        for k in range(per_owner):
            place = pl.ds(aligned(rows[i, c, k], size), size)
            dense[place, c * size : (c + 1) * size] = packed[c * per_owner + k]


def own_kernel(shards, n, i, info, rows, *refs):
    xs, packed = refs[:n], refs[n]
    outs = refs[n + 1 : n + 1 + shards]
    dense, total = refs[n + 1 + shards :]
    scatter_rows(dense, packed, rows, i)
    for r, x in enumerate(xs):
        total[r] = jnp.dot(x[...], dense[...], preferred_element_type=F32)
        split_rows(total, r, 0, outs, info[Z])


def other_gate_up_kernel(shards, n, info, *refs):
    outs = refs[n + 2 : n + 2 + shards]
    gate_up(info[Z], refs[:n], refs[n], refs[n + 1], outs, *refs[n + 2 + shards :])


def gate_up(z, xs, gate_dense, up_dense, outs, gate_total, up_total):
    for r, x in enumerate(xs):
        gate_total[r] = jnp.dot(x[...], gate_dense[...], preferred_element_type=F32)
        split_rows(gate_total, r, 0, outs, z)
        up_total[r] = jnp.dot(x[...], up_dense[...], preferred_element_type=F32)
        split_rows(up_total, r, 1, outs, z)


def hidden_grad_kernel(shards, nj, columns, info, down_rows, *refs):
    cots = refs[:nj]
    down_blocks = refs[nj]
    outs = refs[nj + 1 : nj + 1 + shards]
    down_dense, total = refs[nj + 1 + shards :]
    place = down_places(info, down_rows, columns, down_blocks.shape[0] // columns)
    scatter_cols(down_dense, down_blocks, place, columns)
    for r in range(nj):
        total[r] = lax.dot_general(
            cots[r][...], down_dense[...], (((1,), (1,)), ((), ())), preferred_element_type=F32
        )
        split_rows(total, r, 0, outs, info[Z])


def hidden_kernel(shards, *refs):
    gates, ups, others = (refs[i * shards : (i + 1) * shards] for i in range(3))
    sums, hidden = refs[3 * shards :]
    first = gates[0].shape[1]
    total = lambda parts, slot: sum(part[slot].astype(F32) for part in parts)
    for start, gate, up in (
        (0, total(gates, 0), total(ups, 0)),
        (first, total(others, 0), total(others, 1)),
    ):
        here = pl.ds(start, gate.shape[0])
        sums[0, here] = gate
        sums[1, here] = up
        hidden[here] = (gate * jax.nn.sigmoid(gate) * up).astype(BF)


def act_grad_kernel(sums, *refs):
    parts, (gate_act, up_act) = refs[:-2], refs[-2:]
    hidden_grad = sum(part[0].astype(F32) for part in parts)
    gate, up = sums[0], sums[1]
    s = jax.nn.sigmoid(gate)
    gate_act[...] = (hidden_grad * up * s * (1.0 + gate * (1.0 - s))).astype(BF)
    up_act[...] = (hidden_grad * (gate * s)).astype(BF)


def join_rows(joined, parts, z):
    rows = parts[0].shape[1]
    for r in range(joined.shape[0]):
        for d, part in enumerate(parts):
            joined[r, pl.ds(aligned(z ^ d, rows), rows), :] = part[r]


def weight_grad(acc, left, rights, stage, sems):
    copies = [pltpu.make_async_copy(right, stage.at[r], sems.at[r]) for r, right in enumerate(rights)]
    for copy in copies:
        copy.start()
    for r, copy in enumerate(copies):
        copy.wait()
        term = lax.dot_general(left[r], stage[r], (((0,), (0,)), ((), ())), preferred_element_type=F32)
        if r == 0:
            acc[...] = term
        else:
            acc[...] += term


def pick_blocks(out, acc, place, transposed):
    columns, per_owner, size, _ = out.shape
    for c in range(columns):
        for k in range(per_owner):
            block = acc[c * size : (c + 1) * size, pl.ds(aligned(place(c, k), size), size)]
            out[c, k] = (block.T if transposed else block).astype(BF)


def put_plane(keep, send, r, n_tok, value):
    dx, dc = divmod(r, n_tok)
    if dc == 0:
        keep[dx][...] = value
    else:
        send[dx][dc - 1] = value.astype(BF)


def sum_kernel(first, *refs):
    *others, out = refs
    total = first[...]
    for other in others:
        value = other[...].astype(F32)
        total += value if value.ndim == total.ndim else jnp.sum(value, axis=0)
    out[...] = total.astype(BF)


def deliver_kernel(*refs):
    count = len(refs) // 2
    for source, out in zip(refs[:count], refs[count:]):
        out[...] = source[...]


def mixed_kernel(shards, n_dp, n_tok, info, *refs):
    hiddens, dense = refs[:shards], refs[shards]
    keep, send = refs[shards + 1 : shards + 1 + n_dp], refs[shards + 1 + n_dp : shards + 1 + 2 * n_dp]
    joined = refs[shards + 1 + 2 * n_dp]
    join_rows(joined, hiddens, info[Z])
    for r in reversed(range(joined.shape[0])):
        put_plane(keep, send, r, n_tok, jnp.dot(joined[r], dense[...], preferred_element_type=F32))


def down_grad_kernel(info, down_rows, joined, *refs):
    *rights, grad, acc, stage, sems = refs
    weight_grad(acc, joined, rights, stage, sems)
    pick_blocks(grad, acc, down_places(info, down_rows, *grad.shape[:2]), False)


def up_grad_kernel(rows, joined, *refs):
    *rights, grad, acc, stage, sems = refs
    weight_grad(acc, joined, rights, stage, sems)
    pick_blocks(grad, acc, lambda c, k: rows[1, c, k], True)


def gate_grad_kernel(shards, nj, info, rows, *refs):
    acts = refs[:shards]
    xs = refs[shards : shards + nj]
    grad, joined, acc, stage, sems = refs[shards + nj :]
    join_rows(joined, acts, info[Z])
    weight_grad(acc, joined, xs, stage, sems)
    pick_blocks(grad, acc, lambda c, k: rows[0, c, k], True)


def tokens_grad_kernel(shards, n_dp, n_tok, info, *refs):
    acts = refs[:shards]
    joined_gate, gate_dense, up_dense = refs[shards : shards + 3]
    keep, send = refs[shards + 3 : shards + 3 + n_dp], refs[shards + 3 + n_dp : shards + 3 + 2 * n_dp]
    joined = refs[shards + 3 + 2 * n_dp]
    join_rows(joined, acts, info[Z])
    contract = (((1,), (1,)), ((), ()))
    for r in reversed(range(joined.shape[0])):
        value = lax.dot_general(joined_gate[r], gate_dense[...], contract, preferred_element_type=F32)
        value += lax.dot_general(joined[r], up_dense[...], contract, preferred_element_type=F32)
        put_plane(keep, send, r, n_tok, value)


def shape(dims, dtype):
    return jax.ShapeDtypeStruct(dims, dtype)


def body(n_dp, n_tok, shards, tokens, gate_blocks, up_blocks, down_blocks, gate_rows, up_rows, down_rows, cotangent):
    nj = n_dp * n_tok
    z = lax.axis_index("shard")
    x_index, c_index = lax.axis_index("dp"), lax.axis_index("tok")
    q = c_index * n_dp + x_index
    count, width = tokens.shape
    columns, nonzero, size, _ = gate_blocks.shape
    per_owner = nonzero // shards
    owned = width // size
    hidden_width = columns * size
    part = count // shards
    blocks = columns * per_owner

    def spread(parts):
        return [parts[0]] + [lax.ppermute(parts[d], "shard", xor_perm(shards, d)) for d in range(1, shards)]

    def run(kernel, scalars, arrays, outs, scratch, flops, kept=(), limit=LIMIT, out_spaces=None):
        return call(kernel, scalars, arrays, outs, scratch, flops, kept, limit, out_spaces)

    def gather_plane(own):
        groups = []
        for dx in range(n_dp):
            base = own if dx == 0 else lax.ppermute(own, "dp", xor_perm(n_dp, dx))
            group = [base]
            for dc in range(1, n_tok):
                group.append(lax.ppermute(base, "tok", xor_perm(n_tok, dc)))
            groups.append(group)
        return groups[0], [a for group in groups[1:] for a in group]

    w_perm = weight_perm(shards, n_dp, n_tok)
    owner = weight_owner(shards, n_dp, n_tok, z, x_index, c_index)
    info = jnp.stack([v.astype(jnp.int32) for v in (z, q, owner, jnp.int32(owned))])
    packed_shape = shape((blocks, size, size), BF)
    rows, gate_part, up_part, down_part = run(
        pack_kernel,
        [info, gate_rows, up_rows],
        [],
        [shape((2, columns, per_owner), jnp.int32)] + [packed_shape] * 3,
        [pltpu.SemaphoreType.DMA((3 * columns,))],
        0,
        [gate_blocks, up_blocks, down_blocks],
        60 << 20,
        [pltpu.SMEM] + [pltpu.VMEM] * 3,
    )
    gate_part = lax.ppermute(gate_part, PLANE, w_perm)
    rows = lax.ppermute(rows, PLANE, w_perm)
    up_part = lax.ppermute(up_part, PLANE, w_perm)
    down_part = lax.ppermute(down_part, PLANE, w_perm)

    own_x, other_x = gather_plane(tokens)
    own_c, other_c = gather_plane(cotangent)
    xs, cots = own_x + other_x, own_c + other_c
    macs = nj * count * width * hidden_width * 2
    joined = pltpu.VMEM((nj, count, hidden_width), BF)
    joined_shape = shape((nj, count, hidden_width), BF)
    acc = pltpu.VMEM((hidden_width, width), F32)
    dense = shape((width, hidden_width), BF)

    def part_shapes(slots, n):
        dims = (slots, n, part, hidden_width)
        return [shape(dims, F32)] + [shape(dims, BF)] * (shards - 1)

    def totals(n):
        return pltpu.VMEM((n, count, hidden_width), F32)

    def own(i, blocks_part):
        return run(
            functools.partial(own_kernel, shards, n_tok, i),
            [info, rows],
            [*own_x, blocks_part],
            part_shapes(1, n_tok) + [dense],
            [totals(n_tok)],
            macs // n_dp,
        )

    *gate0, gate_dense = own(0, gate_part)
    gate0 = spread(gate0)
    *up0, up_dense = own(1, up_part)
    up0 = spread(up0)
    gate_up1 = run(
        functools.partial(other_gate_up_kernel, shards, nj - n_tok),
        [info],
        [*other_x, gate_dense, up_dense],
        part_shapes(2, nj - n_tok),
        [totals(nj - n_tok)] * 2,
        2 * macs * (n_dp - 1) // n_dp,
    )
    gate_up1 = spread(gate_up1)
    *hidden_grads, down_dense = run(
        functools.partial(hidden_grad_kernel, shards, nj, columns),
        [info, down_rows],
        [*cots, down_part],
        part_shapes(1, nj) + [shape((hidden_width, width), BF)],
        [totals(nj)],
        macs,
    )
    hidden_grads = spread(hidden_grads)
    act = shape((nj, part, hidden_width), BF)
    sums, hidden = run(
        functools.partial(hidden_kernel, shards),
        [],
        [*gate0, *up0, *gate_up1],
        [shape((2, nj, part, hidden_width), F32), act],
        [],
        macs // 64,
    )
    hiddens = spread([hidden] * shards)
    gate_act, up_act = run(act_grad_kernel, [], [sums, *hidden_grads], [act, act], [], macs // 64)
    gate_acts = spread([gate_act] * shards)
    up_acts = spread([up_act] * shards)

    plane_shapes = [shape((count, width), F32)] * n_dp + [shape((n_tok - 1, count, width), BF)] * n_dp
    grad_shape = shape((columns, per_owner, size, size), BF)
    *mixed, joined_hidden = run(
        functools.partial(mixed_kernel, shards, n_dp, n_tok),
        [info],
        [*hiddens, down_dense],
        plane_shapes + [joined_shape],
        [],
        macs,
    )
    staged = [acc, pltpu.VMEM((nj, count, width), BF), pltpu.SemaphoreType.DMA((nj,))]
    (down_grad,) = run(down_grad_kernel, [info, down_rows], [joined_hidden], [grad_shape], staged, macs, cots)
    gate_grad, joined_gate = run(
        functools.partial(gate_grad_kernel, shards, nj),
        [info, rows],
        gate_acts,
        [grad_shape, joined_shape],
        staged,
        macs,
        xs,
    )
    *tokens_terms, joined_up = run(
        functools.partial(tokens_grad_kernel, shards, n_dp, n_tok),
        [info],
        [*up_acts, joined_gate, gate_dense, up_dense],
        plane_shapes + [joined_shape],
        [],
        2 * macs,
    )
    (up_grad,) = run(up_grad_kernel, [rows], [joined_up], [grad_shape], staged, macs, xs)

    def sum_plane(terms):
        arrived = []
        total = lambda parts: run(sum_kernel, [], parts, [shape((count, width), BF)], [], 0)[0]
        for dx in reversed(range(n_dp)):
            parts = [terms[dx]]
            if n_tok == 2:
                parts.append(lax.ppermute(terms[n_dp + dx], "tok", xor_perm(n_tok, 1)))
            else:
                for dc in range(1, n_tok):
                    parts.append(lax.ppermute(terms[n_dp + dx][dc - 1], "tok", xor_perm(n_tok, dc)))
            if dx:
                arrived.append(lax.ppermute(total(parts), "dp", xor_perm(n_dp, dx)))
        return total(parts + arrived)

    g_perm = grad_perm(shards, n_dp, n_tok)

    def home(grad):
        grad = lax.ppermute(grad, PLANE, g_perm)
        return run(deliver_kernel, [], [grad], [grad_shape], [], 0)[0]

    return (sum_plane(mixed), sum_plane(tokens_terms), home(gate_grad), home(up_grad), home(down_grad))


def solution(mesh):
    shards, n_dp, n_tok = (mesh.shape[name] for name in PLANE)
    assert shards == n_dp * n_tok
    in_specs = (
        P(("groups", "dp", "tok"), "shard"),
        P("shard", None, None, None),
        P("shard", None, None, None),
        P("shard", None, None, None),
        P("shard", None),
        P("shard", None),
        P(),
        P(("groups", "dp", "tok"), "shard"),
    )
    out_specs = (
        P(("groups", "dp", "tok"), "shard"),
        P(("groups", "dp", "tok"), "shard"),
        P(("groups", "shard"), ("dp", "tok"), None, None),
        P(("groups", "shard"), ("dp", "tok"), None, None),
        P(("groups", "shard"), ("dp", "tok"), None, None),
    )
    program = functools.partial(body, n_dp, n_tok, shards)
    return jax.shard_map(program, mesh=mesh, in_specs=in_specs, out_specs=out_specs, check_vma=False)
```

profile of v0, /device:TPU:0, one launch (start us, length us, event | category | flops | bytes accessed | tf_op | source)
XLA Modules:
  0.0 169.9 jit_solution(9495690445413713516)
XLA Ops:
  0.6 3.0 %collective-permute-start.10 = (bf16[256,1024]{1,0:T(8,128)(2,1)}, bf16[256,1024]{1,0:T(8,128)(2,1)S(1)}, u32[]{:S(2)}, u32[]{:S(2)}) collective-permute-start(bf16[256,1024]{1,0:T(8,128)(2,1)} %refs_0_.8), channel_id=1, source_target_pairs={{0,2},{2,0},{1,3},{3,1},{4,6},{6,4},{5,7},{7,5},{8,10},{10,8},{9,1... | collective-permute-start | bytes 1572872 | tf_op jit(solution)/shard_map/ppermute | solution.py:318
  4.3 3.0 %shard_map.119 = (s32[2,2,4]{2,1,0:T(2,128)}, bf16[8,128,128]{2,1,0:T(8,128)(2,1)}, bf16[8,128,128]{2,1,0:T(8,128)(2,1)}, bf16[8,128,128]{2,1,0:T(8,128)(2,1)}) custom-call(s32[4]{0:T(128)} %pad_add_fusion.info, s32[2,16]{1,0:T(2,128)} %gate_rows.1, s32[2,16]{1,0:T(2,128)} %up_rows.1, bf16[2,16,128,128]{3,2,1,0:T(8,128)(2,1)} %gate.1, ...), custom_call_target="tpu_custom_call" | custom-call | bytes 3932224 | tf_op jit(solution)/shard_map/pallas_call | solution.py:66
  7.3 3.1 %collective-permute-start.6 = (bf16[8,128,128]{2,1,0:T(8,128)(2,1)}, bf16[8,128,128]{2,1,0:T(8,128)(2,1)S(1)}, u32[]{:S(2)}, u32[]{:S(2)}) collective-permute-start(bf16[8,128,128]{2,1,0:T(8,128)(2,1)} %get-tuple-element.50), channel_id=1, source_target_pairs={{2,0},{8,1},{4,2},{14,3},{3,4},{9,5},{5,6},{15,7},{0,8},{10,9},{6,... | collective-permute-start | bytes 786440 | tf_op jit(solution)/shard_map/ppermute | solution.py:342
  10.4 8.7 %collective-permute-done.10.refs_0_.refs_6_.refs_2_ = bf16[256,1024]{1,0:T(8,128)(2,1)S(1)} collective-permute-done((bf16[256,1024]{1,0:T(8,128)(2,1)}, bf16[256,1024]{1,0:T(8,128)(2,1)S(1)}, u32[]{:S(2)}, u32[]{:S(2)}) %collective-permute-start.10) | collective-permute-done | bytes 524320 | tf_op jit(solution)/shard_map/ppermute | solution.py:318
  19.1 2.6 %collective-permute-start = (s32[2,2,4]{2,1,0:T(2,128)S(1)}, s32[2,2,4]{2,1,0:T(2,128)S(1)}, u32[]{:S(2)}, u32[]{:S(2)}) collective-permute-start(s32[2,2,4]{2,1,0:T(2,128)S(1)} %copy-done.4), channel_id=1, source_target_pairs={{2,0},{8,1},{4,2},{14,3},{3,4},{9,5},{5,6},{15,7},{0,8},{10,9},{6,... | collective-permute-start | bytes 200 | tf_op jit(solution)/shard_map/ppermute | solution.py:341
  21.7 8.2 %collective-permute-done.rows = s32[2,2,4]{2,1,0:T(2,128)S(1)} collective-permute-done((s32[2,2,4]{2,1,0:T(2,128)S(1)}, s32[2,2,4]{2,1,0:T(2,128)S(1)}, u32[]{:S(2)}, u32[]{:S(2)}) %collective-permute-start) | collective-permute-done | bytes 96 | tf_op jit(solution)/shard_map/ppermute | solution.py:341
  30.4 2.2 %collective-permute-start.2 = (bf16[8,128,128]{2,1,0:T(8,128)(2,1)}, bf16[8,128,128]{2,1,0:T(8,128)(2,1)S(1)}, u32[]{:S(2)}, u32[]{:S(2)}) collective-permute-start(bf16[8,128,128]{2,1,0:T(8,128)(2,1)} %get-tuple-element.45), channel_id=1, source_target_pairs={{2,0},{8,1},{4,2},{14,3},{3,4},{9,5},{5,6},{15,7},{0,8},{10,9},{6,... | collective-permute-start | bytes 786440 | tf_op jit(solution)/shard_map/ppermute | solution.py:340
  34.1 4.9 %collective-permute-done.2.refs_2_ = bf16[8,128,128]{2,1,0:T(8,128)(2,1)S(1)} collective-permute-done((bf16[8,128,128]{2,1,0:T(8,128)(2,1)}, bf16[8,128,128]{2,1,0:T(8,128)(2,1)S(1)}, u32[]{:S(2)}, u32[]{:S(2)}) %collective-permute-start.2) | collective-permute-done | bytes 262176 | tf_op jit(solution)/shard_map/ppermute | solution.py:340
  41.1 3.5 %collective-permute-done.21.refs_4_ = bf16[8,128,128]{2,1,0:T(8,128)(2,1)S(1)} collective-permute-done((bf16[8,128,128]{2,1,0:T(8,128)(2,1)}, bf16[8,128,128]{2,1,0:T(8,128)(2,1)S(1)}, u32[]{:S(2)}, u32[]{:S(2)}) %collective-permute-start.21) | collective-permute-done | bytes 262176 | tf_op jit(solution)/shard_map/ppermute | solution.py:343
  44.6 3.3 %collective-permute-start.8 = (bf16[1,2,64,256]{3,2,1,0:T(8,128)(2,1)S(1)}, bf16[1,2,64,256]{3,2,1,0:T(8,128)(2,1)S(1)}, u32[]{:S(2)}, u32[]{:S(2)}) collective-permute-start(bf16[1,2,64,256]{3,2,1,0:T(8,128)(2,1)S(1)} %get-tuple-element.53), channel_id=1, source_target_pairs={{0,8},{4,12},{8,0},{12,4},{1,9},{5,13},{9,1},{13,5},{2,10},{6,14},... | collective-permute-start | bytes 196616 | tf_op jit(solution)/shard_map/ppermute | solution.py:310
  56.9 3.1 %collective-permute-done.3.refs_1_ = bf16[1,2,64,256]{3,2,1,0:T(8,128)(2,1)S(1)} collective-permute-done((bf16[1,2,64,256]{3,2,1,0:T(8,128)(2,1)S(1)}, bf16[1,2,64,256]{3,2,1,0:T(8,128)(2,1)S(1)}, u32[]{:S(2)}, u32[]{:S(2)}) %collective-permute-start.3) | collective-permute-done | bytes 65568 | tf_op jit(solution)/shard_map/ppermute | solution.py:310
  65.1 6.0 %collective-permute-start.26 = (bf16[1,4,64,256]{3,2,1,0:T(8,128)(2,1)S(1)}, bf16[1,4,64,256]{3,2,1,0:T(8,128)(2,1)S(1)}, u32[]{:S(2)}, u32[]{:S(2)}) collective-permute-start(bf16[1,4,64,256]{3,2,1,0:T(8,128)(2,1)S(1)} %get-tuple-element.71), channel_id=1, source_target_pairs={{0,8},{4,12},{8,0},{12,4},{1,9},{5,13},{9,1},{13,5},{2,10},{6,14},... | collective-permute-start | bytes 393224 | tf_op jit(solution)/shard_map/ppermute | solution.py:310
  71.1 4.1 %collective-permute-done.13.refs_10_ = bf16[2,2,64,256]{3,2,1,0:T(8,128)(2,1)S(1)} collective-permute-done((bf16[2,2,64,256]{3,2,1,0:T(8,128)(2,1)S(1)}, bf16[2,2,64,256]{3,2,1,0:T(8,128)(2,1)S(1)}, u32[]{:S(2)}, u32[]{:S(2)}) %collective-permute-start.13) | collective-permute-done | bytes 131104 | tf_op jit(solution)/shard_map/ppermute | solution.py:310
  75.4 6.9 %collective-permute-done.26.refs_2_ = bf16[1,4,64,256]{3,2,1,0:T(8,128)(2,1)S(1)} collective-permute-done((bf16[1,4,64,256]{3,2,1,0:T(8,128)(2,1)S(1)}, bf16[1,4,64,256]{3,2,1,0:T(8,128)(2,1)S(1)}, u32[]{:S(2)}, u32[]{:S(2)}) %collective-permute-start.26) | collective-permute-done | bytes 131104 | tf_op jit(solution)/shard_map/ppermute | solution.py:310
  82.4 2.7 %collective-permute-start.31 = (bf16[4,64,256]{2,1,0:T(8,128)(2,1)S(1)}, bf16[4,64,256]{2,1,0:T(8,128)(2,1)S(1)}, u32[]{:S(2)}, u32[]{:S(2)}) collective-permute-start(bf16[4,64,256]{2,1,0:T(8,128)(2,1)S(1)} %get-tuple-element.74.refs_0_), channel_id=1, source_target_pairs={{0,4},{4,0},{8,12},{12,8},{1,5},{5,1},{9,13},{13,9},{2,6},{6,2},{1... | collective-permute-start | bytes 393224 | tf_op jit(solution)/shard_map/ppermute | solution.py:310
  92.4 5.6 %collective-permute-done.32.refs_2_ = bf16[4,64,256]{2,1,0:T(8,128)(2,1)S(1)} collective-permute-done((bf16[4,64,256]{2,1,0:T(8,128)(2,1)S(1)}, bf16[4,64,256]{2,1,0:T(8,128)(2,1)S(1)}, u32[]{:S(2)}, u32[]{:S(2)}) %collective-permute-start.32) | collective-permute-done | bytes 131104 | tf_op jit(solution)/shard_map/ppermute | solution.py:310
  98.0 9.9 %collective-permute-start.16 = (bf16[4,64,256]{2,1,0:T(8,128)(2,1)S(1)}, bf16[4,64,256]{2,1,0:T(8,128)(2,1)S(1)}, u32[]{:S(2)}, u32[]{:S(2)}) collective-permute-start(bf16[4,64,256]{2,1,0:T(8,128)(2,1)S(1)} %get-tuple-element.61.refs_0_), channel_id=1, source_target_pairs={{0,8},{4,12},{8,0},{12,4},{1,9},{5,13},{9,1},{13,5},{2,10},{6,14},... | collective-permute-start | bytes 393224 | tf_op jit(solution)/shard_map/ppermute | solution.py:310
  114.5 5.1 %collective-permute-done.16.refs_2_ = bf16[4,64,256]{2,1,0:T(8,128)(2,1)S(1)} collective-permute-done((bf16[4,64,256]{2,1,0:T(8,128)(2,1)S(1)}, bf16[4,64,256]{2,1,0:T(8,128)(2,1)S(1)}, u32[]{:S(2)}, u32[]{:S(2)}) %collective-permute-start.16) | collective-permute-done | bytes 131104 | tf_op jit(solution)/shard_map/ppermute | solution.py:310
  123.5 4.3 %collective-permute-start.34 = (bf16[1,256,1024]{2,1,0:T(8,128)(2,1)S(1)}, bf16[1,256,1024]{2,1,0:T(8,128)(2,1)S(1)}, u32[]{:S(2)}, u32[]{:S(2)}) collective-permute-start(bf16[1,256,1024]{2,1,0:T(8,128)(2,1)S(1)} %get-tuple-element.77), channel_id=1, source_target_pairs={{0,1},{1,0},{2,3},{3,2},{4,5},{5,4},{6,7},{7,6},{8,9},{9,8},{10,11... | collective-permute-start | bytes 1572872 | tf_op jit(solution)/shard_map/ppermute | solution.py:444
  128.5 3.2 %collective-permute-start.22 = (bf16[1,256,1024]{2,1,0:T(8,128)(2,1)S(1)}, bf16[1,256,1024]{2,1,0:T(8,128)(2,1)S(1)}, u32[]{:S(2)}, u32[]{:S(2)}) collective-permute-start(bf16[1,256,1024]{2,1,0:T(8,128)(2,1)S(1)} %get-tuple-element.65), channel_id=1, source_target_pairs={{0,1},{1,0},{2,3},{3,2},{4,5},{5,4},{6,7},{7,6},{8,9},{9,8},{10,11... | collective-permute-start | bytes 1572872 | tf_op jit(solution)/shard_map/ppermute | solution.py:444
  131.7 2.5 %collective-permute-start.36 = (bf16[256,1024]{1,0:T(8,128)(2,1)S(1)}, bf16[256,1024]{1,0:T(8,128)(2,1)S(1)}, u32[]{:S(2)}, u32[]{:S(2)}) collective-permute-start(bf16[256,1024]{1,0:T(8,128)(2,1)S(1)} %shard_map.131), channel_id=1, source_target_pairs={{0,2},{2,0},{1,3},{3,1},{4,6},{6,4},{5,7},{7,5},{8,10},{10,8},{9,1... | collective-permute-start | bytes 1572872 | tf_op jit(solution)/shard_map/ppermute | solution.py:449
  134.4 2.4 %collective-permute-start.24 = (bf16[256,1024]{1,0:T(8,128)(2,1)S(1)}, bf16[256,1024]{1,0:T(8,128)(2,1)S(1)}, u32[]{:S(2)}, u32[]{:S(2)}) collective-permute-start(bf16[256,1024]{1,0:T(8,128)(2,1)S(1)} %shard_map.126), channel_id=1, source_target_pairs={{0,2},{2,0},{1,3},{3,1},{4,6},{6,4},{5,7},{7,5},{8,10},{10,8},{9,1... | collective-permute-start | bytes 1572872 | tf_op jit(solution)/shard_map/ppermute | solution.py:449
  141.5 16.4 %collective-permute-done.36.refs_1_ = bf16[256,1024]{1,0:T(8,128)(2,1)S(1)} collective-permute-done((bf16[256,1024]{1,0:T(8,128)(2,1)S(1)}, bf16[256,1024]{1,0:T(8,128)(2,1)S(1)}, u32[]{:S(2)}, u32[]{:S(2)}) %collective-permute-start.36) | collective-permute-done | bytes 524320 | tf_op jit(solution)/shard_map/ppermute | solution.py:449
  158.8 10.2 %collective-permute-done.24.refs_1_ = bf16[256,1024]{1,0:T(8,128)(2,1)S(1)} collective-permute-done((bf16[256,1024]{1,0:T(8,128)(2,1)S(1)}, bf16[256,1024]{1,0:T(8,128)(2,1)S(1)}, u32[]{:S(2)}, u32[]{:S(2)}) %collective-permute-start.24) | collective-permute-done | bytes 524320 | tf_op jit(solution)/shard_map/ppermute | solution.py:449
  (86 shorter events, 44.3 us)
Async XLA Ops:
  0.6 18.5 %collective-permute-start.10 = (bf16[256,1024]{1,0:T(8,128)(2,1)}, bf16[256,1024]{1,0:T(8,128)(2,1)S(1)}, u32[]{:S(2)}, u32[]{:S(2)}) collective-permute-start(bf16[256,1024]{1,0:T(8,128)(2,1)} %refs_0_.8), channel_id=1, source_target_pairs={{0,2},{2,0},{1,3},{3,1},{4,6},{6,4},{5,7},{7,5},{8,10},{10,8},{9,1... | collective-permute-start | bytes 1572872 | tf_op jit(solution)/shard_map/ppermute | solution.py:318
  3.7 26.2 %collective-permute-start.19 = (bf16[256,1024]{1,0:T(8,128)(2,1)}, bf16[256,1024]{1,0:T(8,128)(2,1)S(1)}, u32[]{:S(2)}, u32[]{:S(2)}) collective-permute-start(bf16[256,1024]{1,0:T(8,128)(2,1)} %refs_0_.9), channel_id=1, source_target_pairs={{0,2},{2,0},{1,3},{3,1},{4,6},{6,4},{5,7},{7,5},{8,10},{10,8},{9,1... | collective-permute-start | bytes 1572872 | tf_op jit(solution)/shard_map/ppermute | solution.py:318
  3.7 28.9 %collective-permute-start.1 = (bf16[256,1024]{1,0:T(8,128)(2,1)}, bf16[256,1024]{1,0:T(8,128)(2,1)S(1)}, u32[]{:S(2)}, u32[]{:S(2)}) collective-permute-start(bf16[256,1024]{1,0:T(8,128)(2,1)} %refs_0_.8), channel_id=1, source_target_pairs={{0,1},{1,0},{2,3},{3,2},{4,5},{5,4},{6,7},{7,6},{8,9},{9,8},{10,11... | collective-permute-start | bytes 1572872 | tf_op jit(solution)/shard_map/ppermute | solution.py:321
  7.3 23.0 %collective-permute-start.6 = (bf16[8,128,128]{2,1,0:T(8,128)(2,1)}, bf16[8,128,128]{2,1,0:T(8,128)(2,1)S(1)}, u32[]{:S(2)}, u32[]{:S(2)}) collective-permute-start(bf16[8,128,128]{2,1,0:T(8,128)(2,1)} %get-tuple-element.50), channel_id=1, source_target_pairs={{2,0},{8,1},{4,2},{14,3},{3,4},{9,5},{5,6},{15,7},{0,8},{10,9},{6,... | collective-permute-start | bytes 786440 | tf_op jit(solution)/shard_map/ppermute | solution.py:342
  19.1 28.8 %collective-permute-start.11 = (bf16[256,1024]{1,0:T(8,128)(2,1)S(1)}, bf16[256,1024]{1,0:T(8,128)(2,1)S(1)}, u32[]{:S(2)}, u32[]{:S(2)}) collective-permute-start(bf16[256,1024]{1,0:T(8,128)(2,1)S(1)} %collective-permute-done.10.refs_0_.refs_6_.refs_2_), channel_id=1, source_target_pairs={{0,1},{1,0},{2,3},{3,2},{4,5},{5,4},{6,7},{7,6},{8,9},{9,8},{10,11... | collective-permute-start | bytes 1572872 | tf_op jit(solution)/shard_map/ppermute | solution.py:321
  29.9 21.5 %collective-permute-start.18 = (bf16[256,1024]{1,0:T(8,128)(2,1)S(1)}, bf16[256,1024]{1,0:T(8,128)(2,1)S(1)}, u32[]{:S(2)}, u32[]{:S(2)}) collective-permute-start(bf16[256,1024]{1,0:T(8,128)(2,1)S(1)} %copy-done.1), channel_id=1, source_target_pairs={{0,1},{1,0},{2,3},{3,2},{4,5},{5,4},{6,7},{7,6},{8,9},{9,8},{10,11... | collective-permute-start | bytes 1572872 | tf_op jit(solution)/shard_map/ppermute | solution.py:321
  29.9 30.4 %collective-permute-start.20 = (bf16[256,1024]{1,0:T(8,128)(2,1)S(1)}, bf16[256,1024]{1,0:T(8,128)(2,1)S(1)}, u32[]{:S(2)}, u32[]{:S(2)}) collective-permute-start(bf16[256,1024]{1,0:T(8,128)(2,1)S(1)} %collective-permute-done.19.refs_2_), channel_id=1, source_target_pairs={{0,1},{1,0},{2,3},{3,2},{4,5},{5,4},{6,7},{7,6},{8,9},{9,8},{10,11... | collective-permute-start | bytes 1572872 | tf_op jit(solution)/shard_map/ppermute | solution.py:321
  32.6 12.0 %collective-permute-start.21 = (bf16[8,128,128]{2,1,0:T(8,128)(2,1)}, bf16[8,128,128]{2,1,0:T(8,128)(2,1)S(1)}, u32[]{:S(2)}, u32[]{:S(2)}) collective-permute-start(bf16[8,128,128]{2,1,0:T(8,128)(2,1)} %get-tuple-element.62), channel_id=1, source_target_pairs={{2,0},{8,1},{4,2},{14,3},{3,4},{9,5},{5,6},{15,7},{0,8},{10,9},{6,... | collective-permute-start | bytes 786440 | tf_op jit(solution)/shard_map/ppermute | solution.py:343
  39.0 13.0 %collective-permute-start.7 = (bf16[1,2,64,256]{3,2,1,0:T(8,128)(2,1)S(1)}, bf16[1,2,64,256]{3,2,1,0:T(8,128)(2,1)S(1)}, u32[]{:S(2)}, u32[]{:S(2)}) collective-permute-start(bf16[1,2,64,256]{3,2,1,0:T(8,128)(2,1)S(1)} %get-tuple-element.52), channel_id=1, source_target_pairs={{0,4},{4,0},{8,12},{12,8},{1,5},{5,1},{9,13},{13,9},{2,6},{6,2},{1... | collective-permute-start | bytes 196616 | tf_op jit(solution)/shard_map/ppermute | solution.py:310
  51.4 19.7 %collective-permute-start.12 = (bf16[2,2,64,256]{3,2,1,0:T(8,128)(2,1)S(1)}, bf16[2,2,64,256]{3,2,1,0:T(8,128)(2,1)S(1)}, u32[]{:S(2)}, u32[]{:S(2)}) collective-permute-start(bf16[2,2,64,256]{3,2,1,0:T(8,128)(2,1)S(1)} %get-tuple-element.58), channel_id=1, source_target_pairs={{0,4},{4,0},{8,12},{12,8},{1,5},{5,1},{9,13},{13,9},{2,6},{6,2},{1... | collective-permute-start | bytes 393224 | tf_op jit(solution)/shard_map/ppermute | solution.py:310
  60.0 15.3 %collective-permute-start.13 = (bf16[2,2,64,256]{3,2,1,0:T(8,128)(2,1)S(1)}, bf16[2,2,64,256]{3,2,1,0:T(8,128)(2,1)S(1)}, u32[]{:S(2)}, u32[]{:S(2)}) collective-permute-start(bf16[2,2,64,256]{3,2,1,0:T(8,128)(2,1)S(1)} %get-tuple-element.59), channel_id=1, source_target_pairs={{0,8},{4,12},{8,0},{12,4},{1,9},{5,13},{9,1},{13,5},{2,10},{6,14},... | collective-permute-start | bytes 393224 | tf_op jit(solution)/shard_map/ppermute | solution.py:310
  60.3 15.0 %collective-permute-start.14 = (bf16[2,2,64,256]{3,2,1,0:T(8,128)(2,1)S(1)}, bf16[2,2,64,256]{3,2,1,0:T(8,128)(2,1)S(1)}, u32[]{:S(2)}, u32[]{:S(2)}) collective-permute-start(bf16[2,2,64,256]{3,2,1,0:T(8,128)(2,1)S(1)} %get-tuple-element.60), channel_id=1, source_target_pairs={{0,12},{4,8},{8,4},{12,0},{1,13},{5,9},{9,5},{13,1},{2,14},{6,10},... | collective-permute-start | bytes 393224 | tf_op jit(solution)/shard_map/ppermute | solution.py:310
  65.1 17.2 %collective-permute-start.26 = (bf16[1,4,64,256]{3,2,1,0:T(8,128)(2,1)S(1)}, bf16[1,4,64,256]{3,2,1,0:T(8,128)(2,1)S(1)}, u32[]{:S(2)}, u32[]{:S(2)}) collective-permute-start(bf16[1,4,64,256]{3,2,1,0:T(8,128)(2,1)S(1)} %get-tuple-element.71), channel_id=1, source_target_pairs={{0,8},{4,12},{8,0},{12,4},{1,9},{5,13},{9,1},{13,5},{2,10},{6,14},... | collective-permute-start | bytes 393224 | tf_op jit(solution)/shard_map/ppermute | solution.py:310
  85.1 12.9 %collective-permute-start.32 = (bf16[4,64,256]{2,1,0:T(8,128)(2,1)S(1)}, bf16[4,64,256]{2,1,0:T(8,128)(2,1)S(1)}, u32[]{:S(2)}, u32[]{:S(2)}) collective-permute-start(bf16[4,64,256]{2,1,0:T(8,128)(2,1)S(1)} %get-tuple-element.74.refs_0_), channel_id=1, source_target_pairs={{0,8},{4,12},{8,0},{12,4},{1,9},{5,13},{9,1},{13,5},{2,10},{6,14},... | collective-permute-start | bytes 393224 | tf_op jit(solution)/shard_map/ppermute | solution.py:310
  87.6 20.4 %collective-permute-start.28 = (bf16[4,64,256]{2,1,0:T(8,128)(2,1)S(1)}, bf16[4,64,256]{2,1,0:T(8,128)(2,1)S(1)}, u32[]{:S(2)}, u32[]{:S(2)}) collective-permute-start(bf16[4,64,256]{2,1,0:T(8,128)(2,1)S(1)} %get-tuple-element.73.refs_0_), channel_id=1, source_target_pairs={{0,4},{4,0},{8,12},{12,8},{1,5},{5,1},{9,13},{13,9},{2,6},{6,2},{1... | collective-permute-start | bytes 393224 | tf_op jit(solution)/shard_map/ppermute | solution.py:310
  88.6 23.9 %collective-permute-start.29 = (bf16[4,64,256]{2,1,0:T(8,128)(2,1)S(1)}, bf16[4,64,256]{2,1,0:T(8,128)(2,1)S(1)}, u32[]{:S(2)}, u32[]{:S(2)}) collective-permute-start(bf16[4,64,256]{2,1,0:T(8,128)(2,1)S(1)} %get-tuple-element.73.refs_0_), channel_id=1, source_target_pairs={{0,8},{4,12},{8,0},{12,4},{1,9},{5,13},{9,1},{13,5},{2,10},{6,14},... | collective-permute-start | bytes 393224 | tf_op jit(solution)/shard_map/ppermute | solution.py:310
  90.6 22.0 %collective-permute-start.30 = (bf16[4,64,256]{2,1,0:T(8,128)(2,1)S(1)}, bf16[4,64,256]{2,1,0:T(8,128)(2,1)S(1)}, u32[]{:S(2)}, u32[]{:S(2)}) collective-permute-start(bf16[4,64,256]{2,1,0:T(8,128)(2,1)S(1)} %get-tuple-element.73.refs_0_), channel_id=1, source_target_pairs={{0,12},{4,8},{8,4},{12,0},{1,13},{5,9},{9,5},{13,1},{2,14},{6,10},... | collective-permute-start | bytes 393224 | tf_op jit(solution)/shard_map/ppermute | solution.py:310
  98.0 16.5 %collective-permute-start.15 = (bf16[4,64,256]{2,1,0:T(8,128)(2,1)S(1)}, bf16[4,64,256]{2,1,0:T(8,128)(2,1)S(1)}, u32[]{:S(2)}, u32[]{:S(2)}) collective-permute-start(bf16[4,64,256]{2,1,0:T(8,128)(2,1)S(1)} %get-tuple-element.61.refs_0_), channel_id=1, source_target_pairs={{0,4},{4,0},{8,12},{12,8},{1,5},{5,1},{9,13},{13,9},{2,6},{6,2},{1... | collective-permute-start | bytes 393224 | tf_op jit(solution)/shard_map/ppermute | solution.py:310
  98.0 21.6 %collective-permute-start.16 = (bf16[4,64,256]{2,1,0:T(8,128)(2,1)S(1)}, bf16[4,64,256]{2,1,0:T(8,128)(2,1)S(1)}, u32[]{:S(2)}, u32[]{:S(2)}) collective-permute-start(bf16[4,64,256]{2,1,0:T(8,128)(2,1)S(1)} %get-tuple-element.61.refs_0_), channel_id=1, source_target_pairs={{0,8},{4,12},{8,0},{12,4},{1,9},{5,13},{9,1},{13,5},{2,10},{6,14},... | collective-permute-start | bytes 393224 | tf_op jit(solution)/shard_map/ppermute | solution.py:310
  114.4 14.0 %collective-permute-start.35 = (bf16[1,256,1024]{2,1,0:T(8,128)(2,1)S(1)}, bf16[1,256,1024]{2,1,0:T(8,128)(2,1)S(1)}, u32[]{:S(2)}, u32[]{:S(2)}) collective-permute-start(bf16[1,256,1024]{2,1,0:T(8,128)(2,1)S(1)} %get-tuple-element.79), channel_id=1, source_target_pairs={{0,1},{1,0},{2,3},{3,2},{4,5},{5,4},{6,7},{7,6},{8,9},{9,8},{10,11... | collective-permute-start | bytes 1572872 | tf_op jit(solution)/shard_map/ppermute | solution.py:444
  123.5 18.0 %collective-permute-start.34 = (bf16[1,256,1024]{2,1,0:T(8,128)(2,1)S(1)}, bf16[1,256,1024]{2,1,0:T(8,128)(2,1)S(1)}, u32[]{:S(2)}, u32[]{:S(2)}) collective-permute-start(bf16[1,256,1024]{2,1,0:T(8,128)(2,1)S(1)} %get-tuple-element.77), channel_id=1, source_target_pairs={{0,1},{1,0},{2,3},{3,2},{4,5},{5,4},{6,7},{7,6},{8,9},{9,8},{10,11... | collective-permute-start | bytes 1572872 | tf_op jit(solution)/shard_map/ppermute | solution.py:444
  128.5 30.3 %collective-permute-start.22 = (bf16[1,256,1024]{2,1,0:T(8,128)(2,1)S(1)}, bf16[1,256,1024]{2,1,0:T(8,128)(2,1)S(1)}, u32[]{:S(2)}, u32[]{:S(2)}) collective-permute-start(bf16[1,256,1024]{2,1,0:T(8,128)(2,1)S(1)} %get-tuple-element.65), channel_id=1, source_target_pairs={{0,1},{1,0},{2,3},{3,2},{4,5},{5,4},{6,7},{7,6},{8,9},{9,8},{10,11... | collective-permute-start | bytes 1572872 | tf_op jit(solution)/shard_map/ppermute | solution.py:444
  131.7 26.1 %collective-permute-start.36 = (bf16[256,1024]{1,0:T(8,128)(2,1)S(1)}, bf16[256,1024]{1,0:T(8,128)(2,1)S(1)}, u32[]{:S(2)}, u32[]{:S(2)}) collective-permute-start(bf16[256,1024]{1,0:T(8,128)(2,1)S(1)} %shard_map.131), channel_id=1, source_target_pairs={{0,2},{2,0},{1,3},{3,1},{4,6},{6,4},{5,7},{7,5},{8,10},{10,8},{9,1... | collective-permute-start | bytes 1572872 | tf_op jit(solution)/shard_map/ppermute | solution.py:449
  134.4 34.5 %collective-permute-start.24 = (bf16[256,1024]{1,0:T(8,128)(2,1)S(1)}, bf16[256,1024]{1,0:T(8,128)(2,1)S(1)}, u32[]{:S(2)}, u32[]{:S(2)}) collective-permute-start(bf16[256,1024]{1,0:T(8,128)(2,1)S(1)} %shard_map.126), channel_id=1, source_target_pairs={{0,2},{2,0},{1,3},{3,1},{4,6},{6,4},{5,7},{7,5},{8,10},{10,8},{9,1... | collective-permute-start | bytes 1572872 | tf_op jit(solution)/shard_map/ppermute | solution.py:449
  (21 other events, 232.2 us)
where the time goes:
time: 170 us
  waiting for transfers between devices  77.9 us (46%)
  starting transfers between devices  69.2 us (41%)
  Pallas kernels  21.3 us (13%)
    ppermute x21, starting transfers between devices, spread(): lax.ppermute(parts[d], 'shard', xor_perm(shards, d))  42.8 us
    ppermute x2, waiting for transfers between devices, sum_plane(): arrived.append(lax.ppermute(total(parts), 'dp', xor_perm(n_dp, dx)))  26.5 us
    ppermute x21, waiting for transfers between devices, spread(): lax.ppermute(parts[d], 'shard', xor_perm(shards, d))  26.1 us
    pallas_call x19, Pallas kernels, call(): pl.pallas_call(kernel, out_shape=outs, in_specs=smem(len(scalars)) + vmem...  21.3 us
    ppermute x2, waiting for transfers between devices, gather_plane(): base = own if dx == 0 else lax.ppermute(own, 'dp', xor_perm(n_dp, dx))  8.66 us
    ppermute x1, waiting for transfers between devices, body(): rows = lax.ppermute(rows, PLANE, w_perm)  8.17 us
    ppermute x4, starting transfers between devices, sum_plane(): parts.append(lax.ppermute(terms[n_dp + dx], 'tok', xor_perm(n_tok, 1)))  7.6 us
    ppermute x2, starting transfers between devices, sum_plane(): arrived.append(lax.ppermute(total(parts), 'dp', xor_perm(n_dp, dx)))  4.9 us
  transfers between devices with their start and end apart: 40, of which 12 were waited for; matrix products, arithmetic and copies ran while one was open for 0% of the time, Pallas kernels for 12%

commit v1 on v0

--- a/solution.py
+++ b/solution.py
@@ -308,6 +308,15 @@
 
     def spread(parts):
         return [parts[0]] + [lax.ppermute(parts[d], "shard", xor_perm(shards, d)) for d in range(1, shards)]
+
+    def gather(own):
+        have = {0: own}
+        bit = shards // 2
+        while bit:
+            for d in sorted(have):
+                have[d ^ bit] = lax.ppermute(have[d], "shard", xor_perm(shards, bit))
+            bit //= 2
+        return [have[d] for d in range(shards)]
 
     def run(kernel, scalars, arrays, outs, scratch, flops, kept=(), limit=LIMIT, out_spaces=None):
         return call(kernel, scalars, arrays, outs, scratch, flops, kept, limit, out_spaces)
@@ -399,10 +408,10 @@
         [],
         macs // 64,
     )
-    hiddens = spread([hidden] * shards)
+    hiddens = gather(hidden)
     gate_act, up_act = run(act_grad_kernel, [], [sums, *hidden_grads], [act, act], [], macs // 64)
-    gate_acts = spread([gate_act] * shards)
-    up_acts = spread([up_act] * shards)
+    gate_acts = gather(gate_act)
+    up_acts = gather(up_act)
 
     plane_shapes = [shape((count, width), F32)] * n_dp + [shape((n_tok - 1, count, width), BF)] * n_dp
     grad_shape = shape((columns, per_owner, size, size), BF)

time: 170 us -> 164 us (0.965)
  starting transfers between devices: 69.2 us -> 57.6 us
  waiting for transfers between devices: 77.9 us -> 82.9 us
    ppermute x21 -> x12, starting transfers between devices: 42.8 us -> 21.4 us  [spread(): lax.ppermute(parts[d], 'shard', xor_perm(shards, d))]
    ppermute x0 -> x9, waiting for transfers between devices: none -> 17 us  [gather(): have[d ^ bit] = lax.ppermute(have[d], 'shard', xor_perm(shards, bit))]
    ppermute x21 -> x12, waiting for transfers between devices: 26.1 us -> 14.1 us  [spread(): lax.ppermute(parts[d], 'shard', xor_perm(shards, d))]
    ppermute x0 -> x9, starting transfers between devices: none -> 10.7 us  [gather(): have[d ^ bit] = lax.ppermute(have[d], 'shard', xor_perm(shards, bit))]
  transfers between devices with their start and end apart: 40 -> 40, of which waited for: 12 -> 15; matrix products, arithmetic and copies ran while one was open for 0% -> 0% of each run, Pallas kernels for 12% -> 12%
where the time goes in v1:
time: 164 us; the launch traced here: 163 us
  waiting for transfers between devices  82.9 us (51%)
  starting transfers between devices  57.6 us (35%)
  Pallas kernels  21.3 us (13%)
    ppermute x2, waiting for transfers between devices, sum_plane(): arrived.append(lax.ppermute(total(parts), 'dp', xor_perm(n_dp, dx)))  26.5 us
    ppermute x12, starting transfers between devices, spread(): lax.ppermute(parts[d], 'shard', xor_perm(shards, d))  21.4 us
    pallas_call x19, Pallas kernels, call(): pl.pallas_call(kernel, out_shape=outs, in_specs=smem(len(scalars)) + vmem...  21.3 us
    ppermute x9, waiting for transfers between devices, gather(): have[d ^ bit] = lax.ppermute(have[d], 'shard', xor_perm(shards, bit))  17 us
    ppermute x12, waiting for transfers between devices, spread(): lax.ppermute(parts[d], 'shard', xor_perm(shards, d))  14.1 us
    ppermute x9, starting transfers between devices, gather(): have[d ^ bit] = lax.ppermute(have[d], 'shard', xor_perm(shards, bit))  10.7 us
    ppermute x2, waiting for transfers between devices, gather_plane(): base = own if dx == 0 else lax.ppermute(own, 'dp', xor_perm(n_dp, dx))  8.66 us
    ppermute x1, waiting for transfers between devices, body(): rows = lax.ppermute(rows, PLANE, w_perm)  8.17 us
  transfers between devices with their start and end apart: 40, of which 15 were waited for; matrix products, arithmetic and copies ran while one was open for 0% of the time, Pallas kernels for 12%

profile of v1, /device:TPU:0, one launch (start us, length us, event | category | flops | bytes accessed | tf_op | source)
XLA Modules:
  0.0 163.3 jit_solution(11653714578823792001)
XLA Ops:
  0.6 3.0 %collective-permute-start.10 = (bf16[256,1024]{1,0:T(8,128)(2,1)}, bf16[256,1024]{1,0:T(8,128)(2,1)S(1)}, u32[]{:S(2)}, u32[]{:S(2)}) collective-permute-start(bf16[256,1024]{1,0:T(8,128)(2,1)} %refs_0_.8), channel_id=1, source_target_pairs={{0,2},{2,0},{1,3},{3,1},{4,6},{6,4},{5,7},{7,5},{8,10},{10,8},{9,1... | collective-permute-start | bytes 1572872 | tf_op jit(solution)/shard_map/ppermute | solution.py:327
  4.3 3.0 %shard_map.119 = (s32[2,2,4]{2,1,0:T(2,128)}, bf16[8,128,128]{2,1,0:T(8,128)(2,1)}, bf16[8,128,128]{2,1,0:T(8,128)(2,1)}, bf16[8,128,128]{2,1,0:T(8,128)(2,1)}) custom-call(s32[4]{0:T(128)} %pad_add_fusion.info, s32[2,16]{1,0:T(2,128)} %gate_rows.1, s32[2,16]{1,0:T(2,128)} %up_rows.1, bf16[2,16,128,128]{3,2,1,0:T(8,128)(2,1)} %gate.1, ...), custom_call_target="tpu_custom_call" | custom-call | bytes 3932224 | tf_op jit(solution)/shard_map/pallas_call | solution.py:66
  7.3 3.1 %collective-permute-start.6 = (bf16[8,128,128]{2,1,0:T(8,128)(2,1)}, bf16[8,128,128]{2,1,0:T(8,128)(2,1)S(1)}, u32[]{:S(2)}, u32[]{:S(2)}) collective-permute-start(bf16[8,128,128]{2,1,0:T(8,128)(2,1)} %get-tuple-element.50), channel_id=1, source_target_pairs={{2,0},{8,1},{4,2},{14,3},{3,4},{9,5},{5,6},{15,7},{0,8},{10,9},{6,... | collective-permute-start | bytes 786440 | tf_op jit(solution)/shard_map/ppermute | solution.py:351
  10.4 8.7 %collective-permute-done.10.refs_0_.refs_6_.refs_2_ = bf16[256,1024]{1,0:T(8,128)(2,1)S(1)} collective-permute-done((bf16[256,1024]{1,0:T(8,128)(2,1)}, bf16[256,1024]{1,0:T(8,128)(2,1)S(1)}, u32[]{:S(2)}, u32[]{:S(2)}) %collective-permute-start.10) | collective-permute-done | bytes 524320 | tf_op jit(solution)/shard_map/ppermute | solution.py:327
  19.1 2.6 %collective-permute-start = (s32[2,2,4]{2,1,0:T(2,128)S(1)}, s32[2,2,4]{2,1,0:T(2,128)S(1)}, u32[]{:S(2)}, u32[]{:S(2)}) collective-permute-start(s32[2,2,4]{2,1,0:T(2,128)S(1)} %copy-done.4), channel_id=1, source_target_pairs={{2,0},{8,1},{4,2},{14,3},{3,4},{9,5},{5,6},{15,7},{0,8},{10,9},{6,... | collective-permute-start | bytes 200 | tf_op jit(solution)/shard_map/ppermute | solution.py:350
  21.7 8.2 %collective-permute-done.rows = s32[2,2,4]{2,1,0:T(2,128)S(1)} collective-permute-done((s32[2,2,4]{2,1,0:T(2,128)S(1)}, s32[2,2,4]{2,1,0:T(2,128)S(1)}, u32[]{:S(2)}, u32[]{:S(2)}) %collective-permute-start) | collective-permute-done | bytes 96 | tf_op jit(solution)/shard_map/ppermute | solution.py:350
  30.4 2.2 %collective-permute-start.2 = (bf16[8,128,128]{2,1,0:T(8,128)(2,1)}, bf16[8,128,128]{2,1,0:T(8,128)(2,1)S(1)}, u32[]{:S(2)}, u32[]{:S(2)}) collective-permute-start(bf16[8,128,128]{2,1,0:T(8,128)(2,1)} %get-tuple-element.45), channel_id=1, source_target_pairs={{2,0},{8,1},{4,2},{14,3},{3,4},{9,5},{5,6},{15,7},{0,8},{10,9},{6,... | collective-permute-start | bytes 786440 | tf_op jit(solution)/shard_map/ppermute | solution.py:349
  34.1 4.9 %collective-permute-done.2.refs_2_ = bf16[8,128,128]{2,1,0:T(8,128)(2,1)S(1)} collective-permute-done((bf16[8,128,128]{2,1,0:T(8,128)(2,1)}, bf16[8,128,128]{2,1,0:T(8,128)(2,1)S(1)}, u32[]{:S(2)}, u32[]{:S(2)}) %collective-permute-start.2) | collective-permute-done | bytes 262176 | tf_op jit(solution)/shard_map/ppermute | solution.py:349
  41.1 3.5 %collective-permute-done.21.refs_4_ = bf16[8,128,128]{2,1,0:T(8,128)(2,1)S(1)} collective-permute-done((bf16[8,128,128]{2,1,0:T(8,128)(2,1)}, bf16[8,128,128]{2,1,0:T(8,128)(2,1)S(1)}, u32[]{:S(2)}, u32[]{:S(2)}) %collective-permute-start.21) | collective-permute-done | bytes 262176 | tf_op jit(solution)/shard_map/ppermute | solution.py:352
  44.6 3.3 %collective-permute-start.8 = (bf16[1,2,64,256]{3,2,1,0:T(8,128)(2,1)S(1)}, bf16[1,2,64,256]{3,2,1,0:T(8,128)(2,1)S(1)}, u32[]{:S(2)}, u32[]{:S(2)}) collective-permute-start(bf16[1,2,64,256]{3,2,1,0:T(8,128)(2,1)S(1)} %get-tuple-element.53), channel_id=1, source_target_pairs={{0,8},{4,12},{8,0},{12,4},{1,9},{5,13},{9,1},{13,5},{2,10},{6,14},... | collective-permute-start | bytes 196616 | tf_op jit(solution)/shard_map/ppermute | solution.py:310
  56.9 3.1 %collective-permute-done.3.refs_1_ = bf16[1,2,64,256]{3,2,1,0:T(8,128)(2,1)S(1)} collective-permute-done((bf16[1,2,64,256]{3,2,1,0:T(8,128)(2,1)S(1)}, bf16[1,2,64,256]{3,2,1,0:T(8,128)(2,1)S(1)}, u32[]{:S(2)}, u32[]{:S(2)}) %collective-permute-start.3) | collective-permute-done | bytes 65568 | tf_op jit(solution)/shard_map/ppermute | solution.py:310
  65.1 6.0 %collective-permute-start.26 = (bf16[1,4,64,256]{3,2,1,0:T(8,128)(2,1)S(1)}, bf16[1,4,64,256]{3,2,1,0:T(8,128)(2,1)S(1)}, u32[]{:S(2)}, u32[]{:S(2)}) collective-permute-start(bf16[1,4,64,256]{3,2,1,0:T(8,128)(2,1)S(1)} %get-tuple-element.71), channel_id=1, source_target_pairs={{0,8},{4,12},{8,0},{12,4},{1,9},{5,13},{9,1},{13,5},{2,10},{6,14},... | collective-permute-start | bytes 393224 | tf_op jit(solution)/shard_map/ppermute | solution.py:310
  71.1 4.1 %collective-permute-done.13.refs_10_ = bf16[2,2,64,256]{3,2,1,0:T(8,128)(2,1)S(1)} collective-permute-done((bf16[2,2,64,256]{3,2,1,0:T(8,128)(2,1)S(1)}, bf16[2,2,64,256]{3,2,1,0:T(8,128)(2,1)S(1)}, u32[]{:S(2)}, u32[]{:S(2)}) %collective-permute-start.13) | collective-permute-done | bytes 131104 | tf_op jit(solution)/shard_map/ppermute | solution.py:310
  75.4 6.9 %collective-permute-done.26.refs_2_ = bf16[1,4,64,256]{3,2,1,0:T(8,128)(2,1)S(1)} collective-permute-done((bf16[1,4,64,256]{3,2,1,0:T(8,128)(2,1)S(1)}, bf16[1,4,64,256]{3,2,1,0:T(8,128)(2,1)S(1)}, u32[]{:S(2)}, u32[]{:S(2)}) %collective-permute-start.26) | collective-permute-done | bytes 131104 | tf_op jit(solution)/shard_map/ppermute | solution.py:310
  82.4 3.7 %collective-permute-start.32 = (bf16[4,64,256]{2,1,0:T(8,128)(2,1)S(1)}, bf16[4,64,256]{2,1,0:T(8,128)(2,1)S(1)}, u32[]{:S(2)}, u32[]{:S(2)}) collective-permute-start(bf16[4,64,256]{2,1,0:T(8,128)(2,1)S(1)} %get-tuple-element.74.refs_0_), channel_id=1, source_target_pairs={{0,8},{4,12},{8,0},{12,4},{1,9},{5,13},{9,1},{13,5},{2,10},{6,14},... | collective-permute-start | bytes 393224 | tf_op jit(solution)/shard_map/ppermute | solution.py:317
  89.0 8.2 %collective-permute-done.32.refs_2_ = bf16[4,64,256]{2,1,0:T(8,128)(2,1)S(1)} collective-permute-done((bf16[4,64,256]{2,1,0:T(8,128)(2,1)S(1)}, bf16[4,64,256]{2,1,0:T(8,128)(2,1)S(1)}, u32[]{:S(2)}, u32[]{:S(2)}) %collective-permute-start.32) | collective-permute-done | bytes 131104 | tf_op jit(solution)/shard_map/ppermute | solution.py:317
  99.3 2.3 %collective-permute-done.29.refs_2_ = bf16[4,64,256]{2,1,0:T(8,128)(2,1)S(1)} collective-permute-done((bf16[4,64,256]{2,1,0:T(8,128)(2,1)S(1)}, bf16[4,64,256]{2,1,0:T(8,128)(2,1)S(1)}, u32[]{:S(2)}, u32[]{:S(2)}) %collective-permute-start.29) | collective-permute-done | bytes 131104 | tf_op jit(solution)/shard_map/ppermute | solution.py:317
  103.6 2.2 %collective-permute-done.33.refs_3_ = bf16[4,64,256]{2,1,0:T(8,128)(2,1)S(1)} collective-permute-done((bf16[4,64,256]{2,1,0:T(8,128)(2,1)S(1)}, bf16[4,64,256]{2,1,0:T(8,128)(2,1)S(1)}, u32[]{:S(2)}, u32[]{:S(2)}) %collective-permute-start.33) | collective-permute-done | bytes 131104 | tf_op jit(solution)/shard_map/ppermute | solution.py:317
  108.6 2.6 %collective-permute-done.30.refs_3_ = bf16[4,64,256]{2,1,0:T(8,128)(2,1)S(1)} collective-permute-done((bf16[4,64,256]{2,1,0:T(8,128)(2,1)S(1)}, bf16[4,64,256]{2,1,0:T(8,128)(2,1)S(1)}, u32[]{:S(2)}, u32[]{:S(2)}) %collective-permute-start.30) | collective-permute-done | bytes 131104 | tf_op jit(solution)/shard_map/ppermute | solution.py:317
  120.4 4.4 %collective-permute-start.22 = (bf16[1,256,1024]{2,1,0:T(8,128)(2,1)S(1)}, bf16[1,256,1024]{2,1,0:T(8,128)(2,1)S(1)}, u32[]{:S(2)}, u32[]{:S(2)}) collective-permute-start(bf16[1,256,1024]{2,1,0:T(8,128)(2,1)S(1)} %get-tuple-element.65), channel_id=1, source_target_pairs={{0,1},{1,0},{2,3},{3,2},{4,5},{5,4},{6,7},{7,6},{8,9},{9,8},{10,11... | collective-permute-start | bytes 1572872 | tf_op jit(solution)/shard_map/ppermute | solution.py:453
  124.9 2.5 %collective-permute-start.36 = (bf16[256,1024]{1,0:T(8,128)(2,1)S(1)}, bf16[256,1024]{1,0:T(8,128)(2,1)S(1)}, u32[]{:S(2)}, u32[]{:S(2)}) collective-permute-start(bf16[256,1024]{1,0:T(8,128)(2,1)S(1)} %shard_map.131), channel_id=1, source_target_pairs={{0,2},{2,0},{1,3},{3,1},{4,6},{6,4},{5,7},{7,5},{8,10},{10,8},{9,1... | collective-permute-start | bytes 1572872 | tf_op jit(solution)/shard_map/ppermute | solution.py:458
  127.5 2.7 %collective-permute-start.24 = (bf16[256,1024]{1,0:T(8,128)(2,1)S(1)}, bf16[256,1024]{1,0:T(8,128)(2,1)S(1)}, u32[]{:S(2)}, u32[]{:S(2)}) collective-permute-start(bf16[256,1024]{1,0:T(8,128)(2,1)S(1)} %shard_map.126), channel_id=1, source_target_pairs={{0,2},{2,0},{1,3},{3,1},{4,6},{6,4},{5,7},{7,5},{8,10},{10,8},{9,1... | collective-permute-start | bytes 1572872 | tf_op jit(solution)/shard_map/ppermute | solution.py:458
  134.9 16.3 %collective-permute-done.36.refs_1_ = bf16[256,1024]{1,0:T(8,128)(2,1)S(1)} collective-permute-done((bf16[256,1024]{1,0:T(8,128)(2,1)S(1)}, bf16[256,1024]{1,0:T(8,128)(2,1)S(1)}, u32[]{:S(2)}, u32[]{:S(2)}) %collective-permute-start.36) | collective-permute-done | bytes 524320 | tf_op jit(solution)/shard_map/ppermute | solution.py:458
  152.2 10.2 %collective-permute-done.24.refs_1_ = bf16[256,1024]{1,0:T(8,128)(2,1)S(1)} collective-permute-done((bf16[256,1024]{1,0:T(8,128)(2,1)S(1)}, bf16[256,1024]{1,0:T(8,128)(2,1)S(1)}, u32[]{:S(2)}, u32[]{:S(2)}) %collective-permute-start.24) | collective-permute-done | bytes 524320 | tf_op jit(solution)/shard_map/ppermute | solution.py:458
  (86 shorter events, 45.0 us)
Async XLA Ops:
  0.6 18.5 %collective-permute-start.10 = (bf16[256,1024]{1,0:T(8,128)(2,1)}, bf16[256,1024]{1,0:T(8,128)(2,1)S(1)}, u32[]{:S(2)}, u32[]{:S(2)}) collective-permute-start(bf16[256,1024]{1,0:T(8,128)(2,1)} %refs_0_.8), channel_id=1, source_target_pairs={{0,2},{2,0},{1,3},{3,1},{4,6},{6,4},{5,7},{7,5},{8,10},{10,8},{9,1... | collective-permute-start | bytes 1572872 | tf_op jit(solution)/shard_map/ppermute | solution.py:327
  3.7 26.2 %collective-permute-start.19 = (bf16[256,1024]{1,0:T(8,128)(2,1)}, bf16[256,1024]{1,0:T(8,128)(2,1)S(1)}, u32[]{:S(2)}, u32[]{:S(2)}) collective-permute-start(bf16[256,1024]{1,0:T(8,128)(2,1)} %refs_0_.9), channel_id=1, source_target_pairs={{0,2},{2,0},{1,3},{3,1},{4,6},{6,4},{5,7},{7,5},{8,10},{10,8},{9,1... | collective-permute-start | bytes 1572872 | tf_op jit(solution)/shard_map/ppermute | solution.py:327
  3.7 28.9 %collective-permute-start.1 = (bf16[256,1024]{1,0:T(8,128)(2,1)}, bf16[256,1024]{1,0:T(8,128)(2,1)S(1)}, u32[]{:S(2)}, u32[]{:S(2)}) collective-permute-start(bf16[256,1024]{1,0:T(8,128)(2,1)} %refs_0_.8), channel_id=1, source_target_pairs={{0,1},{1,0},{2,3},{3,2},{4,5},{5,4},{6,7},{7,6},{8,9},{9,8},{10,11... | collective-permute-start | bytes 1572872 | tf_op jit(solution)/shard_map/ppermute | solution.py:330
  7.3 23.0 %collective-permute-start.6 = (bf16[8,128,128]{2,1,0:T(8,128)(2,1)}, bf16[8,128,128]{2,1,0:T(8,128)(2,1)S(1)}, u32[]{:S(2)}, u32[]{:S(2)}) collective-permute-start(bf16[8,128,128]{2,1,0:T(8,128)(2,1)} %get-tuple-element.50), channel_id=1, source_target_pairs={{2,0},{8,1},{4,2},{14,3},{3,4},{9,5},{5,6},{15,7},{0,8},{10,9},{6,... | collective-permute-start | bytes 786440 | tf_op jit(solution)/shard_map/ppermute | solution.py:351
  19.1 28.8 %collective-permute-start.11 = (bf16[256,1024]{1,0:T(8,128)(2,1)S(1)}, bf16[256,1024]{1,0:T(8,128)(2,1)S(1)}, u32[]{:S(2)}, u32[]{:S(2)}) collective-permute-start(bf16[256,1024]{1,0:T(8,128)(2,1)S(1)} %collective-permute-done.10.refs_0_.refs_6_.refs_2_), channel_id=1, source_target_pairs={{0,1},{1,0},{2,3},{3,2},{4,5},{5,4},{6,7},{7,6},{8,9},{9,8},{10,11... | collective-permute-start | bytes 1572872 | tf_op jit(solution)/shard_map/ppermute | solution.py:330
  29.9 21.5 %collective-permute-start.18 = (bf16[256,1024]{1,0:T(8,128)(2,1)S(1)}, bf16[256,1024]{1,0:T(8,128)(2,1)S(1)}, u32[]{:S(2)}, u32[]{:S(2)}) collective-permute-start(bf16[256,1024]{1,0:T(8,128)(2,1)S(1)} %copy-done.1), channel_id=1, source_target_pairs={{0,1},{1,0},{2,3},{3,2},{4,5},{5,4},{6,7},{7,6},{8,9},{9,8},{10,11... | collective-permute-start | bytes 1572872 | tf_op jit(solution)/shard_map/ppermute | solution.py:330
  29.9 30.4 %collective-permute-start.20 = (bf16[256,1024]{1,0:T(8,128)(2,1)S(1)}, bf16[256,1024]{1,0:T(8,128)(2,1)S(1)}, u32[]{:S(2)}, u32[]{:S(2)}) collective-permute-start(bf16[256,1024]{1,0:T(8,128)(2,1)S(1)} %collective-permute-done.19.refs_2_), channel_id=1, source_target_pairs={{0,1},{1,0},{2,3},{3,2},{4,5},{5,4},{6,7},{7,6},{8,9},{9,8},{10,11... | collective-permute-start | bytes 1572872 | tf_op jit(solution)/shard_map/ppermute | solution.py:330
  32.6 12.0 %collective-permute-start.21 = (bf16[8,128,128]{2,1,0:T(8,128)(2,1)}, bf16[8,128,128]{2,1,0:T(8,128)(2,1)S(1)}, u32[]{:S(2)}, u32[]{:S(2)}) collective-permute-start(bf16[8,128,128]{2,1,0:T(8,128)(2,1)} %get-tuple-element.62), channel_id=1, source_target_pairs={{2,0},{8,1},{4,2},{14,3},{3,4},{9,5},{5,6},{15,7},{0,8},{10,9},{6,... | collective-permute-start | bytes 786440 | tf_op jit(solution)/shard_map/ppermute | solution.py:352
  39.0 13.0 %collective-permute-start.7 = (bf16[1,2,64,256]{3,2,1,0:T(8,128)(2,1)S(1)}, bf16[1,2,64,256]{3,2,1,0:T(8,128)(2,1)S(1)}, u32[]{:S(2)}, u32[]{:S(2)}) collective-permute-start(bf16[1,2,64,256]{3,2,1,0:T(8,128)(2,1)S(1)} %get-tuple-element.52), channel_id=1, source_target_pairs={{0,4},{4,0},{8,12},{12,8},{1,5},{5,1},{9,13},{13,9},{2,6},{6,2},{1... | collective-permute-start | bytes 196616 | tf_op jit(solution)/shard_map/ppermute | solution.py:310
  51.4 19.7 %collective-permute-start.12 = (bf16[2,2,64,256]{3,2,1,0:T(8,128)(2,1)S(1)}, bf16[2,2,64,256]{3,2,1,0:T(8,128)(2,1)S(1)}, u32[]{:S(2)}, u32[]{:S(2)}) collective-permute-start(bf16[2,2,64,256]{3,2,1,0:T(8,128)(2,1)S(1)} %get-tuple-element.58), channel_id=1, source_target_pairs={{0,4},{4,0},{8,12},{12,8},{1,5},{5,1},{9,13},{13,9},{2,6},{6,2},{1... | collective-permute-start | bytes 393224 | tf_op jit(solution)/shard_map/ppermute | solution.py:310
  60.0 15.3 %collective-permute-start.13 = (bf16[2,2,64,256]{3,2,1,0:T(8,128)(2,1)S(1)}, bf16[2,2,64,256]{3,2,1,0:T(8,128)(2,1)S(1)}, u32[]{:S(2)}, u32[]{:S(2)}) collective-permute-start(bf16[2,2,64,256]{3,2,1,0:T(8,128)(2,1)S(1)} %get-tuple-element.59), channel_id=1, source_target_pairs={{0,8},{4,12},{8,0},{12,4},{1,9},{5,13},{9,1},{13,5},{2,10},{6,14},... | collective-permute-start | bytes 393224 | tf_op jit(solution)/shard_map/ppermute | solution.py:310
  60.3 15.0 %collective-permute-start.14 = (bf16[2,2,64,256]{3,2,1,0:T(8,128)(2,1)S(1)}, bf16[2,2,64,256]{3,2,1,0:T(8,128)(2,1)S(1)}, u32[]{:S(2)}, u32[]{:S(2)}) collective-permute-start(bf16[2,2,64,256]{3,2,1,0:T(8,128)(2,1)S(1)} %get-tuple-element.60), channel_id=1, source_target_pairs={{0,12},{4,8},{8,4},{12,0},{1,13},{5,9},{9,5},{13,1},{2,14},{6,10},... | collective-permute-start | bytes 393224 | tf_op jit(solution)/shard_map/ppermute | solution.py:310
  63.7 11.7 %collective-permute-start.25 = (bf16[1,4,64,256]{3,2,1,0:T(8,128)(2,1)S(1)}, bf16[1,4,64,256]{3,2,1,0:T(8,128)(2,1)S(1)}, u32[]{:S(2)}, u32[]{:S(2)}) collective-permute-start(bf16[1,4,64,256]{3,2,1,0:T(8,128)(2,1)S(1)} %get-tuple-element.70), channel_id=1, source_target_pairs={{0,4},{4,0},{8,12},{12,8},{1,5},{5,1},{9,13},{13,9},{2,6},{6,2},{1... | collective-permute-start | bytes 393224 | tf_op jit(solution)/shard_map/ppermute | solution.py:310
  65.1 17.2 %collective-permute-start.26 = (bf16[1,4,64,256]{3,2,1,0:T(8,128)(2,1)S(1)}, bf16[1,4,64,256]{3,2,1,0:T(8,128)(2,1)S(1)}, u32[]{:S(2)}, u32[]{:S(2)}) collective-permute-start(bf16[1,4,64,256]{3,2,1,0:T(8,128)(2,1)S(1)} %get-tuple-element.71), channel_id=1, source_target_pairs={{0,8},{4,12},{8,0},{12,4},{1,9},{5,13},{9,1},{13,5},{2,10},{6,14},... | collective-permute-start | bytes 393224 | tf_op jit(solution)/shard_map/ppermute | solution.py:310
  82.4 14.8 %collective-permute-start.32 = (bf16[4,64,256]{2,1,0:T(8,128)(2,1)S(1)}, bf16[4,64,256]{2,1,0:T(8,128)(2,1)S(1)}, u32[]{:S(2)}, u32[]{:S(2)}) collective-permute-start(bf16[4,64,256]{2,1,0:T(8,128)(2,1)S(1)} %get-tuple-element.74.refs_0_), channel_id=1, source_target_pairs={{0,8},{4,12},{8,0},{12,4},{1,9},{5,13},{9,1},{13,5},{2,10},{6,14},... | collective-permute-start | bytes 393224 | tf_op jit(solution)/shard_map/ppermute | solution.py:317
  86.1 15.4 %collective-permute-start.29 = (bf16[4,64,256]{2,1,0:T(8,128)(2,1)S(1)}, bf16[4,64,256]{2,1,0:T(8,128)(2,1)S(1)}, u32[]{:S(2)}, u32[]{:S(2)}) collective-permute-start(bf16[4,64,256]{2,1,0:T(8,128)(2,1)S(1)} %get-tuple-element.73.refs_0_), channel_id=1, source_target_pairs={{0,8},{4,12},{8,0},{12,4},{1,9},{5,13},{9,1},{13,5},{2,10},{6,14},... | collective-permute-start | bytes 393224 | tf_op jit(solution)/shard_map/ppermute | solution.py:317
  86.2 15.4 %collective-permute-start.31 = (bf16[4,64,256]{2,1,0:T(8,128)(2,1)S(1)}, bf16[4,64,256]{2,1,0:T(8,128)(2,1)S(1)}, u32[]{:S(2)}, u32[]{:S(2)}) collective-permute-start(bf16[4,64,256]{2,1,0:T(8,128)(2,1)S(1)} %get-tuple-element.74.refs_0_), channel_id=1, source_target_pairs={{0,4},{4,0},{8,12},{12,8},{1,5},{5,1},{9,13},{13,9},{2,6},{6,2},{1... | collective-permute-start | bytes 393224 | tf_op jit(solution)/shard_map/ppermute | solution.py:317
  88.1 15.5 %collective-permute-start.16 = (bf16[4,64,256]{2,1,0:T(8,128)(2,1)S(1)}, bf16[4,64,256]{2,1,0:T(8,128)(2,1)S(1)}, u32[]{:S(2)}, u32[]{:S(2)}) collective-permute-start(bf16[4,64,256]{2,1,0:T(8,128)(2,1)S(1)} %get-tuple-element.61.refs_0_), channel_id=1, source_target_pairs={{0,8},{4,12},{8,0},{12,4},{1,9},{5,13},{9,1},{13,5},{2,10},{6,14},... | collective-permute-start | bytes 393224 | tf_op jit(solution)/shard_map/ppermute | solution.py:317
  101.5 11.6 %collective-permute-start.15 = (bf16[4,64,256]{2,1,0:T(8,128)(2,1)S(1)}, bf16[4,64,256]{2,1,0:T(8,128)(2,1)S(1)}, u32[]{:S(2)}, u32[]{:S(2)}) collective-permute-start(bf16[4,64,256]{2,1,0:T(8,128)(2,1)S(1)} %get-tuple-element.61.refs_0_), channel_id=1, source_target_pairs={{0,4},{4,0},{8,12},{12,8},{1,5},{5,1},{9,13},{13,9},{2,6},{6,2},{1... | collective-permute-start | bytes 393224 | tf_op jit(solution)/shard_map/ppermute | solution.py:317
  117.9 17.0 %collective-permute-start.34 = (bf16[1,256,1024]{2,1,0:T(8,128)(2,1)S(1)}, bf16[1,256,1024]{2,1,0:T(8,128)(2,1)S(1)}, u32[]{:S(2)}, u32[]{:S(2)}) collective-permute-start(bf16[1,256,1024]{2,1,0:T(8,128)(2,1)S(1)} %get-tuple-element.77), channel_id=1, source_target_pairs={{0,1},{1,0},{2,3},{3,2},{4,5},{5,4},{6,7},{7,6},{8,9},{9,8},{10,11... | collective-permute-start | bytes 1572872 | tf_op jit(solution)/shard_map/ppermute | solution.py:453
  119.7 12.3 %collective-permute-start.37 = (bf16[2,4,128,128]{3,2,1,0:T(8,128)(2,1)S(1)}, bf16[2,4,128,128]{3,2,1,0:T(8,128)(2,1)S(1)}, u32[]{:S(2)}, u32[]{:S(2)}) collective-permute-start(bf16[2,4,128,128]{3,2,1,0:T(8,128)(2,1)S(1)} %get-tuple-element.80), channel_id=1, source_target_pairs={{0,0},{1,8},{2,4},{3,12},{4,1},{5,9},{6,5},{7,13},{8,2},{9,10},{10... | collective-permute-start | bytes 786440 | tf_op jit(solution)/shard_map/ppermute | solution.py:464
  120.4 31.8 %collective-permute-start.22 = (bf16[1,256,1024]{2,1,0:T(8,128)(2,1)S(1)}, bf16[1,256,1024]{2,1,0:T(8,128)(2,1)S(1)}, u32[]{:S(2)}, u32[]{:S(2)}) collective-permute-start(bf16[1,256,1024]{2,1,0:T(8,128)(2,1)S(1)} %get-tuple-element.65), channel_id=1, source_target_pairs={{0,1},{1,0},{2,3},{3,2},{4,5},{5,4},{6,7},{7,6},{8,9},{9,8},{10,11... | collective-permute-start | bytes 1572872 | tf_op jit(solution)/shard_map/ppermute | solution.py:453
  124.9 26.4 %collective-permute-start.36 = (bf16[256,1024]{1,0:T(8,128)(2,1)S(1)}, bf16[256,1024]{1,0:T(8,128)(2,1)S(1)}, u32[]{:S(2)}, u32[]{:S(2)}) collective-permute-start(bf16[256,1024]{1,0:T(8,128)(2,1)S(1)} %shard_map.131), channel_id=1, source_target_pairs={{0,2},{2,0},{1,3},{3,1},{4,6},{6,4},{5,7},{7,5},{8,10},{10,8},{9,1... | collective-permute-start | bytes 1572872 | tf_op jit(solution)/shard_map/ppermute | solution.py:458
  127.5 34.8 %collective-permute-start.24 = (bf16[256,1024]{1,0:T(8,128)(2,1)S(1)}, bf16[256,1024]{1,0:T(8,128)(2,1)S(1)}, u32[]{:S(2)}, u32[]{:S(2)}) collective-permute-start(bf16[256,1024]{1,0:T(8,128)(2,1)S(1)} %shard_map.126), channel_id=1, source_target_pairs={{0,2},{2,0},{1,3},{3,1},{4,6},{6,4},{5,7},{7,5},{8,10},{10,8},{9,1... | collective-permute-start | bytes 1572872 | tf_op jit(solution)/shard_map/ppermute | solution.py:458
  (21 other events, 222.9 us)

commit v2 on v1

--- a/solution.py
+++ b/solution.py
@@ -18,34 +18,34 @@
     return [(i, i ^ step) for i in range(count)]
 
 
+def column_shard(n_dp, z, x, c):
+    return c * n_dp + (x ^ (z & 1))
+
+
+def shard_perm(shards, n_dp, d):
+    return [(z * n_dp + x, (z ^ d) * n_dp + (x ^ (d & 1))) for z in range(shards) for x in range(n_dp)]
+
+
 def weight_perm(shards, n_dp, n_tok):
     pairs = []
     for z in range(shards):
         for x in range(n_dp):
             for c in range(n_tok):
-                q = c * n_dp + x
-                pairs.append((q * n_dp * n_tok + weight_source(shards, n_dp, n_tok, q, z), (z * n_dp + x) * n_tok + c))
+                source = x * n_tok + z // 2 if (shards, n_dp, n_tok) == (4, 2, 2) else z
+                plane = column_shard(n_dp, z, x, c) * n_dp * n_tok
+                pairs.append((plane + source, (z * n_dp + x) * n_tok + c))
     return pairs
 
 
-def weight_source(shards, n_dp, n_tok, q, z):
+def weight_owner(shards, n_dp, n_tok, z, x, c):
     if (shards, n_dp, n_tok) == (4, 2, 2):
-        x = q % 2
-        far = (q < 2) != (z < 2)
-        return (x if far else 1 - x) * 2 + z % 2
-    return z
-
-
-def weight_owner(shards, n_dp, n_tok, q, x, c):
-    if (shards, n_dp, n_tok) == (4, 2, 2):
-        far = (x == (q & 1)).astype(jnp.int32)
-        return ((q >> 1) ^ far) * 2 + c
+        return c * 2 + (x ^ (z & 1))
     return x * n_tok + c
 
 
 def grad_perm(shards, n_dp, n_tok):
     return [
-        ((z * n_dp + x) * n_tok + c, (c * n_dp + x) * n_dp * n_tok + z)
+        ((z * n_dp + x) * n_tok + c, column_shard(n_dp, z, x, c) * n_dp * n_tok + z)
         for z in range(shards)
         for x in range(n_dp)
         for c in range(n_tok)
@@ -93,10 +93,11 @@
             dense[c * size : (c + 1) * size, here] = packed[c * per_owner + k]
 
 
-def split_rows(total, r, slot, outs, z):
-    rows = outs[0].shape[2]
-    for d, out in enumerate(outs):
-        out[slot, r] = total[r, pl.ds(aligned(z ^ d, rows), rows), :].astype(out.dtype)
+def split_rows(total, r, near, far, z):
+    rows = near.shape[2]
+    for d in range(2 * near.shape[0]):
+        out = far if d % 2 else near
+        out[d // 2, r] = total[r, pl.ds(aligned(z ^ d, rows), rows), :].astype(out.dtype)
 
 
 def copy_owner(pairs, owner, sems):
@@ -113,8 +114,10 @@
     return copies
 
 
-def pack_kernel(info, gate_rows, up_rows, gate, up, down, rows_out, gate_out, up_out, down_out, sems):
-    copies = copy_owner([(gate, gate_out), (up, up_out), (down, down_out)], info[OWNER], sems)
+def pack_kernel(info, gate_rows, up_rows, gate, up, down, rows_out, both_out, down_out, sems):
+    count = down_out.shape[0]
+    targets = both_out.at[pl.ds(0, count)], both_out.at[pl.ds(count, count)], down_out
+    copies = copy_owner(zip((gate, up, down), targets), info[OWNER], sems)
     columns, per_owner = rows_out.shape[1:]
     for i, rows in enumerate((gate_rows, up_rows)):
         for c in range(columns):
@@ -131,75 +134,65 @@
     for c in range(columns):
         for k in range(per_owner):
             place = pl.ds(aligned(rows[i, c, k], size), size)
-            dense[place, c * size : (c + 1) * size] = packed[c * per_owner + k]
-
-
-def own_kernel(shards, n, i, info, rows, *refs):
+            dense[place, c * size : (c + 1) * size] = packed[(i * columns + c) * per_owner + k]
+
+
+def project_kernel(n, i, info, rows, *refs):
     xs, packed = refs[:n], refs[n]
-    outs = refs[n + 1 : n + 1 + shards]
-    dense, total = refs[n + 1 + shards :]
+    near, far, dense, total = refs[n + 1 :]
     scatter_rows(dense, packed, rows, i)
     for r, x in enumerate(xs):
         total[r] = jnp.dot(x[...], dense[...], preferred_element_type=F32)
-        split_rows(total, r, 0, outs, info[Z])
-
-
-def other_gate_up_kernel(shards, n, info, *refs):
-    outs = refs[n + 2 : n + 2 + shards]
-    gate_up(info[Z], refs[:n], refs[n], refs[n + 1], outs, *refs[n + 2 + shards :])
-
-
-def gate_up(z, xs, gate_dense, up_dense, outs, gate_total, up_total):
-    for r, x in enumerate(xs):
-        gate_total[r] = jnp.dot(x[...], gate_dense[...], preferred_element_type=F32)
-        split_rows(gate_total, r, 0, outs, z)
-        up_total[r] = jnp.dot(x[...], up_dense[...], preferred_element_type=F32)
-        split_rows(up_total, r, 1, outs, z)
-
-
-def hidden_grad_kernel(shards, nj, columns, info, down_rows, *refs):
-    cots = refs[:nj]
-    down_blocks = refs[nj]
-    outs = refs[nj + 1 : nj + 1 + shards]
-    down_dense, total = refs[nj + 1 + shards :]
+        split_rows(total, r, near, far, info[Z])
+
+
+def hidden_grad_kernel(nj, columns, info, down_rows, *refs):
+    cots, down_blocks = refs[:nj], refs[nj]
+    near, far, down_dense, total = refs[nj + 1 :]
     place = down_places(info, down_rows, columns, down_blocks.shape[0] // columns)
     scatter_cols(down_dense, down_blocks, place, columns)
     for r in range(nj):
         total[r] = lax.dot_general(
             cots[r][...], down_dense[...], (((1,), (1,)), ((), ())), preferred_element_type=F32
         )
-        split_rows(total, r, 0, outs, info[Z])
-
-
-def hidden_kernel(shards, *refs):
-    gates, ups, others = (refs[i * shards : (i + 1) * shards] for i in range(3))
-    sums, hidden = refs[3 * shards :]
-    first = gates[0].shape[1]
-    total = lambda parts, slot: sum(part[slot].astype(F32) for part in parts)
-    for start, gate, up in (
-        (0, total(gates, 0), total(ups, 0)),
-        (first, total(others, 0), total(others, 1)),
-    ):
-        here = pl.ds(start, gate.shape[0])
-        sums[0, here] = gate
-        sums[1, here] = up
-        hidden[here] = (gate * jax.nn.sigmoid(gate) * up).astype(BF)
-
-
-def act_grad_kernel(sums, *refs):
-    parts, (gate_act, up_act) = refs[:-2], refs[-2:]
-    hidden_grad = sum(part[0].astype(F32) for part in parts)
+        split_rows(total, r, near, far, info[Z])
+
+
+def own_place(dx, d):
+    return dx ^ (d & 1)
+
+
+def add_kernel(n_dp, n_tok, bit, near, arrived, near_out, far_out):
+    for d in range(near.shape[0]):
+        out = far_out if d % 2 else near_out
+        for dx in range(n_dp):
+            there = pl.ds(own_place(dx, bit) * n_tok, n_tok)
+            here = pl.ds(dx * n_tok, n_tok)
+            out[d // 2, here] = (near[d, here] + arrived[d, there].astype(F32)).astype(out.dtype)
+
+
+def hidden_kernel(gate_near, gate_last, up_near, up_last, sums, hidden):
+    gate = gate_near[0] + gate_last[0].astype(F32)
+    up = up_near[0] + up_last[0].astype(F32)
+    sums[0] = gate
+    sums[1] = up
+    hidden[...] = (gate * jax.nn.sigmoid(gate) * up).astype(BF)
+
+
+def act_grad_kernel(sums, near, last, gate_act, up_act):
+    hidden_grad = near[0] + last[0].astype(F32)
     gate, up = sums[0], sums[1]
     s = jax.nn.sigmoid(gate)
     gate_act[...] = (hidden_grad * up * s * (1.0 + gate * (1.0 - s))).astype(BF)
     up_act[...] = (hidden_grad * (gate * s)).astype(BF)
 
 
-def join_rows(joined, parts, z):
+def join_rows(joined, parts, z, n_tok):
     rows = parts[0].shape[1]
     for r in range(joined.shape[0]):
+        dx, dc = divmod(r, n_tok)
         for d, part in enumerate(parts):
-            joined[r, pl.ds(aligned(z ^ d, rows), rows), :] = part[r]
+            joined[r, pl.ds(aligned(z ^ d, rows), rows), :] = part[own_place(dx, d) * n_tok + dc]
 
 
 def weight_grad(acc, left, rights, stage, sems):
@@ -250,7 +243,7 @@
     hiddens, dense = refs[:shards], refs[shards]
     keep, send = refs[shards + 1 : shards + 1 + n_dp], refs[shards + 1 + n_dp : shards + 1 + 2 * n_dp]
     joined = refs[shards + 1 + 2 * n_dp]
-    join_rows(joined, hiddens, info[Z])
+    join_rows(joined, hiddens, info[Z], n_tok)
     for r in reversed(range(joined.shape[0])):
         put_plane(keep, send, r, n_tok, jnp.dot(joined[r], dense[...], preferred_element_type=F32))
 
@@ -267,11 +260,11 @@
     pick_blocks(grad, acc, lambda c, k: rows[1, c, k], True)
 
 
-def gate_grad_kernel(shards, nj, info, rows, *refs):
+def gate_grad_kernel(shards, nj, n_tok, info, rows, *refs):
     acts = refs[:shards]
     xs = refs[shards : shards + nj]
     grad, joined, acc, stage, sems = refs[shards + nj :]
-    join_rows(joined, acts, info[Z])
+    join_rows(joined, acts, info[Z], n_tok)
     weight_grad(acc, joined, xs, stage, sems)
     pick_blocks(grad, acc, lambda c, k: rows[0, c, k], True)
 
@@ -281,7 +274,7 @@
     joined_gate, gate_dense, up_dense = refs[shards : shards + 3]
     keep, send = refs[shards + 3 : shards + 3 + n_dp], refs[shards + 3 + n_dp : shards + 3 + 2 * n_dp]
     joined = refs[shards + 3 + 2 * n_dp]
-    join_rows(joined, acts, info[Z])
+    join_rows(joined, acts, info[Z], n_tok)
     contract = (((1,), (1,)), ((), ()))
     for r in reversed(range(joined.shape[0])):
         value = lax.dot_general(joined_gate[r], gate_dense[...], contract, preferred_element_type=F32)
@@ -297,7 +290,7 @@
     nj = n_dp * n_tok
     z = lax.axis_index("shard")
     x_index, c_index = lax.axis_index("dp"), lax.axis_index("tok")
-    q = c_index * n_dp + x_index
+    q = column_shard(n_dp, z, x_index, c_index)
     count, width = tokens.shape
     columns, nonzero, size, _ = gate_blocks.shape
     per_owner = nonzero // shards
@@ -306,15 +299,24 @@
     part = count // shards
     blocks = columns * per_owner
 
-    def spread(parts):
-        return [parts[0]] + [lax.ppermute(parts[d], "shard", xor_perm(shards, d)) for d in range(1, shards)]
+    def reduce(near, far):
+        bit = 1
+        while bit < shards:
+            arrived = lax.ppermute(far, ("shard", "dp"), shard_perm(shards, n_dp, bit))
+            if near.shape[0] == 1:
+                return near, arrived
+            half = (near.shape[0] // 2, *near.shape[1:])
+            near, far = run(
+                functools.partial(add_kernel, n_dp, n_tok, bit), [], [near, arrived], [shape(half, F32), shape(half, BF)], [], 0
+            )
+            bit *= 2
 
     def gather(own):
         have = {0: own}
         bit = shards // 2
         while bit:
             for d in sorted(have):
-                have[d ^ bit] = lax.ppermute(have[d], "shard", xor_perm(shards, bit))
+                have[d ^ bit] = lax.ppermute(have[d], ("shard", "dp"), shard_perm(shards, n_dp, bit))
             bit //= 2
         return [have[d] for d in range(shards)]
 
@@ -322,91 +324,71 @@
         return call(kernel, scalars, arrays, outs, scratch, flops, kept, limit, out_spaces)
 
     def gather_plane(own):
-        groups = []
+        got = []
         for dx in range(n_dp):
             base = own if dx == 0 else lax.ppermute(own, "dp", xor_perm(n_dp, dx))
-            group = [base]
+            got.append(base)
             for dc in range(1, n_tok):
-                group.append(lax.ppermute(base, "tok", xor_perm(n_tok, dc)))
-            groups.append(group)
-        return groups[0], [a for group in groups[1:] for a in group]
+                got.append(lax.ppermute(base, "tok", xor_perm(n_tok, dc)))
+        return got
 
     w_perm = weight_perm(shards, n_dp, n_tok)
     owner = weight_owner(shards, n_dp, n_tok, z, x_index, c_index)
     info = jnp.stack([v.astype(jnp.int32) for v in (z, q, owner, jnp.int32(owned))])
-    packed_shape = shape((blocks, size, size), BF)
-    rows, gate_part, up_part, down_part = run(
+    rows, both_parts, down_part = run(
         pack_kernel,
         [info, gate_rows, up_rows],
         [],
-        [shape((2, columns, per_owner), jnp.int32)] + [packed_shape] * 3,
+        [shape((2, columns, per_owner), jnp.int32)] + [shape((n * blocks, size, size), BF) for n in (2, 1)],
         [pltpu.SemaphoreType.DMA((3 * columns,))],
         0,
         [gate_blocks, up_blocks, down_blocks],
         60 << 20,
-        [pltpu.SMEM] + [pltpu.VMEM] * 3,
-    )
-    gate_part = lax.ppermute(gate_part, PLANE, w_perm)
+        [pltpu.SMEM] + [pltpu.VMEM] * 2,
+    )
+    both_parts = lax.ppermute(both_parts, PLANE, w_perm)
     rows = lax.ppermute(rows, PLANE, w_perm)
-    up_part = lax.ppermute(up_part, PLANE, w_perm)
     down_part = lax.ppermute(down_part, PLANE, w_perm)
 
-    own_x, other_x = gather_plane(tokens)
-    own_c, other_c = gather_plane(cotangent)
-    xs, cots = own_x + other_x, own_c + other_c
+    xs = gather_plane(tokens)
+    cots = gather_plane(cotangent)
     macs = nj * count * width * hidden_width * 2
     joined = pltpu.VMEM((nj, count, hidden_width), BF)
     joined_shape = shape((nj, count, hidden_width), BF)
     acc = pltpu.VMEM((hidden_width, width), F32)
     dense = shape((width, hidden_width), BF)
 
-    def part_shapes(slots, n):
-        dims = (slots, n, part, hidden_width)
-        return [shape(dims, F32)] + [shape(dims, BF)] * (shards - 1)
-
-    def totals(n):
-        return pltpu.VMEM((n, count, hidden_width), F32)
-
-    def own(i, blocks_part):
+    parts = (shards // 2, nj, part, hidden_width)
+    part_shapes = [shape(parts, F32), shape(parts, BF)]
+
+    sums_scratch = [pltpu.VMEM((nj, count, hidden_width), F32)]
+
+    def project(i):
         return run(
-            functools.partial(own_kernel, shards, n_tok, i),
+            functools.partial(project_kernel, nj, i),
             [info, rows],
-            [*own_x, blocks_part],
-            part_shapes(1, n_tok) + [dense],
-            [totals(n_tok)],
-            macs // n_dp,
+            [*xs, both_parts],
+            part_shapes + [dense],
+            sums_scratch,
+            macs,
         )
 
-    *gate0, gate_dense = own(0, gate_part)
-    gate0 = spread(gate0)
-    *up0, up_dense = own(1, up_part)
-    up0 = spread(up0)
-    gate_up1 = run(
-        functools.partial(other_gate_up_kernel, shards, nj - n_tok),
-        [info],
-        [*other_x, gate_dense, up_dense],
-        part_shapes(2, nj - n_tok),
-        [totals(nj - n_tok)] * 2,
-        2 * macs * (n_dp - 1) // n_dp,
-    )
-    gate_up1 = spread(gate_up1)
-    *hidden_grads, down_dense = run(
-        functools.partial(hidden_grad_kernel, shards, nj, columns),
+    near_gate, far_gate, gate_dense = project(0)
+    gates = reduce(near_gate, far_gate)
+    near_up, far_up, up_dense = project(1)
+    ups = reduce(near_up, far_up)
+    near_hg, far_hg, down_dense = run(
+        functools.partial(hidden_grad_kernel, nj, columns),
         [info, down_rows],
         [*cots, down_part],
-        part_shapes(1, nj) + [shape((hidden_width, width), BF)],
-        [totals(nj)],
+        part_shapes + [shape((hidden_width, width), BF)],
+        sums_scratch,
         macs,
     )
-    hidden_grads = spread(hidden_grads)
+    hidden_grads = reduce(near_hg, far_hg)
     act = shape((nj, part, hidden_width), BF)
     sums, hidden = run(
-        functools.partial(hidden_kernel, shards),
-        [],
-        [*gate0, *up0, *gate_up1],
-        [shape((2, nj, part, hidden_width), F32), act],
-        [],
-        macs // 64,
+        hidden_kernel, [], [*gates, *ups], [shape((2, nj, part, hidden_width), F32), act], [], macs // 64
     )
     hiddens = gather(hidden)
     gate_act, up_act = run(act_grad_kernel, [], [sums, *hidden_grads], [act, act], [], macs // 64)
@@ -426,7 +408,7 @@
     staged = [acc, pltpu.VMEM((nj, count, width), BF), pltpu.SemaphoreType.DMA((nj,))]
     (down_grad,) = run(down_grad_kernel, [info, down_rows], [joined_hidden], [grad_shape], staged, macs, cots)
     gate_grad, joined_gate = run(
-        functools.partial(gate_grad_kernel, shards, nj),
+        functools.partial(gate_grad_kernel, shards, nj, n_tok),
         [info, rows],
         gate_acts,
         [grad_shape, joined_shape],

time: 164 us -> 147 us (0.90)
  waiting for transfers between devices: 82.9 us -> 66.8 us
    ppermute x2, waiting for transfers between devices: 26.5 us -> 17.4 us  [sum_plane(): arrived.append(lax.ppermute(total(parts), 'dp', xor_perm(n_dp, dx)))]
    ppermute x1, waiting for transfers between devices: 8.17 us -> 0.01 us  [body(): rows = lax.ppermute(rows, PLANE, w_perm)]
    ppermute x27 -> x20, waiting for transfers between devices: 36 us -> 43.3 us  [the longest x6 25.7 us: reduce(): arrived = lax.ppermute(far, ('shard', 'dp'), shard_perm(shards, n_dp, bit))]
    ppermute x1, waiting for transfers between devices: 3.51 us -> 0.01 us  [body(): down_part = lax.ppermute(down_part, PLANE, w_perm)]
    ppermute x2, starting transfers between devices: 5.18 us -> 7.83 us  [sum_plane(): arrived.append(lax.ppermute(total(parts), 'dp', xor_perm(n_dp, dx)))]
    ppermute x2, waiting for transfers between devices: 8.66 us -> 6.05 us  [gather_plane(): base = own if dx == 0 else lax.ppermute(own, 'dp', xor_perm(n_dp, dx))]
    ppermute x27 -> x20, starting transfers between devices: 38 us -> 35.5 us  [the longest x9 12 us: gather(): lax.ppermute(have[d], ('shard', 'dp'), shard_perm(shards, n_dp, bit))]
    ppermute x1, starting transfers between devices: 2.59 us -> 0.79 us  [body(): rows = lax.ppermute(rows, PLANE, w_perm)]
  transfers between devices with their start and end apart: 40 -> 33, of which waited for: 15 -> 16; matrix products, arithmetic and copies ran while one was open for 0% -> 0% of each run, Pallas kernels for 12% -> 13%
where the time goes in v2:
time: 147 us; the launch traced here: 146 us
  waiting for transfers between devices  66.8 us (45%)
  starting transfers between devices  57.3 us (39%)
  Pallas kernels  20.8 us (14%)
    ppermute x6, waiting for transfers between devices, reduce(): arrived = lax.ppermute(far, ('shard', 'dp'), shard_perm(shards, n_dp, bit))  25.7 us
    pallas_call x21, Pallas kernels, call(): pl.pallas_call(kernel, out_shape=outs, in_specs=smem(len(scalars)) + vmem...  20.8 us
    ppermute x9, waiting for transfers between devices, gather(): lax.ppermute(have[d], ('shard', 'dp'), shard_perm(shards, n_dp, bit))  17.6 us
    ppermute x2, waiting for transfers between devices, sum_plane(): arrived.append(lax.ppermute(total(parts), 'dp', xor_perm(n_dp, dx)))  17.4 us
    ppermute x9, starting transfers between devices, gather(): lax.ppermute(have[d], ('shard', 'dp'), shard_perm(shards, n_dp, bit))  12 us
    ppermute x4, starting transfers between devices, gather_plane(): got.append(lax.ppermute(base, 'tok', xor_perm(n_tok, dc)))  11.1 us
    ppermute x6, starting transfers between devices, reduce(): arrived = lax.ppermute(far, ('shard', 'dp'), shard_perm(shards, n_dp, bit))  10.6 us
    ppermute x2, starting transfers between devices, sum_plane(): arrived.append(lax.ppermute(total(parts), 'dp', xor_perm(n_dp, dx)))  7.83 us
  transfers between devices with their start and end apart: 33, of which 16 were waited for; matrix products, arithmetic and copies ran while one was open for 0% of the time, Pallas kernels for 13%

profile of v2, /device:TPU:0, one launch (start us, length us, event | category | flops | bytes accessed | tf_op | source)
XLA Modules:
  0.0 146.3 jit_solution(6727153301758089029)
XLA Ops:
  0.6 3.0 %collective-permute-start.2 = (bf16[256,1024]{1,0:T(8,128)(2,1)}, bf16[256,1024]{1,0:T(8,128)(2,1)S(1)}, u32[]{:S(2)}, u32[]{:S(2)}) collective-permute-start(bf16[256,1024]{1,0:T(8,128)(2,1)} %refs_0_.8), channel_id=1, source_target_pairs={{0,2},{2,0},{1,3},{3,1},{4,6},{6,4},{5,7},{7,5},{8,10},{10,8},{9,1... | collective-permute-start | bytes 1572872 | tf_op jit(solution)/shard_map/ppermute | solution.py:329
  4.3 3.0 %shard_map.119 = (s32[2,2,4]{2,1,0:T(2,128)}, bf16[16,128,128]{2,1,0:T(8,128)(2,1)}, bf16[8,128,128]{2,1,0:T(8,128)(2,1)}) custom-call(s32[4]{0:T(128)} %pad_add_fusion.info, s32[2,16]{1,0:T(2,128)} %gate_rows.1, s32[2,16]{1,0:T(2,128)} %up_rows.1, bf16[2,16,128,128]{3,2,1,0:T(8,128)(2,1)} %gate.1, bf16[2,16,128,128]{3,2,1,0:T(8,128)(2,1)} %up.1, ...), custom_call_target="tpu_custom_call" | custom-call | bytes 3932224 | tf_op jit(solution)/shard_map/pallas_call | solution.py:66
  9.0 3.4 %collective-permute-start.1 = (bf16[256,1024]{1,0:T(8,128)(2,1)S(1)}, bf16[256,1024]{1,0:T(8,128)(2,1)S(1)}, u32[]{:S(2)}, u32[]{:S(2)}) collective-permute-start(bf16[256,1024]{1,0:T(8,128)(2,1)S(1)} %copy-done), channel_id=1, source_target_pairs={{0,1},{1,0},{2,3},{3,2},{4,5},{5,4},{6,7},{7,6},{8,9},{9,8},{10,11... | collective-permute-start | bytes 1572872 | tf_op jit(solution)/shard_map/ppermute | solution.py:332
  12.5 4.2 %collective-permute-done.2.refs_2_.refs_6_ = bf16[256,1024]{1,0:T(8,128)(2,1)S(1)} collective-permute-done((bf16[256,1024]{1,0:T(8,128)(2,1)}, bf16[256,1024]{1,0:T(8,128)(2,1)S(1)}, u32[]{:S(2)}, u32[]{:S(2)}) %collective-permute-start.2) | collective-permute-done | bytes 524320 | tf_op jit(solution)/shard_map/ppermute | solution.py:329
  17.5 7.7 %collective-permute-start.12 = (bf16[256,1024]{1,0:T(8,128)(2,1)S(1)}, bf16[256,1024]{1,0:T(8,128)(2,1)S(1)}, u32[]{:S(2)}, u32[]{:S(2)}) collective-permute-start(bf16[256,1024]{1,0:T(8,128)(2,1)S(1)} %copy-done.1), channel_id=1, source_target_pairs={{0,1},{1,0},{2,3},{3,2},{4,5},{5,4},{6,7},{7,6},{8,9},{9,8},{10,11... | collective-permute-start | bytes 1572872 | tf_op jit(solution)/shard_map/ppermute | solution.py:332
  30.1 3.6 %collective-permute-start.7 = (bf16[2,4,64,256]{3,2,1,0:T(8,128)(2,1)S(1)}, bf16[2,4,64,256]{3,2,1,0:T(8,128)(2,1)S(1)}, u32[]{:S(2)}, u32[]{:S(2)}) collective-permute-start(bf16[2,4,64,256]{3,2,1,0:T(8,128)(2,1)S(1)} %get-tuple-element.46), channel_id=1, source_target_pairs={{0,6},{2,4},{4,2},{6,0},{8,14},{10,12},{12,10},{14,8},{1,7},{3,5},... | collective-permute-start | bytes 786440 | tf_op jit(solution)/shard_map/ppermute | solution.py:305
  36.8 4.4 %collective-permute-start.19 = (bf16[2,4,64,256]{3,2,1,0:T(8,128)(2,1)S(1)}, bf16[2,4,64,256]{3,2,1,0:T(8,128)(2,1)S(1)}, u32[]{:S(2)}, u32[]{:S(2)}) collective-permute-start(bf16[2,4,64,256]{3,2,1,0:T(8,128)(2,1)S(1)} %get-tuple-element.58), channel_id=1, source_target_pairs={{0,6},{2,4},{4,2},{6,0},{8,14},{10,12},{12,10},{14,8},{1,7},{3,5},... | collective-permute-start | bytes 786440 | tf_op jit(solution)/shard_map/ppermute | solution.py:305
  41.2 4.2 %collective-permute-done.7.arrived = bf16[2,4,64,256]{3,2,1,0:T(8,128)(2,1)S(1)} collective-permute-done((bf16[2,4,64,256]{3,2,1,0:T(8,128)(2,1)S(1)}, bf16[2,4,64,256]{3,2,1,0:T(8,128)(2,1)S(1)}, u32[]{:S(2)}, u32[]{:S(2)}) %collective-permute-start.7) | collective-permute-done | bytes 262176 | tf_op jit(solution)/shard_map/ppermute | solution.py:305
  45.5 2.2 %collective-permute-start.8 = (bf16[1,4,64,256]{3,2,1,0:T(8,128)(2,1)S(1)}, bf16[1,4,64,256]{3,2,1,0:T(8,128)(2,1)S(1)}, u32[]{:S(2)}, u32[]{:S(2)}) collective-permute-start(bf16[1,4,64,256]{3,2,1,0:T(8,128)(2,1)S(1)} %get-tuple-element.48), channel_id=1, source_target_pairs={{0,8},{2,10},{4,12},{6,14},{8,0},{10,2},{12,4},{14,6},{1,9},{3,11}... | collective-permute-start | bytes 393224 | tf_op jit(solution)/shard_map/ppermute | solution.py:305
  47.7 6.1 %collective-permute-done.5.arrived = bf16[2,4,64,256]{3,2,1,0:T(8,128)(2,1)S(1)} collective-permute-done((bf16[2,4,64,256]{3,2,1,0:T(8,128)(2,1)S(1)}, bf16[2,4,64,256]{3,2,1,0:T(8,128)(2,1)S(1)}, u32[]{:S(2)}, u32[]{:S(2)}) %collective-permute-start.5) | collective-permute-done | bytes 262176 | tf_op jit(solution)/shard_map/ppermute | solution.py:305
  54.1 6.6 %collective-permute-done.19.arrived = bf16[2,4,64,256]{3,2,1,0:T(8,128)(2,1)S(1)} collective-permute-done((bf16[2,4,64,256]{3,2,1,0:T(8,128)(2,1)S(1)}, bf16[2,4,64,256]{3,2,1,0:T(8,128)(2,1)S(1)}, u32[]{:S(2)}, u32[]{:S(2)}) %collective-permute-start.19) | collective-permute-done | bytes 262176 | tf_op jit(solution)/shard_map/ppermute | solution.py:305
  63.2 6.6 %collective-permute-done.20.last = bf16[1,4,64,256]{3,2,1,0:T(8,128)(2,1)S(1)} collective-permute-done((bf16[1,4,64,256]{3,2,1,0:T(8,128)(2,1)S(1)}, bf16[1,4,64,256]{3,2,1,0:T(8,128)(2,1)S(1)}, u32[]{:S(2)}, u32[]{:S(2)}) %collective-permute-start.20) | collective-permute-done | bytes 131104 | tf_op jit(solution)/shard_map/ppermute | solution.py:305
  70.0 2.9 %collective-permute-start.22 = (bf16[4,64,256]{2,1,0:T(8,128)(2,1)S(1)}, bf16[4,64,256]{2,1,0:T(8,128)(2,1)S(1)}, u32[]{:S(2)}, u32[]{:S(2)}) collective-permute-start(bf16[4,64,256]{2,1,0:T(8,128)(2,1)S(1)} %get-tuple-element.61.refs_0_), channel_id=1, source_target_pairs={{0,8},{2,10},{4,12},{6,14},{8,0},{10,2},{12,4},{14,6},{1,9},{3,11}... | collective-permute-start | bytes 393224 | tf_op jit(solution)/shard_map/ppermute | solution.py:319
  73.2 2.8 %collective-permute-start.10 = (bf16[4,64,256]{2,1,0:T(8,128)(2,1)S(1)}, bf16[4,64,256]{2,1,0:T(8,128)(2,1)S(1)}, u32[]{:S(2)}, u32[]{:S(2)}) collective-permute-start(bf16[4,64,256]{2,1,0:T(8,128)(2,1)S(1)} %get-tuple-element.49.refs_0_), channel_id=1, source_target_pairs={{0,8},{2,10},{4,12},{6,14},{8,0},{10,2},{12,4},{14,6},{1,9},{3,11}... | collective-permute-start | bytes 393224 | tf_op jit(solution)/shard_map/ppermute | solution.py:319
  76.1 5.3 %collective-permute-done.25.refs_2_ = bf16[4,64,256]{2,1,0:T(8,128)(2,1)S(1)} collective-permute-done((bf16[4,64,256]{2,1,0:T(8,128)(2,1)S(1)}, bf16[4,64,256]{2,1,0:T(8,128)(2,1)S(1)}, u32[]{:S(2)}, u32[]{:S(2)}) %collective-permute-start.25) | collective-permute-done | bytes 131104 | tf_op jit(solution)/shard_map/ppermute | solution.py:319
  81.4 2.9 %collective-permute-start.21 = (bf16[4,64,256]{2,1,0:T(8,128)(2,1)S(1)}, bf16[4,64,256]{2,1,0:T(8,128)(2,1)S(1)}, u32[]{:S(2)}, u32[]{:S(2)}) collective-permute-start(bf16[4,64,256]{2,1,0:T(8,128)(2,1)S(1)} %get-tuple-element.61.refs_0_), channel_id=1, source_target_pairs={{0,6},{2,4},{4,2},{6,0},{8,14},{10,12},{12,10},{14,8},{1,7},{3,5},... | collective-permute-start | bytes 393224 | tf_op jit(solution)/shard_map/ppermute | solution.py:319
  86.4 2.9 %collective-permute-start.9 = (bf16[4,64,256]{2,1,0:T(8,128)(2,1)S(1)}, bf16[4,64,256]{2,1,0:T(8,128)(2,1)S(1)}, u32[]{:S(2)}, u32[]{:S(2)}) collective-permute-start(bf16[4,64,256]{2,1,0:T(8,128)(2,1)S(1)} %get-tuple-element.49.refs_0_), channel_id=1, source_target_pairs={{0,6},{2,4},{4,2},{6,0},{8,14},{10,12},{12,10},{14,8},{1,7},{3,5},... | collective-permute-start | bytes 393224 | tf_op jit(solution)/shard_map/ppermute | solution.py:319
  89.4 2.8 %collective-permute-done.26.refs_3_ = bf16[4,64,256]{2,1,0:T(8,128)(2,1)S(1)} collective-permute-done((bf16[4,64,256]{2,1,0:T(8,128)(2,1)S(1)}, bf16[4,64,256]{2,1,0:T(8,128)(2,1)S(1)}, u32[]{:S(2)}, u32[]{:S(2)}) %collective-permute-start.26) | collective-permute-done | bytes 131104 | tf_op jit(solution)/shard_map/ppermute | solution.py:319
  95.1 2.8 %collective-permute-done.23.refs_3_ = bf16[4,64,256]{2,1,0:T(8,128)(2,1)S(1)} collective-permute-done((bf16[4,64,256]{2,1,0:T(8,128)(2,1)S(1)}, bf16[4,64,256]{2,1,0:T(8,128)(2,1)S(1)}, u32[]{:S(2)}, u32[]{:S(2)}) %collective-permute-start.23) | collective-permute-done | bytes 131104 | tf_op jit(solution)/shard_map/ppermute | solution.py:319
  100.7 2.7 %collective-permute-done.11.refs_3_ = bf16[4,64,256]{2,1,0:T(8,128)(2,1)S(1)} collective-permute-done((bf16[4,64,256]{2,1,0:T(8,128)(2,1)S(1)}, bf16[4,64,256]{2,1,0:T(8,128)(2,1)S(1)}, u32[]{:S(2)}, u32[]{:S(2)}) %collective-permute-start.11) | collective-permute-done | bytes 131104 | tf_op jit(solution)/shard_map/ppermute | solution.py:319
  109.8 4.5 %collective-permute-start.16 = (bf16[1,256,1024]{2,1,0:T(8,128)(2,1)S(1)}, bf16[1,256,1024]{2,1,0:T(8,128)(2,1)S(1)}, u32[]{:S(2)}, u32[]{:S(2)}) collective-permute-start(bf16[1,256,1024]{2,1,0:T(8,128)(2,1)S(1)} %get-tuple-element.53), channel_id=1, source_target_pairs={{0,1},{1,0},{2,3},{3,2},{4,5},{5,4},{6,7},{7,6},{8,9},{9,8},{10,11... | collective-permute-start | bytes 1572872 | tf_op jit(solution)/shard_map/ppermute | solution.py:435
  115.8 6.5 %collective-permute-start.18 = (bf16[256,1024]{1,0:T(8,128)(2,1)S(1)}, bf16[256,1024]{1,0:T(8,128)(2,1)S(1)}, u32[]{:S(2)}, u32[]{:S(2)}) collective-permute-start(bf16[256,1024]{1,0:T(8,128)(2,1)S(1)} %shard_map.127), channel_id=1, source_target_pairs={{0,2},{2,0},{1,3},{3,1},{4,6},{6,4},{5,7},{7,5},{8,10},{10,8},{9,1... | collective-permute-start | bytes 1572872 | tf_op jit(solution)/shard_map/ppermute | solution.py:440
  127.0 5.5 %collective-permute-done.29.refs_1_ = bf16[256,1024]{1,0:T(8,128)(2,1)S(1)} collective-permute-done((bf16[256,1024]{1,0:T(8,128)(2,1)S(1)}, bf16[256,1024]{1,0:T(8,128)(2,1)S(1)}, u32[]{:S(2)}, u32[]{:S(2)}) %collective-permute-start.29) | collective-permute-done | bytes 524320 | tf_op jit(solution)/shard_map/ppermute | solution.py:440
  133.5 11.9 %collective-permute-done.18.refs_1_ = bf16[256,1024]{1,0:T(8,128)(2,1)S(1)} collective-permute-done((bf16[256,1024]{1,0:T(8,128)(2,1)S(1)}, bf16[256,1024]{1,0:T(8,128)(2,1)S(1)}, u32[]{:S(2)}, u32[]{:S(2)}) %collective-permute-start.18) | collective-permute-done | bytes 524320 | tf_op jit(solution)/shard_map/ppermute | solution.py:440
  (74 shorter events, 36.8 us)
Async XLA Ops:
  0.6 16.0 %collective-permute-start.2 = (bf16[256,1024]{1,0:T(8,128)(2,1)}, bf16[256,1024]{1,0:T(8,128)(2,1)S(1)}, u32[]{:S(2)}, u32[]{:S(2)}) collective-permute-start(bf16[256,1024]{1,0:T(8,128)(2,1)} %refs_0_.8), channel_id=1, source_target_pairs={{0,2},{2,0},{1,3},{3,1},{4,6},{6,4},{5,7},{7,5},{8,10},{10,8},{9,1... | collective-permute-start | bytes 1572872 | tf_op jit(solution)/shard_map/ppermute | solution.py:329
  3.7 23.4 %collective-permute-start.13 = (bf16[256,1024]{1,0:T(8,128)(2,1)}, bf16[256,1024]{1,0:T(8,128)(2,1)S(1)}, u32[]{:S(2)}, u32[]{:S(2)}) collective-permute-start(bf16[256,1024]{1,0:T(8,128)(2,1)} %refs_0_.9), channel_id=1, source_target_pairs={{0,2},{2,0},{1,3},{3,1},{4,6},{6,4},{5,7},{7,5},{8,10},{10,8},{9,1... | collective-permute-start | bytes 1572872 | tf_op jit(solution)/shard_map/ppermute | solution.py:329
  7.3 19.7 %collective-permute-start.4 = (bf16[16,128,128]{2,1,0:T(8,128)(2,1)}, bf16[16,128,128]{2,1,0:T(8,128)(2,1)S(1)}, u32[]{:S(2)}, u32[]{:S(2)}) collective-permute-start(bf16[16,128,128]{2,1,0:T(8,128)(2,1)} %get-tuple-element.40), channel_id=1, source_target_pairs={{0,0},{8,1},{6,2},{14,3},{4,4},{12,5},{2,6},{10,7},{1,8},{9,9},{7,... | collective-permute-start | bytes 1572872 | tf_op jit(solution)/shard_map/ppermute | solution.py:349
  9.0 19.6 %collective-permute-start.1 = (bf16[256,1024]{1,0:T(8,128)(2,1)S(1)}, bf16[256,1024]{1,0:T(8,128)(2,1)S(1)}, u32[]{:S(2)}, u32[]{:S(2)}) collective-permute-start(bf16[256,1024]{1,0:T(8,128)(2,1)S(1)} %copy-done), channel_id=1, source_target_pairs={{0,1},{1,0},{2,3},{3,2},{4,5},{5,4},{6,7},{7,6},{8,9},{9,8},{10,11... | collective-permute-start | bytes 1572872 | tf_op jit(solution)/shard_map/ppermute | solution.py:332
  16.6 12.0 %collective-permute-start.3 = (bf16[256,1024]{1,0:T(8,128)(2,1)S(1)}, bf16[256,1024]{1,0:T(8,128)(2,1)S(1)}, u32[]{:S(2)}, u32[]{:S(2)}) collective-permute-start(bf16[256,1024]{1,0:T(8,128)(2,1)S(1)} %collective-permute-done.2.refs_2_.refs_6_), channel_id=1, source_target_pairs={{0,1},{1,0},{2,3},{3,2},{4,5},{5,4},{6,7},{7,6},{8,9},{9,8},{10,11... | collective-permute-start | bytes 1572872 | tf_op jit(solution)/shard_map/ppermute | solution.py:332
  17.5 17.8 %collective-permute-start.12 = (bf16[256,1024]{1,0:T(8,128)(2,1)S(1)}, bf16[256,1024]{1,0:T(8,128)(2,1)S(1)}, u32[]{:S(2)}, u32[]{:S(2)}) collective-permute-start(bf16[256,1024]{1,0:T(8,128)(2,1)S(1)} %copy-done.1), channel_id=1, source_target_pairs={{0,1},{1,0},{2,3},{3,2},{4,5},{5,4},{6,7},{7,6},{8,9},{9,8},{10,11... | collective-permute-start | bytes 1572872 | tf_op jit(solution)/shard_map/ppermute | solution.py:332
  30.1 15.3 %collective-permute-start.7 = (bf16[2,4,64,256]{3,2,1,0:T(8,128)(2,1)S(1)}, bf16[2,4,64,256]{3,2,1,0:T(8,128)(2,1)S(1)}, u32[]{:S(2)}, u32[]{:S(2)}) collective-permute-start(bf16[2,4,64,256]{3,2,1,0:T(8,128)(2,1)S(1)} %get-tuple-element.46), channel_id=1, source_target_pairs={{0,6},{2,4},{4,2},{6,0},{8,14},{10,12},{12,10},{14,8},{1,7},{3,5},... | collective-permute-start | bytes 786440 | tf_op jit(solution)/shard_map/ppermute | solution.py:305
  35.2 18.7 %collective-permute-start.5 = (bf16[2,4,64,256]{3,2,1,0:T(8,128)(2,1)S(1)}, bf16[2,4,64,256]{3,2,1,0:T(8,128)(2,1)S(1)}, u32[]{:S(2)}, u32[]{:S(2)}) collective-permute-start(bf16[2,4,64,256]{3,2,1,0:T(8,128)(2,1)S(1)} %get-tuple-element.42), channel_id=1, source_target_pairs={{0,6},{2,4},{4,2},{6,0},{8,14},{10,12},{12,10},{14,8},{1,7},{3,5},... | collective-permute-start | bytes 786440 | tf_op jit(solution)/shard_map/ppermute | solution.py:305
  36.8 23.9 %collective-permute-start.19 = (bf16[2,4,64,256]{3,2,1,0:T(8,128)(2,1)S(1)}, bf16[2,4,64,256]{3,2,1,0:T(8,128)(2,1)S(1)}, u32[]{:S(2)}, u32[]{:S(2)}) collective-permute-start(bf16[2,4,64,256]{3,2,1,0:T(8,128)(2,1)S(1)} %get-tuple-element.58), channel_id=1, source_target_pairs={{0,6},{2,4},{4,2},{6,0},{8,14},{10,12},{12,10},{14,8},{1,7},{3,5},... | collective-permute-start | bytes 786440 | tf_op jit(solution)/shard_map/ppermute | solution.py:305
  45.5 15.4 %collective-permute-start.8 = (bf16[1,4,64,256]{3,2,1,0:T(8,128)(2,1)S(1)}, bf16[1,4,64,256]{3,2,1,0:T(8,128)(2,1)S(1)}, u32[]{:S(2)}, u32[]{:S(2)}) collective-permute-start(bf16[1,4,64,256]{3,2,1,0:T(8,128)(2,1)S(1)} %get-tuple-element.48), channel_id=1, source_target_pairs={{0,8},{2,10},{4,12},{6,14},{8,0},{10,2},{12,4},{14,6},{1,9},{3,11}... | collective-permute-start | bytes 393224 | tf_op jit(solution)/shard_map/ppermute | solution.py:305
  69.9 11.4 %collective-permute-start.25 = (bf16[4,64,256]{2,1,0:T(8,128)(2,1)S(1)}, bf16[4,64,256]{2,1,0:T(8,128)(2,1)S(1)}, u32[]{:S(2)}, u32[]{:S(2)}) collective-permute-start(bf16[4,64,256]{2,1,0:T(8,128)(2,1)S(1)} %get-tuple-element.62.refs_0_), channel_id=1, source_target_pairs={{0,8},{2,10},{4,12},{6,14},{8,0},{10,2},{12,4},{14,6},{1,9},{3,11}... | collective-permute-start | bytes 393224 | tf_op jit(solution)/shard_map/ppermute | solution.py:319
  70.0 16.4 %collective-permute-start.22 = (bf16[4,64,256]{2,1,0:T(8,128)(2,1)S(1)}, bf16[4,64,256]{2,1,0:T(8,128)(2,1)S(1)}, u32[]{:S(2)}, u32[]{:S(2)}) collective-permute-start(bf16[4,64,256]{2,1,0:T(8,128)(2,1)S(1)} %get-tuple-element.61.refs_0_), channel_id=1, source_target_pairs={{0,8},{2,10},{4,12},{6,14},{8,0},{10,2},{12,4},{14,6},{1,9},{3,11}... | collective-permute-start | bytes 393224 | tf_op jit(solution)/shard_map/ppermute | solution.py:319
  72.9 13.5 %collective-permute-start.24 = (bf16[4,64,256]{2,1,0:T(8,128)(2,1)S(1)}, bf16[4,64,256]{2,1,0:T(8,128)(2,1)S(1)}, u32[]{:S(2)}, u32[]{:S(2)}) collective-permute-start(bf16[4,64,256]{2,1,0:T(8,128)(2,1)S(1)} %get-tuple-element.62.refs_0_), channel_id=1, source_target_pairs={{0,6},{2,4},{4,2},{6,0},{8,14},{10,12},{12,10},{14,8},{1,7},{3,5},... | collective-permute-start | bytes 393224 | tf_op jit(solution)/shard_map/ppermute | solution.py:319
  73.2 16.1 %collective-permute-start.10 = (bf16[4,64,256]{2,1,0:T(8,128)(2,1)S(1)}, bf16[4,64,256]{2,1,0:T(8,128)(2,1)S(1)}, u32[]{:S(2)}, u32[]{:S(2)}) collective-permute-start(bf16[4,64,256]{2,1,0:T(8,128)(2,1)S(1)} %get-tuple-element.49.refs_0_), channel_id=1, source_target_pairs={{0,8},{2,10},{4,12},{6,14},{8,0},{10,2},{12,4},{14,6},{1,9},{3,11}... | collective-permute-start | bytes 393224 | tf_op jit(solution)/shard_map/ppermute | solution.py:319
  81.4 10.9 %collective-permute-start.26 = (bf16[4,64,256]{2,1,0:T(8,128)(2,1)S(1)}, bf16[4,64,256]{2,1,0:T(8,128)(2,1)S(1)}, u32[]{:S(2)}, u32[]{:S(2)}) collective-permute-start(bf16[4,64,256]{2,1,0:T(8,128)(2,1)S(1)} %collective-permute-done.25.refs_2_), channel_id=1, source_target_pairs={{0,6},{2,4},{4,2},{6,0},{8,14},{10,12},{12,10},{14,8},{1,7},{3,5},... | collective-permute-start | bytes 393224 | tf_op jit(solution)/shard_map/ppermute | solution.py:319
  81.4 13.7 %collective-permute-start.21 = (bf16[4,64,256]{2,1,0:T(8,128)(2,1)S(1)}, bf16[4,64,256]{2,1,0:T(8,128)(2,1)S(1)}, u32[]{:S(2)}, u32[]{:S(2)}) collective-permute-start(bf16[4,64,256]{2,1,0:T(8,128)(2,1)S(1)} %get-tuple-element.61.refs_0_), channel_id=1, source_target_pairs={{0,6},{2,4},{4,2},{6,0},{8,14},{10,12},{12,10},{14,8},{1,7},{3,5},... | collective-permute-start | bytes 393224 | tf_op jit(solution)/shard_map/ppermute | solution.py:319
  86.4 11.5 %collective-permute-start.23 = (bf16[4,64,256]{2,1,0:T(8,128)(2,1)S(1)}, bf16[4,64,256]{2,1,0:T(8,128)(2,1)S(1)}, u32[]{:S(2)}, u32[]{:S(2)}) collective-permute-start(bf16[4,64,256]{2,1,0:T(8,128)(2,1)S(1)} %collective-permute-done.22.refs_2_), channel_id=1, source_target_pairs={{0,6},{2,4},{4,2},{6,0},{8,14},{10,12},{12,10},{14,8},{1,7},{3,5},... | collective-permute-start | bytes 393224 | tf_op jit(solution)/shard_map/ppermute | solution.py:319
  86.4 14.3 %collective-permute-start.9 = (bf16[4,64,256]{2,1,0:T(8,128)(2,1)S(1)}, bf16[4,64,256]{2,1,0:T(8,128)(2,1)S(1)}, u32[]{:S(2)}, u32[]{:S(2)}) collective-permute-start(bf16[4,64,256]{2,1,0:T(8,128)(2,1)S(1)} %get-tuple-element.49.refs_0_), channel_id=1, source_target_pairs={{0,6},{2,4},{4,2},{6,0},{8,14},{10,12},{12,10},{14,8},{1,7},{3,5},... | collective-permute-start | bytes 393224 | tf_op jit(solution)/shard_map/ppermute | solution.py:319
  89.3 14.0 %collective-permute-start.11 = (bf16[4,64,256]{2,1,0:T(8,128)(2,1)S(1)}, bf16[4,64,256]{2,1,0:T(8,128)(2,1)S(1)}, u32[]{:S(2)}, u32[]{:S(2)}) collective-permute-start(bf16[4,64,256]{2,1,0:T(8,128)(2,1)S(1)} %collective-permute-done.10.refs_2_), channel_id=1, source_target_pairs={{0,6},{2,4},{4,2},{6,0},{8,14},{10,12},{12,10},{14,8},{1,7},{3,5},... | collective-permute-start | bytes 393224 | tf_op jit(solution)/shard_map/ppermute | solution.py:319
  107.3 19.7 %collective-permute-start.27 = (bf16[1,256,1024]{2,1,0:T(8,128)(2,1)S(1)}, bf16[1,256,1024]{2,1,0:T(8,128)(2,1)S(1)}, u32[]{:S(2)}, u32[]{:S(2)}) collective-permute-start(bf16[1,256,1024]{2,1,0:T(8,128)(2,1)S(1)} %get-tuple-element.67), channel_id=1, source_target_pairs={{0,1},{1,0},{2,3},{3,2},{4,5},{5,4},{6,7},{7,6},{8,9},{9,8},{10,11... | collective-permute-start | bytes 1572872 | tf_op jit(solution)/shard_map/ppermute | solution.py:435
  109.1 15.1 %collective-permute-start.30 = (bf16[2,4,128,128]{3,2,1,0:T(8,128)(2,1)S(1)}, bf16[2,4,128,128]{3,2,1,0:T(8,128)(2,1)S(1)}, u32[]{:S(2)}, u32[]{:S(2)}) collective-permute-start(bf16[2,4,128,128]{3,2,1,0:T(8,128)(2,1)S(1)} %get-tuple-element.70), channel_id=1, source_target_pairs={{0,0},{1,8},{2,4},{3,12},{4,5},{5,13},{6,1},{7,9},{8,2},{9,10},{10... | collective-permute-start | bytes 786440 | tf_op jit(solution)/shard_map/ppermute | solution.py:446
  109.8 23.7 %collective-permute-start.16 = (bf16[1,256,1024]{2,1,0:T(8,128)(2,1)S(1)}, bf16[1,256,1024]{2,1,0:T(8,128)(2,1)S(1)}, u32[]{:S(2)}, u32[]{:S(2)}) collective-permute-start(bf16[1,256,1024]{2,1,0:T(8,128)(2,1)S(1)} %get-tuple-element.53), channel_id=1, source_target_pairs={{0,1},{1,0},{2,3},{3,2},{4,5},{5,4},{6,7},{7,6},{8,9},{9,8},{10,11... | collective-permute-start | bytes 1572872 | tf_op jit(solution)/shard_map/ppermute | solution.py:435
  114.4 18.2 %collective-permute-start.29 = (bf16[256,1024]{1,0:T(8,128)(2,1)S(1)}, bf16[256,1024]{1,0:T(8,128)(2,1)S(1)}, u32[]{:S(2)}, u32[]{:S(2)}) collective-permute-start(bf16[256,1024]{1,0:T(8,128)(2,1)S(1)} %shard_map.133), channel_id=1, source_target_pairs={{0,2},{2,0},{1,3},{3,1},{4,6},{6,4},{5,7},{7,5},{8,10},{10,8},{9,1... | collective-permute-start | bytes 1572872 | tf_op jit(solution)/shard_map/ppermute | solution.py:440
  115.8 29.5 %collective-permute-start.18 = (bf16[256,1024]{1,0:T(8,128)(2,1)S(1)}, bf16[256,1024]{1,0:T(8,128)(2,1)S(1)}, u32[]{:S(2)}, u32[]{:S(2)}) collective-permute-start(bf16[256,1024]{1,0:T(8,128)(2,1)S(1)} %shard_map.127), channel_id=1, source_target_pairs={{0,2},{2,0},{1,3},{3,1},{4,6},{6,4},{5,7},{7,5},{8,10},{10,8},{9,1... | collective-permute-start | bytes 1572872 | tf_op jit(solution)/shard_map/ppermute | solution.py:440
  (14 other events, 107.3 us)

commit v3 on v2

--- a/solution.py
+++ b/solution.py
@@ -78,8 +78,8 @@
     return pl.multiple_of(value * size, size)
 
 
-def down_places(info, down_rows, columns, per_owner):
-    first_row, first = info[Q] * columns, info[Z] * per_owner
+def down_places(info, down_rows, columns, per_owner, dx=0):
+    first_row, first = (info[Q] ^ dx) * columns, info[Z] * per_owner
     return lambda c, k: down_rows[first_row + c, first + k] - info[Z] * info[OWNED]
 
 
@@ -187,21 +187,25 @@
     up_act[...] = (hidden_grad * (gate * s)).astype(BF)
 
 
-def join_rows(joined, parts, z, n_tok):
+def join_kernel(shards, n_dp, n_tok, info, *refs):
+    parts, joined = refs[:shards], refs[shards:]
     rows = parts[0].shape[1]
-    for r in range(joined.shape[0]):
-        dx, dc = divmod(r, n_tok)
-        for d, part in enumerate(parts):
-            joined[r, pl.ds(aligned(z ^ d, rows), rows), :] = part[own_place(dx, d) * n_tok + dc]
-
-
-def weight_grad(acc, left, rights, stage, sems):
+    for dx in range(n_dp):
+        for dc in range(n_tok):
+            for d, part in enumerate(parts):
+                here = pl.ds(aligned(info[Z] ^ d, rows), rows)
+                joined[dx][dc, here, :] = part[own_place(dx, d) * n_tok + dc]
+
+
+def weight_grad(acc, lefts, rights, stage, sems):
     copies = [pltpu.make_async_copy(right, stage.at[r], sems.at[r]) for r, right in enumerate(rights)]
     for copy in copies:
         copy.start()
+    n_tok = lefts[0].shape[0]
     for r, copy in enumerate(copies):
         copy.wait()
-        term = lax.dot_general(left[r], stage[r], (((0,), (0,)), ((), ())), preferred_element_type=F32)
+        left = lefts[r // n_tok][r % n_tok]
+        term = lax.dot_general(left, stage[r], (((0,), (0,)), ((), ())), preferred_element_type=F32)
         if r == 0:
             acc[...] = term
         else:
@@ -214,14 +218,6 @@
         for k in range(per_owner):
             block = acc[c * size : (c + 1) * size, pl.ds(aligned(place(c, k), size), size)]
             out[c, k] = (block.T if transposed else block).astype(BF)
-
-
-def put_plane(keep, send, r, n_tok, value):
-    dx, dc = divmod(r, n_tok)
-    if dc == 0:
-        keep[dx][...] = value
-    else:
-        send[dx][dc - 1] = value.astype(BF)
 
 
 def sum_kernel(first, *refs):
@@ -239,47 +235,61 @@
         out[...] = source[...]
 
 
-def mixed_kernel(shards, n_dp, n_tok, info, *refs):
-    hiddens, dense = refs[:shards], refs[shards]
-    keep, send = refs[shards + 1 : shards + 1 + n_dp], refs[shards + 1 + n_dp : shards + 1 + 2 * n_dp]
-    joined = refs[shards + 1 + 2 * n_dp]
-    join_rows(joined, hiddens, info[Z], n_tok)
-    for r in reversed(range(joined.shape[0])):
-        put_plane(keep, send, r, n_tok, jnp.dot(joined[r], dense[...], preferred_element_type=F32))
-
-
-def down_grad_kernel(info, down_rows, joined, *refs):
-    *rights, grad, acc, stage, sems = refs
-    weight_grad(acc, joined, rights, stage, sems)
+def put_plane(keep, send, dc, value):
+    if dc == 0:
+        keep[...] = value
+    else:
+        send[dc - 1] = value.astype(BF)
+
+
+def mixed_kernel(n_dp, columns, info, down_rows, *refs):
+    hiddens, dense = refs[:n_dp], refs[n_dp]
+    others = refs[n_dp + 1 : 2 * n_dp]
+    keep, send = refs[2 * n_dp : 2 * n_dp + 2]
+    denses = [dense, *refs[2 * n_dp + 2 :]]
+    for dx in range(1, n_dp):
+        packed = others[dx - 1]
+        place = down_places(info, down_rows, columns, packed.shape[0] // columns, dx)
+        scatter_cols(denses[dx], packed, place, columns)
+    for dc in reversed(range(hiddens[0].shape[0])):
+        value = 0.0
+        for hidden, weights in zip(hiddens, denses):
+            value += jnp.dot(hidden[dc], weights[...], preferred_element_type=F32)
+        put_plane(keep, send, dc, value)
+
+
+def down_grad_kernel(n_dp, info, down_rows, *refs):
+    lefts = refs[:n_dp]
+    *rights, grad, acc, stage, sems = refs[n_dp:]
+    weight_grad(acc, lefts, rights, stage, sems)
     pick_blocks(grad, acc, down_places(info, down_rows, *grad.shape[:2]), False)
 
 
-def up_grad_kernel(rows, joined, *refs):
-    *rights, grad, acc, stage, sems = refs
-    weight_grad(acc, joined, rights, stage, sems)
-    pick_blocks(grad, acc, lambda c, k: rows[1, c, k], True)
-
-
-def gate_grad_kernel(shards, nj, n_tok, info, rows, *refs):
-    acts = refs[:shards]
-    xs = refs[shards : shards + nj]
-    grad, joined, acc, stage, sems = refs[shards + nj :]
-    join_rows(joined, acts, info[Z], n_tok)
-    weight_grad(acc, joined, xs, stage, sems)
-    pick_blocks(grad, acc, lambda c, k: rows[0, c, k], True)
-
-
-def tokens_grad_kernel(shards, n_dp, n_tok, info, *refs):
-    acts = refs[:shards]
-    joined_gate, gate_dense, up_dense = refs[shards : shards + 3]
-    keep, send = refs[shards + 3 : shards + 3 + n_dp], refs[shards + 3 + n_dp : shards + 3 + 2 * n_dp]
-    joined = refs[shards + 3 + 2 * n_dp]
-    join_rows(joined, acts, info[Z], n_tok)
-    contract = (((1,), (1,)), ((), ()))
-    for r in reversed(range(joined.shape[0])):
-        value = lax.dot_general(joined_gate[r], gate_dense[...], contract, preferred_element_type=F32)
-        value += lax.dot_general(joined[r], up_dense[...], contract, preferred_element_type=F32)
-        put_plane(keep, send, r, n_tok, value)
+def row_grad_kernel(n_dp, i, rows, *refs):
+    lefts = refs[:n_dp]
+    *rights, grad, acc, stage, sems = refs[n_dp:]
+    weight_grad(acc, lefts, rights, stage, sems)
+    pick_blocks(grad, acc, lambda c, k: rows[i, c, k], True)
+
+
+def tokens_grad_kernel(n_dp, *refs):
+    other_rows = refs[: n_dp - 1]
+    refs = refs[n_dp - 1 :]
+    sides = refs[:n_dp], refs[n_dp : 2 * n_dp]
+    gate_dense, up_dense = refs[2 * n_dp : 2 * n_dp + 2]
+    others = refs[2 * n_dp + 2 : 3 * n_dp + 1]
+    keep, send = refs[3 * n_dp + 1 : 3 * n_dp + 3]
+    scratch = refs[3 * n_dp + 3 :]
+    denses = [gate_dense, *scratch[: n_dp - 1]], [up_dense, *scratch[n_dp - 1 :]]
+    for i, side in enumerate(denses):
+        for packed, rows, dense in zip(others, other_rows, side[1:]):
+            scatter_rows(dense, packed, rows, i)
+    for dc in reversed(range(sides[0][0].shape[0])):
+        value = 0.0
+        for acts, side in zip(sides, denses):
+            for act, weights in zip(acts, side):
+                value += lax.dot_general(act[dc], weights[...], (((1,), (1,)), ((), ())), preferred_element_type=F32)
+        put_plane(keep, send, dc, value)
 
 
 def shape(dims, dtype):
@@ -353,8 +363,6 @@
     xs = gather_plane(tokens)
     cots = gather_plane(cotangent)
     macs = nj * count * width * hidden_width * 2
-    joined = pltpu.VMEM((nj, count, hidden_width), BF)
-    joined_shape = shape((nj, count, hidden_width), BF)
     acc = pltpu.VMEM((hidden_width, width), F32)
     dense = shape((width, hidden_width), BF)
 
@@ -385,60 +393,66 @@
         sums_scratch,
         macs,
     )
-    hidden_grads = reduce(near_hg, far_hg)
+    near_hg, last_hg = reduce(near_hg, far_hg)
     act = shape((nj, part, hidden_width), BF)
     sums, hidden = run(
         hidden_kernel, [], [*gates, *ups], [shape((2, nj, part, hidden_width), F32), act], [], macs // 64
     )
-    hiddens = gather(hidden)
-    gate_act, up_act = run(act_grad_kernel, [], [sums, *hidden_grads], [act, act], [], macs // 64)
-    gate_acts = gather(gate_act)
-    up_acts = gather(up_act)
-
-    plane_shapes = [shape((count, width), F32)] * n_dp + [shape((n_tok - 1, count, width), BF)] * n_dp
+    gate_act, up_act = run(act_grad_kernel, [], [sums, near_hg, last_hg], [act, act], [], macs // 64)
+
+    chip = shape((n_tok, count, hidden_width), BF)
+    others = range(1, n_dp)
+    to_dp = lambda a, dx: lax.ppermute(a, "dp", xor_perm(n_dp, dx))
+    other_both = [to_dp(both_parts, dx) for dx in others]
+    other_rows = [to_dp(rows, dx) for dx in others]
+    other_down = [to_dp(down_part, dx) for dx in others]
+
+    def join(own):
+        parts = gather(own)
+        joined = run(functools.partial(join_kernel, shards, n_dp, n_tok), [info], parts, [chip] * n_dp, [], 0)
+        return joined, [joined[0]] + [to_dp(joined[dx], dx) for dx in others]
+
+    all_hidden, chip_hidden = join(hidden)
+    all_gate, chip_gate = join(gate_act)
+    all_up, chip_up = join(up_act)
+
+    plane_shapes = [shape((count, width), F32), shape((n_tok - 1, count, width), BF)]
     grad_shape = shape((columns, per_owner, size, size), BF)
-    *mixed, joined_hidden = run(
-        functools.partial(mixed_kernel, shards, n_dp, n_tok),
-        [info],
-        [*hiddens, down_dense],
-        plane_shapes + [joined_shape],
-        [],
+    staged = [acc, pltpu.VMEM((nj, count, width), BF), pltpu.SemaphoreType.DMA((nj,))]
+    mixed = run(
+        functools.partial(mixed_kernel, n_dp, columns),
+        [info, down_rows],
+        [*chip_hidden, down_dense, *other_down],
+        plane_shapes,
+        [pltpu.VMEM((hidden_width, width), BF)] * (n_dp - 1),
         macs,
     )
-    staged = [acc, pltpu.VMEM((nj, count, width), BF), pltpu.SemaphoreType.DMA((nj,))]
-    (down_grad,) = run(down_grad_kernel, [info, down_rows], [joined_hidden], [grad_shape], staged, macs, cots)
-    gate_grad, joined_gate = run(
-        functools.partial(gate_grad_kernel, shards, nj, n_tok),
-        [info, rows],
-        gate_acts,
-        [grad_shape, joined_shape],
-        staged,
-        macs,
-        xs,
-    )
-    *tokens_terms, joined_up = run(
-        functools.partial(tokens_grad_kernel, shards, n_dp, n_tok),
-        [info],
-        [*up_acts, joined_gate, gate_dense, up_dense],
-        plane_shapes + [joined_shape],
-        [],
+    (down_grad,) = run(
+        functools.partial(down_grad_kernel, n_dp), [info, down_rows], all_hidden, [grad_shape], staged, macs, cots
+    )
+
+    def row_grad(i, lefts):
+        kernel = functools.partial(row_grad_kernel, n_dp, i)
+        return run(kernel, [rows], lefts, [grad_shape], staged, macs, xs)[0]
+
+    gate_grad = row_grad(0, all_gate)
+    up_grad = row_grad(1, all_up)
+    tokens_terms = run(
+        functools.partial(tokens_grad_kernel, n_dp),
+        other_rows,
+        [*chip_gate, *chip_up, gate_dense, up_dense, *other_both],
+        plane_shapes,
+        [pltpu.VMEM((width, hidden_width), BF)] * (2 * n_dp - 2),
         2 * macs,
     )
-    (up_grad,) = run(up_grad_kernel, [rows], [joined_up], [grad_shape], staged, macs, xs)
 
     def sum_plane(terms):
-        arrived = []
-        total = lambda parts: run(sum_kernel, [], parts, [shape((count, width), BF)], [], 0)[0]
-        for dx in reversed(range(n_dp)):
-            parts = [terms[dx]]
-            if n_tok == 2:
-                parts.append(lax.ppermute(terms[n_dp + dx], "tok", xor_perm(n_tok, 1)))
-            else:
-                for dc in range(1, n_tok):
-                    parts.append(lax.ppermute(terms[n_dp + dx][dc - 1], "tok", xor_perm(n_tok, dc)))
-            if dx:
-                arrived.append(lax.ppermute(total(parts), "dp", xor_perm(n_dp, dx)))
-        return total(parts + arrived)
+        keep, send = terms
+        if n_tok == 2:
+            arrived = [lax.ppermute(send, "tok", xor_perm(n_tok, 1))]
+        else:
+            arrived = [lax.ppermute(send[dc - 1], "tok", xor_perm(n_tok, dc)) for dc in range(1, n_tok)]
+        return run(sum_kernel, [], [keep, *arrived], [shape((count, width), BF)], [], 0)[0]
 
     g_perm = grad_perm(shards, n_dp, n_tok)
 

time: 147 us -> 153 us (1.041)
  the two profiles are of different devices: /device:TPU:0 before, /device:TPU:2 now
where the time goes in v3:
time: 153 us
  waiting for transfers between devices  76.3 us (50%)
  starting transfers between devices  52.9 us (35%)
  Pallas kernels  22.4 us (15%)
    pallas_call x22, Pallas kernels, call(): pl.pallas_call(kernel, out_shape=outs, in_specs=smem(len(scalars)) + vmem...  22.4 us
    ppermute x9, waiting for transfers between devices, gather(): lax.ppermute(have[d], ('shard', 'dp'), shard_perm(shards, n_dp, bit))  19.6 us
    ppermute x6, waiting for transfers between devices, reduce(): arrived = lax.ppermute(far, ('shard', 'dp'), shard_perm(shards, n_dp, bit))  19 us
    ppermute x6, waiting for transfers between devices, body(): to_dp = lambda a, dx: lax.ppermute(a, 'dp', xor_perm(n_dp, dx))  18.6 us
    ppermute x6, starting transfers between devices, reduce(): arrived = lax.ppermute(far, ('shard', 'dp'), shard_perm(shards, n_dp, bit))  13.2 us
    ppermute x3, waiting for transfers between devices, home(): grad = lax.ppermute(grad, PLANE, g_perm)  10.2 us
    ppermute x3, starting transfers between devices, home(): grad = lax.ppermute(grad, PLANE, g_perm)  9.39 us
    ppermute x9, starting transfers between devices, gather(): lax.ppermute(have[d], ('shard', 'dp'), shard_perm(shards, n_dp, bit))  9.16 us
  transfers between devices with their start and end apart: 35, of which 22 were waited for; matrix products, arithmetic and copies ran while one was open for 0% of the time, Pallas kernels for 14%

profile of v3, /device:TPU:2, one launch (start us, length us, event | category | flops | bytes accessed | tf_op | source)
XLA Modules:
  0.0 153.1 jit_solution(17807239997587266504)
XLA Ops:
  3.3 3.0 %shard_map.119 = (s32[2,2,4]{2,1,0:T(2,128)}, bf16[16,128,128]{2,1,0:T(8,128)(2,1)}, bf16[8,128,128]{2,1,0:T(8,128)(2,1)}) custom-call(s32[4]{0:T(128)} %pad_add_fusion.info, s32[2,16]{1,0:T(2,128)} %gate_rows.1, s32[2,16]{1,0:T(2,128)} %up_rows.1, bf16[2,16,128,128]{3,2,1,0:T(8,128)(2,1)} %gate.1, bf16[2,16,128,128]{3,2,1,0:T(8,128)(2,1)} %up.1, ...), custom_call_target="tpu_custom_call" | custom-call | bytes 3932224 | tf_op jit(solution)/shard_map/pallas_call | solution.py:66
  6.3 3.5 %collective-permute-start.4 = (bf16[16,128,128]{2,1,0:T(8,128)(2,1)}, bf16[16,128,128]{2,1,0:T(8,128)(2,1)S(1)}, u32[]{:S(2)}, u32[]{:S(2)}) collective-permute-start(bf16[16,128,128]{2,1,0:T(8,128)(2,1)} %get-tuple-element.38), channel_id=1, source_target_pairs={{0,0},{8,1},{6,2},{14,3},{4,4},{12,5},{2,6},{10,7},{1,8},{9,9},{7,... | collective-permute-start | bytes 1572872 | tf_op jit(solution)/shard_map/ppermute | solution.py:359
  12.0 3.7 %collective-permute-done.2.refs_2_.refs_4_ = bf16[256,1024]{1,0:T(8,128)(2,1)S(1)} collective-permute-done((bf16[256,1024]{1,0:T(8,128)(2,1)}, bf16[256,1024]{1,0:T(8,128)(2,1)S(1)}, u32[]{:S(2)}, u32[]{:S(2)}) %collective-permute-start.2) | collective-permute-done | bytes 524320 | tf_op jit(solution)/shard_map/ppermute | solution.py:339
  15.7 3.6 %collective-permute-start = (s32[2,2,4]{2,1,0:T(2,128)S(1)}, s32[2,2,4]{2,1,0:T(2,128)S(1)}, u32[]{:S(2)}, u32[]{:S(2)}) collective-permute-start(s32[2,2,4]{2,1,0:T(2,128)S(1)} %copy-done.4), channel_id=1, source_target_pairs={{0,0},{8,1},{6,2},{14,3},{4,4},{12,5},{2,6},{10,7},{1,8},{9,9},{7,... | collective-permute-start | bytes 200 | tf_op jit(solution)/shard_map/ppermute | solution.py:360
  25.8 3.5 %collective-permute-start.16 = (bf16[8,128,128]{2,1,0:T(8,128)(2,1)}, bf16[8,128,128]{2,1,0:T(8,128)(2,1)S(1)}, u32[]{:S(2)}, u32[]{:S(2)}) collective-permute-start(bf16[8,128,128]{2,1,0:T(8,128)(2,1)} %get-tuple-element.50), channel_id=1, source_target_pairs={{0,0},{8,1},{6,2},{14,3},{4,4},{12,5},{2,6},{10,7},{1,8},{9,9},{7,... | collective-permute-start | bytes 786440 | tf_op jit(solution)/shard_map/ppermute | solution.py:361
  32.3 3.0 %collective-permute-start.5 = (bf16[2,4,64,256]{3,2,1,0:T(8,128)(2,1)S(1)}, bf16[2,4,64,256]{3,2,1,0:T(8,128)(2,1)S(1)}, u32[]{:S(2)}, u32[]{:S(2)}) collective-permute-start(bf16[2,4,64,256]{3,2,1,0:T(8,128)(2,1)S(1)} %get-tuple-element.40), channel_id=1, source_target_pairs={{0,6},{2,4},{4,2},{6,0},{8,14},{10,12},{12,10},{14,8},{1,7},{3,5},... | collective-permute-start | bytes 786440 | tf_op jit(solution)/shard_map/ppermute | solution.py:315
  37.4 3.8 %collective-permute-done.7.arrived = bf16[2,4,64,256]{3,2,1,0:T(8,128)(2,1)S(1)} collective-permute-done((bf16[2,4,64,256]{3,2,1,0:T(8,128)(2,1)S(1)}, bf16[2,4,64,256]{3,2,1,0:T(8,128)(2,1)S(1)}, u32[]{:S(2)}, u32[]{:S(2)}) %collective-permute-start.7) | collective-permute-done | bytes 262176 | tf_op jit(solution)/shard_map/ppermute | solution.py:315
  43.3 3.5 %collective-permute-done.5.arrived = bf16[2,4,64,256]{3,2,1,0:T(8,128)(2,1)S(1)} collective-permute-done((bf16[2,4,64,256]{3,2,1,0:T(8,128)(2,1)S(1)}, bf16[2,4,64,256]{3,2,1,0:T(8,128)(2,1)S(1)}, u32[]{:S(2)}, u32[]{:S(2)}) %collective-permute-start.5) | collective-permute-done | bytes 262176 | tf_op jit(solution)/shard_map/ppermute | solution.py:315
  46.9 4.8 %collective-permute-start.6 = (bf16[1,4,64,256]{3,2,1,0:T(8,128)(2,1)S(1)}, bf16[1,4,64,256]{3,2,1,0:T(8,128)(2,1)S(1)}, u32[]{:S(2)}, u32[]{:S(2)}) collective-permute-start(bf16[1,4,64,256]{3,2,1,0:T(8,128)(2,1)S(1)} %get-tuple-element.42), channel_id=1, source_target_pairs={{0,8},{2,10},{4,12},{6,14},{8,0},{10,2},{12,4},{14,6},{1,9},{3,11}... | collective-permute-start | bytes 393224 | tf_op jit(solution)/shard_map/ppermute | solution.py:315
  51.6 3.6 %collective-permute-done.20.arrived = bf16[2,4,64,256]{3,2,1,0:T(8,128)(2,1)S(1)} collective-permute-done((bf16[2,4,64,256]{3,2,1,0:T(8,128)(2,1)S(1)}, bf16[2,4,64,256]{3,2,1,0:T(8,128)(2,1)S(1)}, u32[]{:S(2)}, u32[]{:S(2)}) %collective-permute-start.20) | collective-permute-done | bytes 262176 | tf_op jit(solution)/shard_map/ppermute | solution.py:315
  55.3 3.3 %collective-permute-start.21 = (bf16[1,4,64,256]{3,2,1,0:T(8,128)(2,1)S(1)}, bf16[1,4,64,256]{3,2,1,0:T(8,128)(2,1)S(1)}, u32[]{:S(2)}, u32[]{:S(2)}) collective-permute-start(bf16[1,4,64,256]{3,2,1,0:T(8,128)(2,1)S(1)} %get-tuple-element.58), channel_id=1, source_target_pairs={{0,8},{2,10},{4,12},{6,14},{8,0},{10,2},{12,4},{14,6},{1,9},{3,11}... | collective-permute-start | bytes 393224 | tf_op jit(solution)/shard_map/ppermute | solution.py:315
  58.7 8.1 %collective-permute-done.21.last = bf16[1,4,64,256]{3,2,1,0:T(8,128)(2,1)S(1)} collective-permute-done((bf16[1,4,64,256]{3,2,1,0:T(8,128)(2,1)S(1)}, bf16[1,4,64,256]{3,2,1,0:T(8,128)(2,1)S(1)}, u32[]{:S(2)}, u32[]{:S(2)}) %collective-permute-start.21) | collective-permute-done | bytes 131104 | tf_op jit(solution)/shard_map/ppermute | solution.py:315
  67.1 3.2 %collective-permute-start.26 = (bf16[4,64,256]{2,1,0:T(8,128)(2,1)S(1)}, bf16[4,64,256]{2,1,0:T(8,128)(2,1)S(1)}, u32[]{:S(2)}, u32[]{:S(2)}) collective-permute-start(bf16[4,64,256]{2,1,0:T(8,128)(2,1)S(1)} %get-tuple-element.62.refs_0_), channel_id=1, source_target_pairs={{0,6},{2,4},{4,2},{6,0},{8,14},{10,12},{12,10},{14,8},{1,7},{3,5},... | collective-permute-start | bytes 393224 | tf_op jit(solution)/shard_map/ppermute | solution.py:329
  72.3 2.8 %collective-permute-start.10 = (bf16[4,64,256]{2,1,0:T(8,128)(2,1)S(1)}, bf16[4,64,256]{2,1,0:T(8,128)(2,1)S(1)}, u32[]{:S(2)}, u32[]{:S(2)}) collective-permute-start(bf16[4,64,256]{2,1,0:T(8,128)(2,1)S(1)} %get-tuple-element.47.refs_0_), channel_id=1, source_target_pairs={{0,8},{2,10},{4,12},{6,14},{8,0},{10,2},{12,4},{14,6},{1,9},{3,11}... | collective-permute-start | bytes 393224 | tf_op jit(solution)/shard_map/ppermute | solution.py:329
  79.6 4.6 %collective-permute-done.23.refs_2_ = bf16[4,64,256]{2,1,0:T(8,128)(2,1)S(1)} collective-permute-done((bf16[4,64,256]{2,1,0:T(8,128)(2,1)S(1)}, bf16[4,64,256]{2,1,0:T(8,128)(2,1)S(1)}, u32[]{:S(2)}, u32[]{:S(2)}) %collective-permute-start.23) | collective-permute-done | bytes 131104 | tf_op jit(solution)/shard_map/ppermute | solution.py:329
  84.2 2.8 %collective-permute-done.10.refs_2_ = bf16[4,64,256]{2,1,0:T(8,128)(2,1)S(1)} collective-permute-done((bf16[4,64,256]{2,1,0:T(8,128)(2,1)S(1)}, bf16[4,64,256]{2,1,0:T(8,128)(2,1)S(1)}, u32[]{:S(2)}, u32[]{:S(2)}) %collective-permute-start.10) | collective-permute-done | bytes 131104 | tf_op jit(solution)/shard_map/ppermute | solution.py:329
  92.5 2.5 %collective-permute-done.24.refs_3_ = bf16[4,64,256]{2,1,0:T(8,128)(2,1)S(1)} collective-permute-done((bf16[4,64,256]{2,1,0:T(8,128)(2,1)S(1)}, bf16[4,64,256]{2,1,0:T(8,128)(2,1)S(1)}, u32[]{:S(2)}, u32[]{:S(2)}) %collective-permute-start.24) | collective-permute-done | bytes 131104 | tf_op jit(solution)/shard_map/ppermute | solution.py:329
  100.6 10.7 %collective-permute-done.19.refs_0_ = s32[2,2,4]{2,1,0:T(2,128)S(1)} collective-permute-done((s32[2,2,4]{2,1,0:T(2,128)S(1)}, s32[2,2,4]{2,1,0:T(2,128)S(1)}, u32[]{:S(2)}, u32[]{:S(2)}) %collective-permute-start.19) | collective-permute-done | bytes 96 | tf_op jit(solution)/shard_map/ppermute | solution.py:405
  114.6 2.4 %collective-permute-done.17.refs_3_ = bf16[8,128,128]{2,1,0:T(8,128)(2,1)S(1)} collective-permute-done((bf16[8,128,128]{2,1,0:T(8,128)(2,1)S(1)}, bf16[8,128,128]{2,1,0:T(8,128)(2,1)S(1)}, u32[]{:S(2)}, u32[]{:S(2)}) %collective-permute-start.17) | collective-permute-done | bytes 262176 | tf_op jit(solution)/shard_map/ppermute | solution.py:405
  117.0 5.5 %collective-permute-done.12.refs_1_ = bf16[2,256,256]{2,1,0:T(8,128)(2,1)S(1)} collective-permute-done((bf16[2,256,256]{2,1,0:T(8,128)(2,1)S(1)}, bf16[2,256,256]{2,1,0:T(8,128)(2,1)S(1)}, u32[]{:S(2)}, u32[]{:S(2)}) %collective-permute-start.12) | collective-permute-done | bytes 262176 | tf_op jit(solution)/shard_map/ppermute | solution.py:405
  125.8 4.4 %collective-permute-start.33 = (bf16[2,4,128,128]{3,2,1,0:T(8,128)(2,1)S(1)}, bf16[2,4,128,128]{3,2,1,0:T(8,128)(2,1)S(1)}, u32[]{:S(2)}, u32[]{:S(2)}) collective-permute-start(bf16[2,4,128,128]{3,2,1,0:T(8,128)(2,1)S(1)} %shard_map.137), channel_id=1, source_target_pairs={{0,0},{1,8},{2,4},{3,12},{4,5},{5,13},{6,1},{7,9},{8,2},{9,10},{10... | collective-permute-start | bytes 786440 | tf_op jit(solution)/shard_map/ppermute | solution.py:460
  132.1 2.4 %collective-permute-start.32 = (bf16[2,4,128,128]{3,2,1,0:T(8,128)(2,1)S(1)}, bf16[2,4,128,128]{3,2,1,0:T(8,128)(2,1)S(1)}, u32[]{:S(2)}, u32[]{:S(2)}) collective-permute-start(bf16[2,4,128,128]{3,2,1,0:T(8,128)(2,1)S(1)} %shard_map.135), channel_id=1, source_target_pairs={{0,0},{1,8},{2,4},{3,12},{4,5},{5,13},{6,1},{7,9},{8,2},{9,10},{10... | collective-permute-start | bytes 786440 | tf_op jit(solution)/shard_map/ppermute | solution.py:460
  136.3 2.6 %collective-permute-start.34 = (bf16[2,4,128,128]{3,2,1,0:T(8,128)(2,1)S(1)}, bf16[2,4,128,128]{3,2,1,0:T(8,128)(2,1)S(1)}, u32[]{:S(2)}, u32[]{:S(2)}) collective-permute-start(bf16[2,4,128,128]{3,2,1,0:T(8,128)(2,1)S(1)} %shard_map.139), channel_id=1, source_target_pairs={{0,0},{1,8},{2,4},{3,12},{4,5},{5,13},{6,1},{7,9},{8,2},{9,10},{10... | collective-permute-start | bytes 786440 | tf_op jit(solution)/shard_map/ppermute | solution.py:460
  139.6 8.1 %collective-permute-done.32.refs_0_ = bf16[2,4,128,128]{3,2,1,0:T(8,128)(2,1)S(1)} collective-permute-done((bf16[2,4,128,128]{3,2,1,0:T(8,128)(2,1)S(1)}, bf16[2,4,128,128]{3,2,1,0:T(8,128)(2,1)S(1)}, u32[]{:S(2)}, u32[]{:S(2)}) %collective-permute-start.32) | collective-permute-done | bytes 262176 | tf_op jit(solution)/shard_map/ppermute | solution.py:460
  (79 shorter events, 52.8 us)
Async XLA Ops:
  0.6 15.1 %collective-permute-start.2 = (bf16[256,1024]{1,0:T(8,128)(2,1)}, bf16[256,1024]{1,0:T(8,128)(2,1)S(1)}, u32[]{:S(2)}, u32[]{:S(2)}) collective-permute-start(bf16[256,1024]{1,0:T(8,128)(2,1)} %refs_2_.4), channel_id=1, source_target_pairs={{0,2},{2,0},{1,3},{3,1},{4,6},{6,4},{5,7},{7,5},{8,10},{10,8},{9,1... | collective-permute-start | bytes 1572872 | tf_op jit(solution)/shard_map/ppermute | solution.py:339
  0.7 25.1 %collective-permute-start.14 = (bf16[256,1024]{1,0:T(8,128)(2,1)}, bf16[256,1024]{1,0:T(8,128)(2,1)S(1)}, u32[]{:S(2)}, u32[]{:S(2)}) collective-permute-start(bf16[256,1024]{1,0:T(8,128)(2,1)} %refs_2_.5), channel_id=1, source_target_pairs={{0,2},{2,0},{1,3},{3,1},{4,6},{6,4},{5,7},{7,5},{8,10},{10,8},{9,1... | collective-permute-start | bytes 1572872 | tf_op jit(solution)/shard_map/ppermute | solution.py:339
  6.3 19.5 %collective-permute-start.4 = (bf16[16,128,128]{2,1,0:T(8,128)(2,1)}, bf16[16,128,128]{2,1,0:T(8,128)(2,1)S(1)}, u32[]{:S(2)}, u32[]{:S(2)}) collective-permute-start(bf16[16,128,128]{2,1,0:T(8,128)(2,1)} %get-tuple-element.38), channel_id=1, source_target_pairs={{0,0},{8,1},{6,2},{14,3},{4,4},{12,5},{2,6},{10,7},{1,8},{9,9},{7,... | collective-permute-start | bytes 1572872 | tf_op jit(solution)/shard_map/ppermute | solution.py:359
  9.8 19.5 %collective-permute-start.1 = (bf16[256,1024]{1,0:T(8,128)(2,1)S(1)}, bf16[256,1024]{1,0:T(8,128)(2,1)S(1)}, u32[]{:S(2)}, u32[]{:S(2)}) collective-permute-start(bf16[256,1024]{1,0:T(8,128)(2,1)S(1)} %copy-done), channel_id=1, source_target_pairs={{0,1},{1,0},{2,3},{3,2},{4,5},{5,4},{6,7},{7,6},{8,9},{9,8},{10,11... | collective-permute-start | bytes 1572872 | tf_op jit(solution)/shard_map/ppermute | solution.py:342
  15.7 13.6 %collective-permute-start.3 = (bf16[256,1024]{1,0:T(8,128)(2,1)S(1)}, bf16[256,1024]{1,0:T(8,128)(2,1)S(1)}, u32[]{:S(2)}, u32[]{:S(2)}) collective-permute-start(bf16[256,1024]{1,0:T(8,128)(2,1)S(1)} %collective-permute-done.2.refs_2_.refs_4_), channel_id=1, source_target_pairs={{0,1},{1,0},{2,3},{3,2},{4,5},{5,4},{6,7},{7,6},{8,9},{9,8},{10,11... | collective-permute-start | bytes 1572872 | tf_op jit(solution)/shard_map/ppermute | solution.py:342
  21.7 14.1 %collective-permute-start.13 = (bf16[256,1024]{1,0:T(8,128)(2,1)S(1)}, bf16[256,1024]{1,0:T(8,128)(2,1)S(1)}, u32[]{:S(2)}, u32[]{:S(2)}) collective-permute-start(bf16[256,1024]{1,0:T(8,128)(2,1)S(1)} %copy-done.1), channel_id=1, source_target_pairs={{0,1},{1,0},{2,3},{3,2},{4,5},{5,4},{6,7},{7,6},{8,9},{9,8},{10,11... | collective-permute-start | bytes 1572872 | tf_op jit(solution)/shard_map/ppermute | solution.py:342
  32.3 14.5 %collective-permute-start.5 = (bf16[2,4,64,256]{3,2,1,0:T(8,128)(2,1)S(1)}, bf16[2,4,64,256]{3,2,1,0:T(8,128)(2,1)S(1)}, u32[]{:S(2)}, u32[]{:S(2)}) collective-permute-start(bf16[2,4,64,256]{3,2,1,0:T(8,128)(2,1)S(1)} %get-tuple-element.40), channel_id=1, source_target_pairs={{0,6},{2,4},{4,2},{6,0},{8,14},{10,12},{12,10},{14,8},{1,7},{3,5},... | collective-permute-start | bytes 786440 | tf_op jit(solution)/shard_map/ppermute | solution.py:315
  37.4 17.9 %collective-permute-start.20 = (bf16[2,4,64,256]{3,2,1,0:T(8,128)(2,1)S(1)}, bf16[2,4,64,256]{3,2,1,0:T(8,128)(2,1)S(1)}, u32[]{:S(2)}, u32[]{:S(2)}) collective-permute-start(bf16[2,4,64,256]{3,2,1,0:T(8,128)(2,1)S(1)} %get-tuple-element.56), channel_id=1, source_target_pairs={{0,6},{2,4},{4,2},{6,0},{8,14},{10,12},{12,10},{14,8},{1,7},{3,5},... | collective-permute-start | bytes 786440 | tf_op jit(solution)/shard_map/ppermute | solution.py:315
  41.3 17.4 %collective-permute-start.8 = (bf16[1,4,64,256]{3,2,1,0:T(8,128)(2,1)S(1)}, bf16[1,4,64,256]{3,2,1,0:T(8,128)(2,1)S(1)}, u32[]{:S(2)}, u32[]{:S(2)}) collective-permute-start(bf16[1,4,64,256]{3,2,1,0:T(8,128)(2,1)S(1)} %get-tuple-element.46), channel_id=1, source_target_pairs={{0,8},{2,10},{4,12},{6,14},{8,0},{10,2},{12,4},{14,6},{1,9},{3,11}... | collective-permute-start | bytes 393224 | tf_op jit(solution)/shard_map/ppermute | solution.py:315
  46.9 11.8 %collective-permute-start.6 = (bf16[1,4,64,256]{3,2,1,0:T(8,128)(2,1)S(1)}, bf16[1,4,64,256]{3,2,1,0:T(8,128)(2,1)S(1)}, u32[]{:S(2)}, u32[]{:S(2)}) collective-permute-start(bf16[1,4,64,256]{3,2,1,0:T(8,128)(2,1)S(1)} %get-tuple-element.42), channel_id=1, source_target_pairs={{0,8},{2,10},{4,12},{6,14},{8,0},{10,2},{12,4},{14,6},{1,9},{3,11}... | collective-permute-start | bytes 393224 | tf_op jit(solution)/shard_map/ppermute | solution.py:315
  70.2 14.0 %collective-permute-start.23 = (bf16[4,64,256]{2,1,0:T(8,128)(2,1)S(1)}, bf16[4,64,256]{2,1,0:T(8,128)(2,1)S(1)}, u32[]{:S(2)}, u32[]{:S(2)}) collective-permute-start(bf16[4,64,256]{2,1,0:T(8,128)(2,1)S(1)} %get-tuple-element.59.refs_0_), channel_id=1, source_target_pairs={{0,8},{2,10},{4,12},{6,14},{8,0},{10,2},{12,4},{14,6},{1,9},{3,11}... | collective-permute-start | bytes 393224 | tf_op jit(solution)/shard_map/ppermute | solution.py:329
  70.3 42.2 %collective-permute-start.30 = (bf16[16,128,128]{2,1,0:T(8,128)(2,1)S(1)}, bf16[16,128,128]{2,1,0:T(8,128)(2,1)S(1)}, u32[]{:S(2)}, u32[]{:S(2)}) collective-permute-start(bf16[16,128,128]{2,1,0:T(8,128)(2,1)S(1)} %collective-permute-done.4.refs_4_), channel_id=1, source_target_pairs={{0,2},{2,0},{1,3},{3,1},{4,6},{6,4},{5,7},{7,5},{8,10},{10,8},{9,1... | collective-permute-start | bytes 1572872 | tf_op jit(solution)/shard_map/ppermute | solution.py:405
  72.3 14.7 %collective-permute-start.10 = (bf16[4,64,256]{2,1,0:T(8,128)(2,1)S(1)}, bf16[4,64,256]{2,1,0:T(8,128)(2,1)S(1)}, u32[]{:S(2)}, u32[]{:S(2)}) collective-permute-start(bf16[4,64,256]{2,1,0:T(8,128)(2,1)S(1)} %get-tuple-element.47.refs_0_), channel_id=1, source_target_pairs={{0,8},{2,10},{4,12},{6,14},{8,0},{10,2},{12,4},{14,6},{1,9},{3,11}... | collective-permute-start | bytes 393224 | tf_op jit(solution)/shard_map/ppermute | solution.py:329
  76.6 12.6 %collective-permute-start.28 = (bf16[4,64,256]{2,1,0:T(8,128)(2,1)S(1)}, bf16[4,64,256]{2,1,0:T(8,128)(2,1)S(1)}, u32[]{:S(2)}, u32[]{:S(2)}) collective-permute-start(bf16[4,64,256]{2,1,0:T(8,128)(2,1)S(1)} %collective-permute-done.27.refs_2_), channel_id=1, source_target_pairs={{0,6},{2,4},{4,2},{6,0},{8,14},{10,12},{12,10},{14,8},{1,7},{3,5},... | collective-permute-start | bytes 393224 | tf_op jit(solution)/shard_map/ppermute | solution.py:329
  77.6 14.5 %collective-permute-start.22 = (bf16[4,64,256]{2,1,0:T(8,128)(2,1)S(1)}, bf16[4,64,256]{2,1,0:T(8,128)(2,1)S(1)}, u32[]{:S(2)}, u32[]{:S(2)}) collective-permute-start(bf16[4,64,256]{2,1,0:T(8,128)(2,1)S(1)} %get-tuple-element.59.refs_0_), channel_id=1, source_target_pairs={{0,6},{2,4},{4,2},{6,0},{8,14},{10,12},{12,10},{14,8},{1,7},{3,5},... | collective-permute-start | bytes 393224 | tf_op jit(solution)/shard_map/ppermute | solution.py:329
  92.1 20.4 %collective-permute-start.29 = (bf16[2,256,256]{2,1,0:T(8,128)(2,1)S(1)}, bf16[2,256,256]{2,1,0:T(8,128)(2,1)S(1)}, u32[]{:S(2)}, u32[]{:S(2)}) collective-permute-start(bf16[2,256,256]{2,1,0:T(8,128)(2,1)S(1)} %get-tuple-element.64.refs_1_), channel_id=1, source_target_pairs={{0,2},{2,0},{1,3},{3,1},{4,6},{6,4},{5,7},{7,5},{8,10},{10,8},{9,1... | collective-permute-start | bytes 786440 | tf_op jit(solution)/shard_map/ppermute | solution.py:405
  95.6 16.9 %collective-permute-start.25 = (bf16[2,256,256]{2,1,0:T(8,128)(2,1)S(1)}, bf16[2,256,256]{2,1,0:T(8,128)(2,1)S(1)}, u32[]{:S(2)}, u32[]{:S(2)}) collective-permute-start(bf16[2,256,256]{2,1,0:T(8,128)(2,1)S(1)} %get-tuple-element.61.refs_1_), channel_id=1, source_target_pairs={{0,2},{2,0},{1,3},{3,1},{4,6},{6,4},{5,7},{7,5},{8,10},{10,8},{9,1... | collective-permute-start | bytes 786440 | tf_op jit(solution)/shard_map/ppermute | solution.py:405
  97.8 13.5 %collective-permute-start.19 = (s32[2,2,4]{2,1,0:T(2,128)S(1)}, s32[2,2,4]{2,1,0:T(2,128)S(1)}, u32[]{:S(2)}, u32[]{:S(2)}) collective-permute-start(s32[2,2,4]{2,1,0:T(2,128)S(1)} %collective-permute-done.rows), channel_id=1, source_target_pairs={{0,2},{2,0},{1,3},{3,1},{4,6},{6,4},{5,7},{7,5},{8,10},{10,8},{9,1... | collective-permute-start | bytes 200 | tf_op jit(solution)/shard_map/ppermute | solution.py:405
  100.1 16.9 %collective-permute-start.17 = (bf16[8,128,128]{2,1,0:T(8,128)(2,1)S(1)}, bf16[8,128,128]{2,1,0:T(8,128)(2,1)S(1)}, u32[]{:S(2)}, u32[]{:S(2)}) collective-permute-start(bf16[8,128,128]{2,1,0:T(8,128)(2,1)S(1)} %collective-permute-done.16.refs_4_), channel_id=1, source_target_pairs={{0,2},{2,0},{1,3},{3,1},{4,6},{6,4},{5,7},{7,5},{8,10},{10,8},{9,1... | collective-permute-start | bytes 786440 | tf_op jit(solution)/shard_map/ppermute | solution.py:405
  114.5 36.8 %collective-permute-start.31 = (bf16[1,256,1024]{2,1,0:T(8,128)(2,1)S(1)}, bf16[1,256,1024]{2,1,0:T(8,128)(2,1)S(1)}, u32[]{:S(2)}, u32[]{:S(2)}) collective-permute-start(bf16[1,256,1024]{2,1,0:T(8,128)(2,1)S(1)} %get-tuple-element.68), channel_id=1, source_target_pairs={{0,1},{1,0},{2,3},{3,2},{4,5},{5,4},{6,7},{7,6},{8,9},{9,8},{10,11... | collective-permute-start | bytes 1572872 | tf_op jit(solution)/shard_map/ppermute | solution.py:452
  123.9 28.3 %collective-permute-start.18 = (bf16[1,256,1024]{2,1,0:T(8,128)(2,1)S(1)}, bf16[1,256,1024]{2,1,0:T(8,128)(2,1)S(1)}, u32[]{:S(2)}, u32[]{:S(2)}) collective-permute-start(bf16[1,256,1024]{2,1,0:T(8,128)(2,1)S(1)} %get-tuple-element.53), channel_id=1, source_target_pairs={{0,1},{1,0},{2,3},{3,2},{4,5},{5,4},{6,7},{7,6},{8,9},{9,8},{10,11... | collective-permute-start | bytes 1572872 | tf_op jit(solution)/shard_map/ppermute | solution.py:452
  125.8 13.1 %collective-permute-start.33 = (bf16[2,4,128,128]{3,2,1,0:T(8,128)(2,1)S(1)}, bf16[2,4,128,128]{3,2,1,0:T(8,128)(2,1)S(1)}, u32[]{:S(2)}, u32[]{:S(2)}) collective-permute-start(bf16[2,4,128,128]{3,2,1,0:T(8,128)(2,1)S(1)} %shard_map.137), channel_id=1, source_target_pairs={{0,0},{1,8},{2,4},{3,12},{4,5},{5,13},{6,1},{7,9},{8,2},{9,10},{10... | collective-permute-start | bytes 786440 | tf_op jit(solution)/shard_map/ppermute | solution.py:460
  132.1 15.7 %collective-permute-start.32 = (bf16[2,4,128,128]{3,2,1,0:T(8,128)(2,1)S(1)}, bf16[2,4,128,128]{3,2,1,0:T(8,128)(2,1)S(1)}, u32[]{:S(2)}, u32[]{:S(2)}) collective-permute-start(bf16[2,4,128,128]{3,2,1,0:T(8,128)(2,1)S(1)} %shard_map.135), channel_id=1, source_target_pairs={{0,0},{1,8},{2,4},{3,12},{4,5},{5,13},{6,1},{7,9},{8,2},{9,10},{10... | collective-permute-start | bytes 786440 | tf_op jit(solution)/shard_map/ppermute | solution.py:460
  136.3 14.3 %collective-permute-start.34 = (bf16[2,4,128,128]{3,2,1,0:T(8,128)(2,1)S(1)}, bf16[2,4,128,128]{3,2,1,0:T(8,128)(2,1)S(1)}, u32[]{:S(2)}, u32[]{:S(2)}) collective-permute-start(bf16[2,4,128,128]{3,2,1,0:T(8,128)(2,1)S(1)} %shard_map.139), channel_id=1, source_target_pairs={{0,0},{1,8},{2,4},{3,12},{4,5},{5,13},{6,1},{7,9},{8,2},{9,10},{10... | collective-permute-start | bytes 786440 | tf_op jit(solution)/shard_map/ppermute | solution.py:460
  (16 other events, 164.4 us)

commit v4 on v3

--- a/solution.py
+++ b/solution.py
@@ -10,7 +10,7 @@
 BF = jnp.bfloat16
 F32 = jnp.float32
 LIMIT = 16 << 20
-Z, Q, OWNER, OWNED = range(4)
+Z, Q, OWNER, OWNED, GROUP = range(5)
 PLANE = ("shard", "dp", "tok")
 
 
@@ -75,7 +75,7 @@
 
 
 def aligned(value, size):
-    return pl.multiple_of(value * size, size)
+    return value * size if isinstance(value, int) else pl.multiple_of(value * size, size)
 
 
 def down_places(info, down_rows, columns, per_owner, dx=0):
@@ -83,14 +83,13 @@
     return lambda c, k: down_rows[first_row + c, first + k] - info[Z] * info[OWNED]
 
 
-def scatter_cols(dense, packed, place, columns):
-    count, size, _ = packed.shape
-    per_owner = count // columns
+def scatter_cols(dense, pieces, place):
     dense[...] = jnp.zeros_like(dense)
-    for c in range(columns):
+    for blocks, c in pieces:
+        per_owner, size, _ = blocks.shape
         for k in range(per_owner):
             here = pl.ds(aligned(place(c, k), size), size)
-            dense[c * size : (c + 1) * size, here] = packed[c * per_owner + k]
+            dense[pl.ds(aligned(c, size), size), here] = blocks[k]
 
 
 def split_rows(total, r, near, far, z):
@@ -100,57 +99,69 @@
         out[d // 2, r] = total[r, pl.ds(aligned(z ^ d, rows), rows), :].astype(out.dtype)
 
 
-def copy_owner(pairs, owner, sems):
-    copies = []
-    for i, (source, target) in enumerate(pairs):
-        columns = source.shape[0]
-        per_owner = target.shape[0] // columns
-        for c in range(columns):
-            part = source.at[c, pl.ds(owner * per_owner, per_owner)]
-            place = target.at[pl.ds(c * per_owner, per_owner)]
-            copies.append(pltpu.make_async_copy(part, place, sems.at[i * columns + c]))
+def pack_kernel(info, gate_rows, up_rows, gate, up, down, rows_out, gate_out, half_out, sems):
+    columns, per_owner = rows_out.shape[1:]
+    owner, group = info[OWNER], info[GROUP]
+    here = pl.ds(owner * per_owner, per_owner)
+    pairs = [(gate.at[c, here], gate_out.at[pl.ds(c * per_owner, per_owner)]) for c in range(columns)]
+    pairs.append((up.at[group, here], half_out.at[pl.ds(0, per_owner)]))
+    pairs.append((down.at[group, here], half_out.at[pl.ds(per_owner, per_owner)]))
+    copies = [pltpu.make_async_copy(source, target, sems.at[n]) for n, (source, target) in enumerate(pairs)]
     for copy in copies:
         copy.start()
-    return copies
-
-
-def pack_kernel(info, gate_rows, up_rows, gate, up, down, rows_out, both_out, down_out, sems):
-    count = down_out.shape[0]
-    targets = both_out.at[pl.ds(0, count)], both_out.at[pl.ds(count, count)], down_out
-    copies = copy_owner(zip((gate, up, down), targets), info[OWNER], sems)
-    columns, per_owner = rows_out.shape[1:]
     for i, rows in enumerate((gate_rows, up_rows)):
         for c in range(columns):
             for k in range(per_owner):
-                rows_out[i, c, k] = rows[c, info[OWNER] * per_owner + k] - info[OWNER] * info[OWNED]
+                rows_out[i, c, k] = rows[c, owner * per_owner + k] - owner * info[OWNED]
     for copy in copies:
         copy.wait()
 
 
-def scatter_rows(dense, packed, rows, i):
-    columns, per_owner = rows.shape[1:]
-    size = packed.shape[1]
+def gate_pieces(packed):
+    per_owner = packed.shape[0] // 2
+    return [(packed.at[pl.ds(c * per_owner, per_owner)], c) for c in range(2)]
+
+
+def half_pieces(mine, other, group, i):
+    per_owner = mine.shape[0] // 2
+    here = pl.ds(i * per_owner, per_owner)
+    return [(mine.at[here], group), (other.at[here], 1 - group)]
+
+
+def scatter_rows(dense, pieces, rows, i):
     dense[...] = jnp.zeros_like(dense)
-    for c in range(columns):
+    for blocks, c in pieces:
+        per_owner, size, _ = blocks.shape
         for k in range(per_owner):
             place = pl.ds(aligned(rows[i, c, k], size), size)
-            dense[place, c * size : (c + 1) * size] = packed[(i * columns + c) * per_owner + k]
-
-
-def project_kernel(n, i, info, rows, *refs):
+            dense[place, pl.ds(aligned(c, size), size)] = blocks[k]
+
+
+def gate_kernel(n, info, rows, *refs):
     xs, packed = refs[:n], refs[n]
     near, far, dense, total = refs[n + 1 :]
-    scatter_rows(dense, packed, rows, i)
+    scatter_rows(dense, gate_pieces(packed), rows, 0)
+    project(xs, near, far, dense, total, info[Z])
+
+
+def up_kernel(n, info, rows, *refs):
+    xs, (mine, other) = refs[:n], refs[n : n + 2]
+    near, far, dense, total = refs[n + 2 :]
+    scatter_rows(dense, half_pieces(mine, other, info[GROUP], 0), rows, 1)
+    project(xs, near, far, dense, total, info[Z])
+
+
+def project(xs, near, far, dense, total, z):
     for r, x in enumerate(xs):
         total[r] = jnp.dot(x[...], dense[...], preferred_element_type=F32)
-        split_rows(total, r, near, far, info[Z])
+        split_rows(total, r, near, far, z)
 
 
 def hidden_grad_kernel(nj, columns, info, down_rows, *refs):
-    cots, down_blocks = refs[:nj], refs[nj]
-    near, far, down_dense, total = refs[nj + 1 :]
-    place = down_places(info, down_rows, columns, down_blocks.shape[0] // columns)
-    scatter_cols(down_dense, down_blocks, place, columns)
+    cots, (mine, other) = refs[:nj], refs[nj : nj + 2]
+    near, far, down_dense, total = refs[nj + 2 :]
+    place = down_places(info, down_rows, columns, mine.shape[0] // 2)
+    scatter_cols(down_dense, half_pieces(mine, other, info[GROUP], 1), place)
     for r in range(nj):
         total[r] = lax.dot_general(
             cots[r][...], down_dense[...], (((1,), (1,)), ((), ())), preferred_element_type=F32
@@ -244,13 +255,13 @@
 
 def mixed_kernel(n_dp, columns, info, down_rows, *refs):
     hiddens, dense = refs[:n_dp], refs[n_dp]
-    others = refs[n_dp + 1 : 2 * n_dp]
-    keep, send = refs[2 * n_dp : 2 * n_dp + 2]
-    denses = [dense, *refs[2 * n_dp + 2 :]]
+    halves = refs[n_dp + 1 : 3 * n_dp - 1]
+    keep, send = refs[3 * n_dp - 1 : 3 * n_dp + 1]
+    denses = [dense, *refs[3 * n_dp + 1 :]]
     for dx in range(1, n_dp):
-        packed = others[dx - 1]
-        place = down_places(info, down_rows, columns, packed.shape[0] // columns, dx)
-        scatter_cols(denses[dx], packed, place, columns)
+        mine, other = halves[dx - 1], halves[n_dp + dx - 2]
+        place = down_places(info, down_rows, columns, mine.shape[0] // 2, dx)
+        scatter_cols(denses[dx], half_pieces(mine, other, info[GROUP], 1), place)
     for dc in reversed(range(hiddens[0].shape[0])):
         value = 0.0
         for hidden, weights in zip(hiddens, denses):
@@ -272,18 +283,19 @@
     pick_blocks(grad, acc, lambda c, k: rows[i, c, k], True)
 
 
-def tokens_grad_kernel(n_dp, *refs):
+def tokens_grad_kernel(n_dp, info, *refs):
     other_rows = refs[: n_dp - 1]
     refs = refs[n_dp - 1 :]
     sides = refs[:n_dp], refs[n_dp : 2 * n_dp]
     gate_dense, up_dense = refs[2 * n_dp : 2 * n_dp + 2]
-    others = refs[2 * n_dp + 2 : 3 * n_dp + 1]
-    keep, send = refs[3 * n_dp + 1 : 3 * n_dp + 3]
-    scratch = refs[3 * n_dp + 3 :]
+    others = refs[2 * n_dp + 2 : 5 * n_dp - 1]
+    keep, send = refs[5 * n_dp - 1 : 5 * n_dp + 1]
+    scratch = refs[5 * n_dp + 1 :]
     denses = [gate_dense, *scratch[: n_dp - 1]], [up_dense, *scratch[n_dp - 1 :]]
-    for i, side in enumerate(denses):
-        for packed, rows, dense in zip(others, other_rows, side[1:]):
-            scatter_rows(dense, packed, rows, i)
+    for n, rows in enumerate(other_rows):
+        packed, mine, other = others[n :: n_dp - 1]
+        scatter_rows(denses[0][n + 1], gate_pieces(packed), rows, 0)
+        scatter_rows(denses[1][n + 1], half_pieces(mine, other, info[GROUP], 0), rows, 1)
     for dc in reversed(range(sides[0][0].shape[0])):
         value = 0.0
         for acts, side in zip(sides, denses):
@@ -300,6 +312,8 @@
     nj = n_dp * n_tok
     z = lax.axis_index("shard")
     x_index, c_index = lax.axis_index("dp"), lax.axis_index("tok")
+    group = lax.axis_index("groups")
+    assert gate_blocks.shape[0] == lax.axis_size("groups") == 2
     q = column_shard(n_dp, z, x_index, c_index)
     count, width = tokens.shape
     columns, nonzero, size, _ = gate_blocks.shape
@@ -344,21 +358,22 @@
 
     w_perm = weight_perm(shards, n_dp, n_tok)
     owner = weight_owner(shards, n_dp, n_tok, z, x_index, c_index)
-    info = jnp.stack([v.astype(jnp.int32) for v in (z, q, owner, jnp.int32(owned))])
-    rows, both_parts, down_part = run(
+    info = jnp.stack([v.astype(jnp.int32) for v in (z, q, owner, jnp.int32(owned), group)])
+    rows, gate_part, half_mine = run(
         pack_kernel,
         [info, gate_rows, up_rows],
         [],
-        [shape((2, columns, per_owner), jnp.int32)] + [shape((n * blocks, size, size), BF) for n in (2, 1)],
-        [pltpu.SemaphoreType.DMA((3 * columns,))],
+        [shape((2, columns, per_owner), jnp.int32)] + [shape((n * blocks, size, size), BF) for n in (1, 1)],
+        [pltpu.SemaphoreType.DMA((columns + 2,))],
         0,
         [gate_blocks, up_blocks, down_blocks],
         60 << 20,
         [pltpu.SMEM] + [pltpu.VMEM] * 2,
     )
-    both_parts = lax.ppermute(both_parts, PLANE, w_perm)
+    gate_part = lax.ppermute(gate_part, PLANE, w_perm)
     rows = lax.ppermute(rows, PLANE, w_perm)
-    down_part = lax.ppermute(down_part, PLANE, w_perm)
+    half_mine = lax.ppermute(half_mine, PLANE, w_perm)
+    half_other = lax.ppermute(half_mine, "groups", [(0, 1), (1, 0)])
 
     xs = gather_plane(tokens)
     cots = gather_plane(cotangent)
@@ -371,24 +386,19 @@
 
     sums_scratch = [pltpu.VMEM((nj, count, hidden_width), F32)]
 
-    def project(i):
+    def project(kernel, weights):
         return run(
-            functools.partial(project_kernel, nj, i),
-            [info, rows],
-            [*xs, both_parts],
-            part_shapes + [dense],
-            sums_scratch,
-            macs,
+            functools.partial(kernel, nj), [info, rows], [*xs, *weights], part_shapes + [dense], sums_scratch, macs
         )
 
-    near_gate, far_gate, gate_dense = project(0)
+    near_gate, far_gate, gate_dense = project(gate_kernel, [gate_part])
     gates = reduce(near_gate, far_gate)
-    near_up, far_up, up_dense = project(1)
+    near_up, far_up, up_dense = project(up_kernel, [half_mine, half_other])
     ups = reduce(near_up, far_up)
     near_hg, far_hg, down_dense = run(
         functools.partial(hidden_grad_kernel, nj, columns),
         [info, down_rows],
-        [*cots, down_part],
+        [*cots, half_mine, half_other],
         part_shapes + [shape((hidden_width, width), BF)],
         sums_scratch,
         macs,
@@ -403,9 +413,9 @@
     chip = shape((n_tok, count, hidden_width), BF)
     others = range(1, n_dp)
     to_dp = lambda a, dx: lax.ppermute(a, "dp", xor_perm(n_dp, dx))
-    other_both = [to_dp(both_parts, dx) for dx in others]
+    other_gate = [to_dp(gate_part, dx) for dx in others]
     other_rows = [to_dp(rows, dx) for dx in others]
-    other_down = [to_dp(down_part, dx) for dx in others]
+    other_halves = [to_dp(half, dx) for half in (half_mine, half_other) for dx in others]
 
     def join(own):
         parts = gather(own)
@@ -422,7 +432,7 @@
     mixed = run(
         functools.partial(mixed_kernel, n_dp, columns),
         [info, down_rows],
-        [*chip_hidden, down_dense, *other_down],
+        [*chip_hidden, down_dense, *other_halves],
         plane_shapes,
         [pltpu.VMEM((hidden_width, width), BF)] * (n_dp - 1),
         macs,
@@ -439,8 +449,8 @@
     up_grad = row_grad(1, all_up)
     tokens_terms = run(
         functools.partial(tokens_grad_kernel, n_dp),
-        other_rows,
-        [*chip_gate, *chip_up, gate_dense, up_dense, *other_both],
+        [info, *other_rows],
+        [*chip_gate, *chip_up, gate_dense, up_dense, *other_gate, *other_halves],
         plane_shapes,
         [pltpu.VMEM((width, hidden_width), BF)] * (2 * n_dp - 2),
         2 * macs,

time: 153 us -> 158 us (1.033)
  the two profiles are of different devices: /device:TPU:2 before, /device:TPU:3 now
where the time goes in v4:
time: 158 us
  waiting for transfers between devices  71.5 us (45%)
  starting transfers between devices  62.4 us (39%)
  Pallas kernels  22.2 us (14%)
    ppermute x7, waiting for transfers between devices, body(): to_dp = lambda a, dx: lax.ppermute(a, 'dp', xor_perm(n_dp, dx))  22.7 us
    pallas_call x22, Pallas kernels, call(): pl.pallas_call(kernel, out_shape=outs, in_specs=smem(len(scalars)) + vmem...  22.2 us
    ppermute x6, waiting for transfers between devices, reduce(): arrived = lax.ppermute(far, ('shard', 'dp'), shard_perm(shards, n_dp, bit))  20.3 us
    ppermute x3, starting transfers between devices, home(): grad = lax.ppermute(grad, PLANE, g_perm)  11.7 us
    ppermute x9, waiting for transfers between devices, gather(): lax.ppermute(have[d], ('shard', 'dp'), shard_perm(shards, n_dp, bit))  11.7 us
    ppermute x7, starting transfers between devices, body(): to_dp = lambda a, dx: lax.ppermute(a, 'dp', xor_perm(n_dp, dx))  10.8 us
    ppermute x9, starting transfers between devices, gather(): lax.ppermute(have[d], ('shard', 'dp'), shard_perm(shards, n_dp, bit))  10.1 us
    ppermute x3, waiting for transfers between devices, home(): grad = lax.ppermute(grad, PLANE, g_perm)  6.9 us
  transfers between devices with their start and end apart: 37, of which 19 were waited for; matrix products, arithmetic and copies ran while one was open for 0% of the time, Pallas kernels for 13%

profile of v4, /device:TPU:3, one launch (start us, length us, event | category | flops | bytes accessed | tf_op | source)
XLA Modules:
  0.0 157.7 jit_solution(468550822599614446)
XLA Ops:
  2.8 2.8 %shard_map.119 = (s32[2,2,4]{2,1,0:T(2,128)}, bf16[8,128,128]{2,1,0:T(8,128)(2,1)}, bf16[8,128,128]{2,1,0:T(8,128)(2,1)}) custom-call(s32[5]{0:T(128)} %stack.16.info, s32[2,16]{1,0:T(2,128)} %gate_rows.1, s32[2,16]{1,0:T(2,128)} %up_rows.1, bf16[2,16,128,128]{3,2,1,0:T(8,128)(2,1)} %gate.1, bf16[2,16,128,128]{3,2,1,0:T(8,128)(2,1)} %up.1, ...), custom_call_target="tpu_custom_call" | custom-call | bytes 3670080 | tf_op jit(solution)/shard_map/pallas_call | solution.py:66
  5.6 6.3 %collective-permute-start.7 = (bf16[8,128,128]{2,1,0:T(8,128)(2,1)}, bf16[8,128,128]{2,1,0:T(8,128)(2,1)S(1)}, u32[]{:S(2)}, u32[]{:S(2)}) collective-permute-start(bf16[8,128,128]{2,1,0:T(8,128)(2,1)} %get-tuple-element.43), channel_id=1, source_target_pairs={{0,0},{8,1},{6,2},{14,3},{4,4},{12,5},{2,6},{10,7},{1,8},{9,9},{7,... | collective-permute-start | bytes 786440 | tf_op jit(solution)/shard_map/ppermute | solution.py:375
  13.7 2.7 %collective-permute-start.3 = (bf16[256,1024]{1,0:T(8,128)(2,1)S(1)}, bf16[256,1024]{1,0:T(8,128)(2,1)S(1)}, u32[]{:S(2)}, u32[]{:S(2)}) collective-permute-start(bf16[256,1024]{1,0:T(8,128)(2,1)S(1)} %collective-permute-done.2.refs_2_.refs_4_), channel_id=1, source_target_pairs={{0,1},{1,0},{2,3},{3,2},{4,5},{5,4},{6,7},{7,6},{8,9},{9,8},{10,11... | collective-permute-start | bytes 1572872 | tf_op jit(solution)/shard_map/ppermute | solution.py:356
  19.1 5.5 %collective-permute-start = (s32[2,2,4]{2,1,0:T(2,128)S(1)}, s32[2,2,4]{2,1,0:T(2,128)S(1)}, u32[]{:S(2)}, u32[]{:S(2)}) collective-permute-start(s32[2,2,4]{2,1,0:T(2,128)S(1)} %copy-done.4), channel_id=1, source_target_pairs={{0,0},{8,1},{6,2},{14,3},{4,4},{12,5},{2,6},{10,7},{1,8},{9,9},{7,... | collective-permute-start | bytes 200 | tf_op jit(solution)/shard_map/ppermute | solution.py:374
  26.5 5.3 %collective-permute-start.4 = (bf16[8,128,128]{2,1,0:T(8,128)(2,1)}, bf16[8,128,128]{2,1,0:T(8,128)(2,1)S(1)}, u32[]{:S(2)}, u32[]{:S(2)}) collective-permute-start(bf16[8,128,128]{2,1,0:T(8,128)(2,1)} %get-tuple-element.38), channel_id=1, source_target_pairs={{0,0},{8,1},{6,2},{14,3},{4,4},{12,5},{2,6},{10,7},{1,8},{9,9},{7,... | collective-permute-start | bytes 786440 | tf_op jit(solution)/shard_map/ppermute | solution.py:373
  33.4 5.6 %collective-permute-done.4.refs_4_ = bf16[8,128,128]{2,1,0:T(8,128)(2,1)S(1)} collective-permute-done((bf16[8,128,128]{2,1,0:T(8,128)(2,1)}, bf16[8,128,128]{2,1,0:T(8,128)(2,1)S(1)}, u32[]{:S(2)}, u32[]{:S(2)}) %collective-permute-start.4) | collective-permute-done | bytes 262176 | tf_op jit(solution)/shard_map/ppermute | solution.py:373
  42.1 2.4 %collective-permute-start.22 = (bf16[2,4,64,256]{3,2,1,0:T(8,128)(2,1)S(1)}, bf16[2,4,64,256]{3,2,1,0:T(8,128)(2,1)S(1)}, u32[]{:S(2)}, u32[]{:S(2)}) collective-permute-start(bf16[2,4,64,256]{3,2,1,0:T(8,128)(2,1)S(1)} %get-tuple-element.56), channel_id=1, source_target_pairs={{0,6},{2,4},{4,2},{6,0},{8,14},{10,12},{12,10},{14,8},{1,7},{3,5},... | collective-permute-start | bytes 786440 | tf_op jit(solution)/shard_map/ppermute | solution.py:329
  44.7 7.9 %collective-permute-done.5.arrived = bf16[2,4,64,256]{3,2,1,0:T(8,128)(2,1)S(1)} collective-permute-done((bf16[2,4,64,256]{3,2,1,0:T(8,128)(2,1)S(1)}, bf16[2,4,64,256]{3,2,1,0:T(8,128)(2,1)S(1)}, u32[]{:S(2)}, u32[]{:S(2)}) %collective-permute-start.5) | collective-permute-done | bytes 262176 | tf_op jit(solution)/shard_map/ppermute | solution.py:329
  52.7 3.8 %collective-permute-done.22.arrived = bf16[2,4,64,256]{3,2,1,0:T(8,128)(2,1)S(1)} collective-permute-done((bf16[2,4,64,256]{3,2,1,0:T(8,128)(2,1)S(1)}, bf16[2,4,64,256]{3,2,1,0:T(8,128)(2,1)S(1)}, u32[]{:S(2)}, u32[]{:S(2)}) %collective-permute-start.22) | collective-permute-done | bytes 262176 | tf_op jit(solution)/shard_map/ppermute | solution.py:329
  56.6 2.7 %collective-permute-start.23 = (bf16[1,4,64,256]{3,2,1,0:T(8,128)(2,1)S(1)}, bf16[1,4,64,256]{3,2,1,0:T(8,128)(2,1)S(1)}, u32[]{:S(2)}, u32[]{:S(2)}) collective-permute-start(bf16[1,4,64,256]{3,2,1,0:T(8,128)(2,1)S(1)} %get-tuple-element.58), channel_id=1, source_target_pairs={{0,8},{2,10},{4,12},{6,14},{8,0},{10,2},{12,4},{14,6},{1,9},{3,11}... | collective-permute-start | bytes 393224 | tf_op jit(solution)/shard_map/ppermute | solution.py:329
  59.3 7.2 %collective-permute-done.6.gate_last = bf16[1,4,64,256]{3,2,1,0:T(8,128)(2,1)S(1)} collective-permute-done((bf16[1,4,64,256]{3,2,1,0:T(8,128)(2,1)S(1)}, bf16[1,4,64,256]{3,2,1,0:T(8,128)(2,1)S(1)}, u32[]{:S(2)}, u32[]{:S(2)}) %collective-permute-start.6) | collective-permute-done | bytes 131104 | tf_op jit(solution)/shard_map/ppermute | solution.py:329
  72.8 3.5 %collective-permute-done.29.refs_2_ = bf16[4,64,256]{2,1,0:T(8,128)(2,1)S(1)} collective-permute-done((bf16[4,64,256]{2,1,0:T(8,128)(2,1)S(1)}, bf16[4,64,256]{2,1,0:T(8,128)(2,1)S(1)}, u32[]{:S(2)}, u32[]{:S(2)}) %collective-permute-start.29) | collective-permute-done | bytes 131104 | tf_op jit(solution)/shard_map/ppermute | solution.py:343
  80.0 4.4 %collective-permute-done.25.refs_2_ = bf16[4,64,256]{2,1,0:T(8,128)(2,1)S(1)} collective-permute-done((bf16[4,64,256]{2,1,0:T(8,128)(2,1)S(1)}, bf16[4,64,256]{2,1,0:T(8,128)(2,1)S(1)}, u32[]{:S(2)}, u32[]{:S(2)}) %collective-permute-start.25) | collective-permute-done | bytes 131104 | tf_op jit(solution)/shard_map/ppermute | solution.py:343
  93.6 6.7 %collective-permute-start.19 = (bf16[8,128,128]{2,1,0:T(8,128)(2,1)S(1)}, bf16[8,128,128]{2,1,0:T(8,128)(2,1)S(1)}, u32[]{:S(2)}, u32[]{:S(2)}) collective-permute-start(bf16[8,128,128]{2,1,0:T(8,128)(2,1)S(1)} %collective-permute-done.8.refs_5_), channel_id=1, source_target_pairs={{0,2},{2,0},{1,3},{3,1},{4,6},{6,4},{5,7},{7,5},{8,10},{10,8},{9,1... | collective-permute-start | bytes 786440 | tf_op jit(solution)/shard_map/ppermute | solution.py:415
  102.4 2.8 %collective-permute-done.32.refs_7_ = bf16[8,128,128]{2,1,0:T(8,128)(2,1)S(1)} collective-permute-done((bf16[8,128,128]{2,1,0:T(8,128)(2,1)S(1)}, bf16[8,128,128]{2,1,0:T(8,128)(2,1)S(1)}, u32[]{:S(2)}, u32[]{:S(2)}) %collective-permute-start.32) | collective-permute-done | bytes 262176 | tf_op jit(solution)/shard_map/ppermute | solution.py:415
  105.2 5.6 %collective-permute-done.19.refs_4_.refs_9_ = bf16[8,128,128]{2,1,0:T(8,128)(2,1)S(1)} collective-permute-done((bf16[8,128,128]{2,1,0:T(8,128)(2,1)S(1)}, bf16[8,128,128]{2,1,0:T(8,128)(2,1)S(1)}, u32[]{:S(2)}, u32[]{:S(2)}) %collective-permute-start.19) | collective-permute-done | bytes 262176 | tf_op jit(solution)/shard_map/ppermute | solution.py:415
  110.8 5.6 %collective-permute-done.31.refs_4_ = bf16[2,256,256]{2,1,0:T(8,128)(2,1)S(1)} collective-permute-done((bf16[2,256,256]{2,1,0:T(8,128)(2,1)S(1)}, bf16[2,256,256]{2,1,0:T(8,128)(2,1)S(1)}, u32[]{:S(2)}, u32[]{:S(2)}) %collective-permute-start.31) | collective-permute-done | bytes 262176 | tf_op jit(solution)/shard_map/ppermute | solution.py:415
  116.5 5.6 %collective-permute-done.27.refs_2_ = bf16[2,256,256]{2,1,0:T(8,128)(2,1)S(1)} collective-permute-done((bf16[2,256,256]{2,1,0:T(8,128)(2,1)S(1)}, bf16[2,256,256]{2,1,0:T(8,128)(2,1)S(1)}, u32[]{:S(2)}, u32[]{:S(2)}) %collective-permute-start.27) | collective-permute-done | bytes 262176 | tf_op jit(solution)/shard_map/ppermute | solution.py:415
  124.6 3.1 %collective-permute-done.14.refs_1_ = bf16[2,256,256]{2,1,0:T(8,128)(2,1)S(1)} collective-permute-done((bf16[2,256,256]{2,1,0:T(8,128)(2,1)S(1)}, bf16[2,256,256]{2,1,0:T(8,128)(2,1)S(1)}, u32[]{:S(2)}, u32[]{:S(2)}) %collective-permute-start.14) | collective-permute-done | bytes 262176 | tf_op jit(solution)/shard_map/ppermute | solution.py:415
  131.5 5.1 %collective-permute-start.35 = (bf16[2,4,128,128]{3,2,1,0:T(8,128)(2,1)S(1)}, bf16[2,4,128,128]{3,2,1,0:T(8,128)(2,1)S(1)}, u32[]{:S(2)}, u32[]{:S(2)}) collective-permute-start(bf16[2,4,128,128]{3,2,1,0:T(8,128)(2,1)S(1)} %shard_map.137), channel_id=1, source_target_pairs={{0,0},{1,8},{2,4},{3,12},{4,5},{5,13},{6,1},{7,9},{8,2},{9,10},{10... | collective-permute-start | bytes 786440 | tf_op jit(solution)/shard_map/ppermute | solution.py:470
  138.5 3.5 %collective-permute-start.34 = (bf16[2,4,128,128]{3,2,1,0:T(8,128)(2,1)S(1)}, bf16[2,4,128,128]{3,2,1,0:T(8,128)(2,1)S(1)}, u32[]{:S(2)}, u32[]{:S(2)}) collective-permute-start(bf16[2,4,128,128]{3,2,1,0:T(8,128)(2,1)S(1)} %shard_map.135), channel_id=1, source_target_pairs={{0,0},{1,8},{2,4},{3,12},{4,5},{5,13},{6,1},{7,9},{8,2},{9,10},{10... | collective-permute-start | bytes 786440 | tf_op jit(solution)/shard_map/ppermute | solution.py:470
  143.8 3.1 %collective-permute-start.36 = (bf16[2,4,128,128]{3,2,1,0:T(8,128)(2,1)S(1)}, bf16[2,4,128,128]{3,2,1,0:T(8,128)(2,1)S(1)}, u32[]{:S(2)}, u32[]{:S(2)}) collective-permute-start(bf16[2,4,128,128]{3,2,1,0:T(8,128)(2,1)S(1)} %shard_map.139), channel_id=1, source_target_pairs={{0,0},{1,8},{2,4},{3,12},{4,5},{5,13},{6,1},{7,9},{8,2},{9,10},{10... | collective-permute-start | bytes 786440 | tf_op jit(solution)/shard_map/ppermute | solution.py:470
  147.6 3.4 %collective-permute-done.34.refs_0_ = bf16[2,4,128,128]{3,2,1,0:T(8,128)(2,1)S(1)} collective-permute-done((bf16[2,4,128,128]{3,2,1,0:T(8,128)(2,1)S(1)}, bf16[2,4,128,128]{3,2,1,0:T(8,128)(2,1)S(1)}, u32[]{:S(2)}, u32[]{:S(2)}) %collective-permute-start.34) | collective-permute-done | bytes 262176 | tf_op jit(solution)/shard_map/ppermute | solution.py:470
  151.8 3.5 %collective-permute-done.36.refs_0_ = bf16[2,4,128,128]{3,2,1,0:T(8,128)(2,1)S(1)} collective-permute-done((bf16[2,4,128,128]{3,2,1,0:T(8,128)(2,1)S(1)}, bf16[2,4,128,128]{3,2,1,0:T(8,128)(2,1)S(1)}, u32[]{:S(2)}, u32[]{:S(2)}) %collective-permute-start.36) | collective-permute-done | bytes 262176 | tf_op jit(solution)/shard_map/ppermute | solution.py:470
  (83 shorter events, 48.6 us)
Async XLA Ops:
  0.6 13.1 %collective-permute-start.2 = (bf16[256,1024]{1,0:T(8,128)(2,1)}, bf16[256,1024]{1,0:T(8,128)(2,1)S(1)}, u32[]{:S(2)}, u32[]{:S(2)}) collective-permute-start(bf16[256,1024]{1,0:T(8,128)(2,1)} %refs_2_.4), channel_id=1, source_target_pairs={{0,2},{2,0},{1,3},{3,1},{4,6},{6,4},{5,7},{7,5},{8,10},{10,8},{9,1... | collective-permute-start | bytes 1572872 | tf_op jit(solution)/shard_map/ppermute | solution.py:353
  0.7 25.2 %collective-permute-start.16 = (bf16[256,1024]{1,0:T(8,128)(2,1)}, bf16[256,1024]{1,0:T(8,128)(2,1)S(1)}, u32[]{:S(2)}, u32[]{:S(2)}) collective-permute-start(bf16[256,1024]{1,0:T(8,128)(2,1)} %refs_2_.5), channel_id=1, source_target_pairs={{0,2},{2,0},{1,3},{3,1},{4,6},{6,4},{5,7},{7,5},{8,10},{10,8},{9,1... | collective-permute-start | bytes 1572872 | tf_op jit(solution)/shard_map/ppermute | solution.py:353
  11.9 19.9 %collective-permute-start.1 = (bf16[256,1024]{1,0:T(8,128)(2,1)S(1)}, bf16[256,1024]{1,0:T(8,128)(2,1)S(1)}, u32[]{:S(2)}, u32[]{:S(2)}) collective-permute-start(bf16[256,1024]{1,0:T(8,128)(2,1)S(1)} %copy-done), channel_id=1, source_target_pairs={{0,1},{1,0},{2,3},{3,2},{4,5},{5,4},{6,7},{7,6},{8,9},{9,8},{10,11... | collective-permute-start | bytes 1572872 | tf_op jit(solution)/shard_map/ppermute | solution.py:356
  13.7 18.1 %collective-permute-start.3 = (bf16[256,1024]{1,0:T(8,128)(2,1)S(1)}, bf16[256,1024]{1,0:T(8,128)(2,1)S(1)}, u32[]{:S(2)}, u32[]{:S(2)}) collective-permute-start(bf16[256,1024]{1,0:T(8,128)(2,1)S(1)} %collective-permute-done.2.refs_2_.refs_4_), channel_id=1, source_target_pairs={{0,1},{1,0},{2,3},{3,2},{4,5},{5,4},{6,7},{7,6},{8,9},{9,8},{10,11... | collective-permute-start | bytes 1572872 | tf_op jit(solution)/shard_map/ppermute | solution.py:356
  25.9 14.6 %collective-permute-start.15 = (bf16[256,1024]{1,0:T(8,128)(2,1)S(1)}, bf16[256,1024]{1,0:T(8,128)(2,1)S(1)}, u32[]{:S(2)}, u32[]{:S(2)}) collective-permute-start(bf16[256,1024]{1,0:T(8,128)(2,1)S(1)} %copy-done.1), channel_id=1, source_target_pairs={{0,1},{1,0},{2,3},{3,2},{4,5},{5,4},{6,7},{7,6},{8,9},{9,8},{10,11... | collective-permute-start | bytes 1572872 | tf_op jit(solution)/shard_map/ppermute | solution.py:356
  25.9 14.6 %collective-permute-start.17 = (bf16[256,1024]{1,0:T(8,128)(2,1)S(1)}, bf16[256,1024]{1,0:T(8,128)(2,1)S(1)}, u32[]{:S(2)}, u32[]{:S(2)}) collective-permute-start(bf16[256,1024]{1,0:T(8,128)(2,1)S(1)} %collective-permute-done.16.refs_2_.refs_4_), channel_id=1, source_target_pairs={{0,1},{1,0},{2,3},{3,2},{4,5},{5,4},{6,7},{7,6},{8,9},{9,8},{10,11... | collective-permute-start | bytes 1572872 | tf_op jit(solution)/shard_map/ppermute | solution.py:356
  26.5 12.5 %collective-permute-start.4 = (bf16[8,128,128]{2,1,0:T(8,128)(2,1)}, bf16[8,128,128]{2,1,0:T(8,128)(2,1)S(1)}, u32[]{:S(2)}, u32[]{:S(2)}) collective-permute-start(bf16[8,128,128]{2,1,0:T(8,128)(2,1)} %get-tuple-element.38), channel_id=1, source_target_pairs={{0,0},{8,1},{6,2},{14,3},{4,4},{12,5},{2,6},{10,7},{1,8},{9,9},{7,... | collective-permute-start | bytes 786440 | tf_op jit(solution)/shard_map/ppermute | solution.py:373
  42.1 14.4 %collective-permute-start.22 = (bf16[2,4,64,256]{3,2,1,0:T(8,128)(2,1)S(1)}, bf16[2,4,64,256]{3,2,1,0:T(8,128)(2,1)S(1)}, u32[]{:S(2)}, u32[]{:S(2)}) collective-permute-start(bf16[2,4,64,256]{3,2,1,0:T(8,128)(2,1)S(1)} %get-tuple-element.56), channel_id=1, source_target_pairs={{0,6},{2,4},{4,2},{6,0},{8,14},{10,12},{12,10},{14,8},{1,7},{3,5},... | collective-permute-start | bytes 786440 | tf_op jit(solution)/shard_map/ppermute | solution.py:329
  44.6 14.7 %collective-permute-start.10 = (bf16[1,4,64,256]{3,2,1,0:T(8,128)(2,1)S(1)}, bf16[1,4,64,256]{3,2,1,0:T(8,128)(2,1)S(1)}, u32[]{:S(2)}, u32[]{:S(2)}) collective-permute-start(bf16[1,4,64,256]{3,2,1,0:T(8,128)(2,1)S(1)} %get-tuple-element.47), channel_id=1, source_target_pairs={{0,8},{2,10},{4,12},{6,14},{8,0},{10,2},{12,4},{14,6},{1,9},{3,11}... | collective-permute-start | bytes 393224 | tf_op jit(solution)/shard_map/ppermute | solution.py:329
  52.6 13.8 %collective-permute-start.6 = (bf16[1,4,64,256]{3,2,1,0:T(8,128)(2,1)S(1)}, bf16[1,4,64,256]{3,2,1,0:T(8,128)(2,1)S(1)}, u32[]{:S(2)}, u32[]{:S(2)}) collective-permute-start(bf16[1,4,64,256]{3,2,1,0:T(8,128)(2,1)S(1)} %get-tuple-element.42), channel_id=1, source_target_pairs={{0,8},{2,10},{4,12},{6,14},{8,0},{10,2},{12,4},{14,6},{1,9},{3,11}... | collective-permute-start | bytes 393224 | tf_op jit(solution)/shard_map/ppermute | solution.py:329
  70.4 13.9 %collective-permute-start.25 = (bf16[4,64,256]{2,1,0:T(8,128)(2,1)S(1)}, bf16[4,64,256]{2,1,0:T(8,128)(2,1)S(1)}, u32[]{:S(2)}, u32[]{:S(2)}) collective-permute-start(bf16[4,64,256]{2,1,0:T(8,128)(2,1)S(1)} %get-tuple-element.59.refs_0_), channel_id=1, source_target_pairs={{0,8},{2,10},{4,12},{6,14},{8,0},{10,2},{12,4},{14,6},{1,9},{3,11}... | collective-permute-start | bytes 393224 | tf_op jit(solution)/shard_map/ppermute | solution.py:343
  70.5 16.7 %collective-permute-start.12 = (bf16[4,64,256]{2,1,0:T(8,128)(2,1)S(1)}, bf16[4,64,256]{2,1,0:T(8,128)(2,1)S(1)}, u32[]{:S(2)}, u32[]{:S(2)}) collective-permute-start(bf16[4,64,256]{2,1,0:T(8,128)(2,1)S(1)} %get-tuple-element.48.refs_0_), channel_id=1, source_target_pairs={{0,8},{2,10},{4,12},{6,14},{8,0},{10,2},{12,4},{14,6},{1,9},{3,11}... | collective-permute-start | bytes 393224 | tf_op jit(solution)/shard_map/ppermute | solution.py:343
  76.5 25.8 %collective-permute-start.18 = (bf16[8,128,128]{2,1,0:T(8,128)(2,1)S(1)}, bf16[8,128,128]{2,1,0:T(8,128)(2,1)S(1)}, u32[]{:S(2)}, u32[]{:S(2)}) collective-permute-start(bf16[8,128,128]{2,1,0:T(8,128)(2,1)S(1)} %collective-permute-done.7.refs_4_), channel_id=1, source_target_pairs={{0,2},{2,0},{1,3},{3,1},{4,6},{6,4},{5,7},{7,5},{8,10},{10,8},{9,1... | collective-permute-start | bytes 786440 | tf_op jit(solution)/shard_map/ppermute | solution.py:415
  77.6 12.5 %collective-permute-start.24 = (bf16[4,64,256]{2,1,0:T(8,128)(2,1)S(1)}, bf16[4,64,256]{2,1,0:T(8,128)(2,1)S(1)}, u32[]{:S(2)}, u32[]{:S(2)}) collective-permute-start(bf16[4,64,256]{2,1,0:T(8,128)(2,1)S(1)} %get-tuple-element.59.refs_0_), channel_id=1, source_target_pairs={{0,6},{2,4},{4,2},{6,0},{8,14},{10,12},{12,10},{14,8},{1,7},{3,5},... | collective-permute-start | bytes 393224 | tf_op jit(solution)/shard_map/ppermute | solution.py:343
  87.2 13.0 %collective-permute-start.11 = (bf16[4,64,256]{2,1,0:T(8,128)(2,1)S(1)}, bf16[4,64,256]{2,1,0:T(8,128)(2,1)S(1)}, u32[]{:S(2)}, u32[]{:S(2)}) collective-permute-start(bf16[4,64,256]{2,1,0:T(8,128)(2,1)S(1)} %get-tuple-element.48.refs_0_), channel_id=1, source_target_pairs={{0,6},{2,4},{4,2},{6,0},{8,14},{10,12},{12,10},{14,8},{1,7},{3,5},... | collective-permute-start | bytes 393224 | tf_op jit(solution)/shard_map/ppermute | solution.py:343
  87.7 12.6 %collective-permute-start.13 = (bf16[4,64,256]{2,1,0:T(8,128)(2,1)S(1)}, bf16[4,64,256]{2,1,0:T(8,128)(2,1)S(1)}, u32[]{:S(2)}, u32[]{:S(2)}) collective-permute-start(bf16[4,64,256]{2,1,0:T(8,128)(2,1)S(1)} %collective-permute-done.12.refs_2_), channel_id=1, source_target_pairs={{0,6},{2,4},{4,2},{6,0},{8,14},{10,12},{12,10},{14,8},{1,7},{3,5},... | collective-permute-start | bytes 393224 | tf_op jit(solution)/shard_map/ppermute | solution.py:343
  93.6 17.3 %collective-permute-start.19 = (bf16[8,128,128]{2,1,0:T(8,128)(2,1)S(1)}, bf16[8,128,128]{2,1,0:T(8,128)(2,1)S(1)}, u32[]{:S(2)}, u32[]{:S(2)}) collective-permute-start(bf16[8,128,128]{2,1,0:T(8,128)(2,1)S(1)} %collective-permute-done.8.refs_5_), channel_id=1, source_target_pairs={{0,2},{2,0},{1,3},{3,1},{4,6},{6,4},{5,7},{7,5},{8,10},{10,8},{9,1... | collective-permute-start | bytes 786440 | tf_op jit(solution)/shard_map/ppermute | solution.py:415
  100.2 16.2 %collective-permute-start.31 = (bf16[2,256,256]{2,1,0:T(8,128)(2,1)S(1)}, bf16[2,256,256]{2,1,0:T(8,128)(2,1)S(1)}, u32[]{:S(2)}, u32[]{:S(2)}) collective-permute-start(bf16[2,256,256]{2,1,0:T(8,128)(2,1)S(1)} %get-tuple-element.64.refs_1_), channel_id=1, source_target_pairs={{0,2},{2,0},{1,3},{3,1},{4,6},{6,4},{5,7},{7,5},{8,10},{10,8},{9,1... | collective-permute-start | bytes 786440 | tf_op jit(solution)/shard_map/ppermute | solution.py:415
  100.3 21.8 %collective-permute-start.27 = (bf16[2,256,256]{2,1,0:T(8,128)(2,1)S(1)}, bf16[2,256,256]{2,1,0:T(8,128)(2,1)S(1)}, u32[]{:S(2)}, u32[]{:S(2)}) collective-permute-start(bf16[2,256,256]{2,1,0:T(8,128)(2,1)S(1)} %get-tuple-element.61.refs_1_), channel_id=1, source_target_pairs={{0,2},{2,0},{1,3},{3,1},{4,6},{6,4},{5,7},{7,5},{8,10},{10,8},{9,1... | collective-permute-start | bytes 786440 | tf_op jit(solution)/shard_map/ppermute | solution.py:415
  102.3 25.4 %collective-permute-start.14 = (bf16[2,256,256]{2,1,0:T(8,128)(2,1)S(1)}, bf16[2,256,256]{2,1,0:T(8,128)(2,1)S(1)}, u32[]{:S(2)}, u32[]{:S(2)}) collective-permute-start(bf16[2,256,256]{2,1,0:T(8,128)(2,1)S(1)} %get-tuple-element.50.refs_1_), channel_id=1, source_target_pairs={{0,2},{2,0},{1,3},{3,1},{4,6},{6,4},{5,7},{7,5},{8,10},{10,8},{9,1... | collective-permute-start | bytes 786440 | tf_op jit(solution)/shard_map/ppermute | solution.py:415
  124.0 31.9 %collective-permute-start.33 = (bf16[1,256,1024]{2,1,0:T(8,128)(2,1)S(1)}, bf16[1,256,1024]{2,1,0:T(8,128)(2,1)S(1)}, u32[]{:S(2)}, u32[]{:S(2)}) collective-permute-start(bf16[1,256,1024]{2,1,0:T(8,128)(2,1)S(1)} %get-tuple-element.68), channel_id=1, source_target_pairs={{0,1},{1,0},{2,3},{3,2},{4,5},{5,4},{6,7},{7,6},{8,9},{9,8},{10,11... | collective-permute-start | bytes 1572872 | tf_op jit(solution)/shard_map/ppermute | solution.py:462
  129.1 27.7 %collective-permute-start.20 = (bf16[1,256,1024]{2,1,0:T(8,128)(2,1)S(1)}, bf16[1,256,1024]{2,1,0:T(8,128)(2,1)S(1)}, u32[]{:S(2)}, u32[]{:S(2)}) collective-permute-start(bf16[1,256,1024]{2,1,0:T(8,128)(2,1)S(1)} %get-tuple-element.53), channel_id=1, source_target_pairs={{0,1},{1,0},{2,3},{3,2},{4,5},{5,4},{6,7},{7,6},{8,9},{9,8},{10,11... | collective-permute-start | bytes 1572872 | tf_op jit(solution)/shard_map/ppermute | solution.py:462
  131.5 15.4 %collective-permute-start.35 = (bf16[2,4,128,128]{3,2,1,0:T(8,128)(2,1)S(1)}, bf16[2,4,128,128]{3,2,1,0:T(8,128)(2,1)S(1)}, u32[]{:S(2)}, u32[]{:S(2)}) collective-permute-start(bf16[2,4,128,128]{3,2,1,0:T(8,128)(2,1)S(1)} %shard_map.137), channel_id=1, source_target_pairs={{0,0},{1,8},{2,4},{3,12},{4,5},{5,13},{6,1},{7,9},{8,2},{9,10},{10... | collective-permute-start | bytes 786440 | tf_op jit(solution)/shard_map/ppermute | solution.py:470
  138.5 12.6 %collective-permute-start.34 = (bf16[2,4,128,128]{3,2,1,0:T(8,128)(2,1)S(1)}, bf16[2,4,128,128]{3,2,1,0:T(8,128)(2,1)S(1)}, u32[]{:S(2)}, u32[]{:S(2)}) collective-permute-start(bf16[2,4,128,128]{3,2,1,0:T(8,128)(2,1)S(1)} %shard_map.135), channel_id=1, source_target_pairs={{0,0},{1,8},{2,4},{3,12},{4,5},{5,13},{6,1},{7,9},{8,2},{9,10},{10... | collective-permute-start | bytes 786440 | tf_op jit(solution)/shard_map/ppermute | solution.py:470
  (18 other events, 187.3 us)

commit v5 on v4

--- a/solution.py
+++ b/solution.py
@@ -10,7 +10,7 @@
 BF = jnp.bfloat16
 F32 = jnp.float32
 LIMIT = 16 << 20
-Z, Q, OWNER, OWNED, GROUP = range(5)
+Z, Q, _, OWNED, GROUP = range(5)
 PLANE = ("shard", "dp", "tok")
 
 
@@ -99,9 +99,10 @@
         out[d // 2, r] = total[r, pl.ds(aligned(z ^ d, rows), rows), :].astype(out.dtype)
 
 
-def pack_kernel(info, gate_rows, up_rows, gate, up, down, rows_out, gate_out, half_out, sems):
+def pack_kernel(mesh_sizes, owned, gate_rows, up_rows, gate, up, down, rows_out, gate_out, half_out, sems):
     columns, per_owner = rows_out.shape[1:]
-    owner, group = info[OWNER], info[GROUP]
+    owner = weight_owner(*mesh_sizes, *(lax.axis_index(name) for name in PLANE))
+    group = lax.axis_index("groups")
     here = pl.ds(owner * per_owner, per_owner)
     pairs = [(gate.at[c, here], gate_out.at[pl.ds(c * per_owner, per_owner)]) for c in range(columns)]
     pairs.append((up.at[group, here], half_out.at[pl.ds(0, per_owner)]))
@@ -112,7 +113,7 @@
     for i, rows in enumerate((gate_rows, up_rows)):
         for c in range(columns):
             for k in range(per_owner):
-                rows_out[i, c, k] = rows[c, owner * per_owner + k] - owner * info[OWNED]
+                rows_out[i, c, k] = rows[c, owner * per_owner + k] - owner * owned
     for copy in copies:
         copy.wait()
 
@@ -360,8 +361,8 @@
     owner = weight_owner(shards, n_dp, n_tok, z, x_index, c_index)
     info = jnp.stack([v.astype(jnp.int32) for v in (z, q, owner, jnp.int32(owned), group)])
     rows, gate_part, half_mine = run(
-        pack_kernel,
-        [info, gate_rows, up_rows],
+        functools.partial(pack_kernel, (shards, n_dp, n_tok), owned),
+        [gate_rows, up_rows],
         [],
         [shape((2, columns, per_owner), jnp.int32)] + [shape((n * blocks, size, size), BF) for n in (1, 1)],
         [pltpu.SemaphoreType.DMA((columns + 2,))],

time: 158 us -> 159 us (level)
  the two profiles are of different devices: /device:TPU:3 before, /device:TPU:6 now
where the time goes in v5:
time: 159 us
  waiting for transfers between devices  75.1 us (47%)
  starting transfers between devices  57.3 us (36%)
  Pallas kernels  23.7 us (15%)
  local copies, waits for them, and re-layouts  1.76 us (1%)
    pallas_call x22, Pallas kernels, call(): pl.pallas_call(kernel, out_shape=outs, in_specs=smem(len(scalars)) + vmem...  23.7 us
    ppermute x7, waiting for transfers between devices, body(): to_dp = lambda a, dx: lax.ppermute(a, 'dp', xor_perm(n_dp, dx))  21.9 us
    ppermute x6, waiting for transfers between devices, reduce(): arrived = lax.ppermute(far, ('shard', 'dp'), shard_perm(shards, n_dp, bit))  21.2 us
    ppermute x9, waiting for transfers between devices, gather(): lax.ppermute(have[d], ('shard', 'dp'), shard_perm(shards, n_dp, bit))  12.4 us
    ppermute x9, starting transfers between devices, gather(): lax.ppermute(have[d], ('shard', 'dp'), shard_perm(shards, n_dp, bit))  10.4 us
    ppermute x7, starting transfers between devices, body(): to_dp = lambda a, dx: lax.ppermute(a, 'dp', xor_perm(n_dp, dx))  10.1 us
    ppermute x6, starting transfers between devices, reduce(): arrived = lax.ppermute(far, ('shard', 'dp'), shard_perm(shards, n_dp, bit))  9.75 us
    ppermute x3, starting transfers between devices, home(): grad = lax.ppermute(grad, PLANE, g_perm)  9.42 us
  transfers between devices with their start and end apart: 37, of which 22 were waited for; matrix products, arithmetic and copies ran while one was open for 0% of the time, Pallas kernels for 14%

profile of v5, /device:TPU:6, one launch (start us, length us, event | category | flops | bytes accessed | tf_op | source)
XLA Modules:
  0.0 158.8 jit_solution(15179185603389432417)
XLA Ops:
  2.7 2.6 %shard_map.119 = (s32[2,2,4]{2,1,0:T(2,128)}, bf16[8,128,128]{2,1,0:T(8,128)(2,1)}, bf16[8,128,128]{2,1,0:T(8,128)(2,1)}) custom-call(s32[2,16]{1,0:T(2,128)} %gate_rows.1, s32[2,16]{1,0:T(2,128)} %up_rows.1, bf16[2,16,128,128]{3,2,1,0:T(8,128)(2,1)} %gate.1, bf16[2,16,128,128]{3,2,1,0:T(8,128)(2,1)} %up.1, bf16[2,16,128,128]{3,2,1,0:T(8,128)(2,1)} %down.1), custom_call_target="tpu_custom_call" | custom-call | bytes 3670080 | tf_op jit(solution)/shard_map/pallas_call | solution.py:66
  5.4 3.5 %collective-permute-start.7 = (bf16[8,128,128]{2,1,0:T(8,128)(2,1)}, bf16[8,128,128]{2,1,0:T(8,128)(2,1)S(1)}, u32[]{:S(2)}, u32[]{:S(2)}) collective-permute-start(bf16[8,128,128]{2,1,0:T(8,128)(2,1)} %get-tuple-element.43), channel_id=1, source_target_pairs={{0,0},{8,1},{6,2},{14,3},{4,4},{12,5},{2,6},{10,7},{1,8},{9,9},{7,... | collective-permute-start | bytes 786440 | tf_op jit(solution)/shard_map/ppermute | solution.py:376
  11.1 4.6 %collective-permute-done.2.refs_2_.refs_4_ = bf16[256,1024]{1,0:T(8,128)(2,1)S(1)} collective-permute-done((bf16[256,1024]{1,0:T(8,128)(2,1)}, bf16[256,1024]{1,0:T(8,128)(2,1)S(1)}, u32[]{:S(2)}, u32[]{:S(2)}) %collective-permute-start.2) | collective-permute-done | bytes 524320 | tf_op jit(solution)/shard_map/ppermute | solution.py:354
  16.2 3.5 %collective-permute-start = (s32[2,2,4]{2,1,0:T(2,128)S(1)}, s32[2,2,4]{2,1,0:T(2,128)S(1)}, u32[]{:S(2)}, u32[]{:S(2)}) collective-permute-start(s32[2,2,4]{2,1,0:T(2,128)S(1)} %copy-done.6), channel_id=1, source_target_pairs={{0,0},{8,1},{6,2},{14,3},{4,4},{12,5},{2,6},{10,7},{1,8},{9,9},{7,... | collective-permute-start | bytes 200 | tf_op jit(solution)/shard_map/ppermute | solution.py:375
  26.5 3.5 %collective-permute-start.4 = (bf16[8,128,128]{2,1,0:T(8,128)(2,1)}, bf16[8,128,128]{2,1,0:T(8,128)(2,1)}, u32[]{:S(2)}, u32[]{:S(2)}) collective-permute-start(bf16[8,128,128]{2,1,0:T(8,128)(2,1)} %get-tuple-element.38), channel_id=1, source_target_pairs={{0,0},{8,1},{6,2},{14,3},{4,4},{12,5},{2,6},{10,7},{1,8},{9,9},{7,... | collective-permute-start | bytes 786440 | tf_op jit(solution)/shard_map/ppermute | solution.py:374
  40.1 3.0 %collective-permute-start.22 = (bf16[2,4,64,256]{3,2,1,0:T(8,128)(2,1)S(1)}, bf16[2,4,64,256]{3,2,1,0:T(8,128)(2,1)S(1)}, u32[]{:S(2)}, u32[]{:S(2)}) collective-permute-start(bf16[2,4,64,256]{3,2,1,0:T(8,128)(2,1)S(1)} %get-tuple-element.56), channel_id=1, source_target_pairs={{0,6},{2,4},{4,2},{6,0},{8,14},{10,12},{12,10},{14,8},{1,7},{3,5},... | collective-permute-start | bytes 786440 | tf_op jit(solution)/shard_map/ppermute | solution.py:330
  46.7 5.4 %collective-permute-done.5.arrived = bf16[2,4,64,256]{3,2,1,0:T(8,128)(2,1)S(1)} collective-permute-done((bf16[2,4,64,256]{3,2,1,0:T(8,128)(2,1)S(1)}, bf16[2,4,64,256]{3,2,1,0:T(8,128)(2,1)S(1)}, u32[]{:S(2)}, u32[]{:S(2)}) %collective-permute-start.5) | collective-permute-done | bytes 262176 | tf_op jit(solution)/shard_map/ppermute | solution.py:330
  52.5 5.3 %collective-permute-done.22.arrived = bf16[2,4,64,256]{3,2,1,0:T(8,128)(2,1)S(1)} collective-permute-done((bf16[2,4,64,256]{3,2,1,0:T(8,128)(2,1)S(1)}, bf16[2,4,64,256]{3,2,1,0:T(8,128)(2,1)S(1)}, u32[]{:S(2)}, u32[]{:S(2)}) %collective-permute-start.22) | collective-permute-done | bytes 262176 | tf_op jit(solution)/shard_map/ppermute | solution.py:330
  60.2 6.6 %collective-permute-done.6.gate_last = bf16[1,4,64,256]{3,2,1,0:T(8,128)(2,1)S(1)} collective-permute-done((bf16[1,4,64,256]{3,2,1,0:T(8,128)(2,1)S(1)}, bf16[1,4,64,256]{3,2,1,0:T(8,128)(2,1)S(1)}, u32[]{:S(2)}, u32[]{:S(2)}) %collective-permute-start.6) | collective-permute-done | bytes 131104 | tf_op jit(solution)/shard_map/ppermute | solution.py:330
  66.9 2.7 %collective-permute-done.23.last = bf16[1,4,64,256]{3,2,1,0:T(8,128)(2,1)S(1)} collective-permute-done((bf16[1,4,64,256]{3,2,1,0:T(8,128)(2,1)S(1)}, bf16[1,4,64,256]{3,2,1,0:T(8,128)(2,1)S(1)}, u32[]{:S(2)}, u32[]{:S(2)}) %collective-permute-start.23) | collective-permute-done | bytes 131104 | tf_op jit(solution)/shard_map/ppermute | solution.py:330
  75.0 2.9 %collective-permute-done.29.refs_2_ = bf16[4,64,256]{2,1,0:T(8,128)(2,1)S(1)} collective-permute-done((bf16[4,64,256]{2,1,0:T(8,128)(2,1)S(1)}, bf16[4,64,256]{2,1,0:T(8,128)(2,1)S(1)}, u32[]{:S(2)}, u32[]{:S(2)}) %collective-permute-start.29) | collective-permute-done | bytes 131104 | tf_op jit(solution)/shard_map/ppermute | solution.py:344
  79.7 2.9 %collective-permute-start.24 = (bf16[4,64,256]{2,1,0:T(8,128)(2,1)S(1)}, bf16[4,64,256]{2,1,0:T(8,128)(2,1)S(1)}, u32[]{:S(2)}, u32[]{:S(2)}) collective-permute-start(bf16[4,64,256]{2,1,0:T(8,128)(2,1)S(1)} %get-tuple-element.59.refs_0_), channel_id=1, source_target_pairs={{0,6},{2,4},{4,2},{6,0},{8,14},{10,12},{12,10},{14,8},{1,7},{3,5},... | collective-permute-start | bytes 393224 | tf_op jit(solution)/shard_map/ppermute | solution.py:344
  82.6 3.1 %collective-permute-done.25.refs_2_ = bf16[4,64,256]{2,1,0:T(8,128)(2,1)S(1)} collective-permute-done((bf16[4,64,256]{2,1,0:T(8,128)(2,1)S(1)}, bf16[4,64,256]{2,1,0:T(8,128)(2,1)S(1)}, u32[]{:S(2)}, u32[]{:S(2)}) %collective-permute-start.25) | collective-permute-done | bytes 131104 | tf_op jit(solution)/shard_map/ppermute | solution.py:344
  97.6 4.1 %collective-permute-start.19 = (bf16[8,128,128]{2,1,0:T(8,128)(2,1)S(1)}, bf16[8,128,128]{2,1,0:T(8,128)(2,1)S(1)}, u32[]{:S(2)}, u32[]{:S(2)}) collective-permute-start(bf16[8,128,128]{2,1,0:T(8,128)(2,1)S(1)} %copy-done.4), channel_id=1, source_target_pairs={{0,2},{2,0},{1,3},{3,1},{4,6},{6,4},{5,7},{7,5},{8,10},{10,8},{9,1... | collective-permute-start | bytes 786440 | tf_op jit(solution)/shard_map/ppermute | solution.py:416
  106.0 5.6 %collective-permute-done.19.refs_4_.refs_9_ = bf16[8,128,128]{2,1,0:T(8,128)(2,1)S(1)} collective-permute-done((bf16[8,128,128]{2,1,0:T(8,128)(2,1)S(1)}, bf16[8,128,128]{2,1,0:T(8,128)(2,1)S(1)}, u32[]{:S(2)}, u32[]{:S(2)}) %collective-permute-start.19) | collective-permute-done | bytes 262176 | tf_op jit(solution)/shard_map/ppermute | solution.py:416
  111.6 5.6 %collective-permute-done.31.refs_4_ = bf16[2,256,256]{2,1,0:T(8,128)(2,1)S(1)} collective-permute-done((bf16[2,256,256]{2,1,0:T(8,128)(2,1)S(1)}, bf16[2,256,256]{2,1,0:T(8,128)(2,1)S(1)}, u32[]{:S(2)}, u32[]{:S(2)}) %collective-permute-start.31) | collective-permute-done | bytes 262176 | tf_op jit(solution)/shard_map/ppermute | solution.py:416
  117.2 5.6 %collective-permute-done.27.refs_2_ = bf16[2,256,256]{2,1,0:T(8,128)(2,1)S(1)} collective-permute-done((bf16[2,256,256]{2,1,0:T(8,128)(2,1)S(1)}, bf16[2,256,256]{2,1,0:T(8,128)(2,1)S(1)}, u32[]{:S(2)}, u32[]{:S(2)}) %collective-permute-start.27) | collective-permute-done | bytes 262176 | tf_op jit(solution)/shard_map/ppermute | solution.py:416
  124.9 3.5 %collective-permute-done.14.refs_1_ = bf16[2,256,256]{2,1,0:T(8,128)(2,1)S(1)} collective-permute-done((bf16[2,256,256]{2,1,0:T(8,128)(2,1)S(1)}, bf16[2,256,256]{2,1,0:T(8,128)(2,1)S(1)}, u32[]{:S(2)}, u32[]{:S(2)}) %collective-permute-start.14) | collective-permute-done | bytes 262176 | tf_op jit(solution)/shard_map/ppermute | solution.py:416
  131.8 4.2 %collective-permute-start.35 = (bf16[2,4,128,128]{3,2,1,0:T(8,128)(2,1)S(1)}, bf16[2,4,128,128]{3,2,1,0:T(8,128)(2,1)S(1)}, u32[]{:S(2)}, u32[]{:S(2)}) collective-permute-start(bf16[2,4,128,128]{3,2,1,0:T(8,128)(2,1)S(1)} %shard_map.137), channel_id=1, source_target_pairs={{0,0},{1,8},{2,4},{3,12},{4,5},{5,13},{6,1},{7,9},{8,2},{9,10},{10... | collective-permute-start | bytes 786440 | tf_op jit(solution)/shard_map/ppermute | solution.py:471
  137.8 2.4 %collective-permute-start.34 = (bf16[2,4,128,128]{3,2,1,0:T(8,128)(2,1)S(1)}, bf16[2,4,128,128]{3,2,1,0:T(8,128)(2,1)S(1)}, u32[]{:S(2)}, u32[]{:S(2)}) collective-permute-start(bf16[2,4,128,128]{3,2,1,0:T(8,128)(2,1)S(1)} %shard_map.135), channel_id=1, source_target_pairs={{0,0},{1,8},{2,4},{3,12},{4,5},{5,13},{6,1},{7,9},{8,2},{9,10},{10... | collective-permute-start | bytes 786440 | tf_op jit(solution)/shard_map/ppermute | solution.py:471
  140.2 2.5 %shard_map.139 = bf16[2,4,128,128]{3,2,1,0:T(8,128)(2,1)S(1)} custom-call(s32[5]{0:T(128)S(1)} %stack.16.info, s32[8,16]{1,0:T(8,128)S(1)} %copy-done.5, bf16[2,256,256]{2,1,0:T(8,128)(2,1)S(1)} %get-tuple-element.49.refs_0_, bf16[2,256,256]{2,1,0:T(8,128)(2,1)S(1)} %get-tuple-element.50.refs_1_, bf16[256,1024]{1,0:T(8,128)(2,1)S(1)} %copy-done.1, ...), custom_call_target="tpu_custom_call" | custom-call | flops 536870912 | bytes 2883584 | tf_op jit(solution)/shard_map/pallas_call | solution.py:66
  142.8 2.9 %collective-permute-start.36 = (bf16[2,4,128,128]{3,2,1,0:T(8,128)(2,1)S(1)}, bf16[2,4,128,128]{3,2,1,0:T(8,128)(2,1)S(1)}, u32[]{:S(2)}, u32[]{:S(2)}) collective-permute-start(bf16[2,4,128,128]{3,2,1,0:T(8,128)(2,1)S(1)} %shard_map.139), channel_id=1, source_target_pairs={{0,0},{1,8},{2,4},{3,12},{4,5},{5,13},{6,1},{7,9},{8,2},{9,10},{10... | collective-permute-start | bytes 786440 | tf_op jit(solution)/shard_map/ppermute | solution.py:471
  146.4 4.3 %collective-permute-done.34.refs_0_ = bf16[2,4,128,128]{3,2,1,0:T(8,128)(2,1)S(1)} collective-permute-done((bf16[2,4,128,128]{3,2,1,0:T(8,128)(2,1)S(1)}, bf16[2,4,128,128]{3,2,1,0:T(8,128)(2,1)S(1)}, u32[]{:S(2)}, u32[]{:S(2)}) %collective-permute-start.34) | collective-permute-done | bytes 262176 | tf_op jit(solution)/shard_map/ppermute | solution.py:471
  151.4 4.9 %collective-permute-done.36.refs_0_ = bf16[2,4,128,128]{3,2,1,0:T(8,128)(2,1)S(1)} collective-permute-done((bf16[2,4,128,128]{3,2,1,0:T(8,128)(2,1)S(1)}, bf16[2,4,128,128]{3,2,1,0:T(8,128)(2,1)S(1)}, u32[]{:S(2)}, u32[]{:S(2)}) %collective-permute-start.36) | collective-permute-done | bytes 262176 | tf_op jit(solution)/shard_map/ppermute | solution.py:471
  (87 shorter events, 62.6 us)
Async XLA Ops:
  0.7 15.1 %collective-permute-start.2 = (bf16[256,1024]{1,0:T(8,128)(2,1)}, bf16[256,1024]{1,0:T(8,128)(2,1)S(1)}, u32[]{:S(2)}, u32[]{:S(2)}) collective-permute-start(bf16[256,1024]{1,0:T(8,128)(2,1)} %refs_2_.4), channel_id=1, source_target_pairs={{0,2},{2,0},{1,3},{3,1},{4,6},{6,4},{5,7},{7,5},{8,10},{10,8},{9,1... | collective-permute-start | bytes 1572872 | tf_op jit(solution)/shard_map/ppermute | solution.py:354
  1.3 24.6 %collective-permute-start.16 = (bf16[256,1024]{1,0:T(8,128)(2,1)}, bf16[256,1024]{1,0:T(8,128)(2,1)S(1)}, u32[]{:S(2)}, u32[]{:S(2)}) collective-permute-start(bf16[256,1024]{1,0:T(8,128)(2,1)} %refs_2_.5), channel_id=1, source_target_pairs={{0,2},{2,0},{1,3},{3,1},{4,6},{6,4},{5,7},{7,5},{8,10},{10,8},{9,1... | collective-permute-start | bytes 1572872 | tf_op jit(solution)/shard_map/ppermute | solution.py:354
  8.9 21.2 %collective-permute-start.1 = (bf16[256,1024]{1,0:T(8,128)(2,1)S(1)}, bf16[256,1024]{1,0:T(8,128)(2,1)S(1)}, u32[]{:S(2)}, u32[]{:S(2)}) collective-permute-start(bf16[256,1024]{1,0:T(8,128)(2,1)S(1)} %copy-done), channel_id=1, source_target_pairs={{0,1},{1,0},{2,3},{3,2},{4,5},{5,4},{6,7},{7,6},{8,9},{9,8},{10,11... | collective-permute-start | bytes 1572872 | tf_op jit(solution)/shard_map/ppermute | solution.py:357
  15.7 14.4 %collective-permute-start.3 = (bf16[256,1024]{1,0:T(8,128)(2,1)S(1)}, bf16[256,1024]{1,0:T(8,128)(2,1)S(1)}, u32[]{:S(2)}, u32[]{:S(2)}) collective-permute-start(bf16[256,1024]{1,0:T(8,128)(2,1)S(1)} %collective-permute-done.2.refs_2_.refs_4_), channel_id=1, source_target_pairs={{0,1},{1,0},{2,3},{3,2},{4,5},{5,4},{6,7},{7,6},{8,9},{9,8},{10,11... | collective-permute-start | bytes 1572872 | tf_op jit(solution)/shard_map/ppermute | solution.py:357
  21.7 16.2 %collective-permute-start.15 = (bf16[256,1024]{1,0:T(8,128)(2,1)S(1)}, bf16[256,1024]{1,0:T(8,128)(2,1)}, u32[]{:S(2)}, u32[]{:S(2)}) collective-permute-start(bf16[256,1024]{1,0:T(8,128)(2,1)S(1)} %copy-done.1), channel_id=1, source_target_pairs={{0,1},{1,0},{2,3},{3,2},{4,5},{5,4},{6,7},{7,6},{8,9},{9,8},{10,11... | collective-permute-start | bytes 1572872 | tf_op jit(solution)/shard_map/ppermute | solution.py:357
  37.9 14.3 %collective-permute-start.5 = (bf16[2,4,64,256]{3,2,1,0:T(8,128)(2,1)S(1)}, bf16[2,4,64,256]{3,2,1,0:T(8,128)(2,1)S(1)}, u32[]{:S(2)}, u32[]{:S(2)}) collective-permute-start(bf16[2,4,64,256]{3,2,1,0:T(8,128)(2,1)S(1)} %get-tuple-element.40), channel_id=1, source_target_pairs={{0,6},{2,4},{4,2},{6,0},{8,14},{10,12},{12,10},{14,8},{1,7},{3,5},... | collective-permute-start | bytes 786440 | tf_op jit(solution)/shard_map/ppermute | solution.py:330
  40.1 17.7 %collective-permute-start.22 = (bf16[2,4,64,256]{3,2,1,0:T(8,128)(2,1)S(1)}, bf16[2,4,64,256]{3,2,1,0:T(8,128)(2,1)S(1)}, u32[]{:S(2)}, u32[]{:S(2)}) collective-permute-start(bf16[2,4,64,256]{3,2,1,0:T(8,128)(2,1)S(1)} %get-tuple-element.56), channel_id=1, source_target_pairs={{0,6},{2,4},{4,2},{6,0},{8,14},{10,12},{12,10},{14,8},{1,7},{3,5},... | collective-permute-start | bytes 786440 | tf_op jit(solution)/shard_map/ppermute | solution.py:330
  44.3 15.9 %collective-permute-start.10 = (bf16[1,4,64,256]{3,2,1,0:T(8,128)(2,1)S(1)}, bf16[1,4,64,256]{3,2,1,0:T(8,128)(2,1)S(1)}, u32[]{:S(2)}, u32[]{:S(2)}) collective-permute-start(bf16[1,4,64,256]{3,2,1,0:T(8,128)(2,1)S(1)} %get-tuple-element.47), channel_id=1, source_target_pairs={{0,8},{2,10},{4,12},{6,14},{8,0},{10,2},{12,4},{14,6},{1,9},{3,11}... | collective-permute-start | bytes 393224 | tf_op jit(solution)/shard_map/ppermute | solution.py:330
  52.2 14.7 %collective-permute-start.6 = (bf16[1,4,64,256]{3,2,1,0:T(8,128)(2,1)S(1)}, bf16[1,4,64,256]{3,2,1,0:T(8,128)(2,1)S(1)}, u32[]{:S(2)}, u32[]{:S(2)}) collective-permute-start(bf16[1,4,64,256]{3,2,1,0:T(8,128)(2,1)S(1)} %get-tuple-element.42), channel_id=1, source_target_pairs={{0,8},{2,10},{4,12},{6,14},{8,0},{10,2},{12,4},{14,6},{1,9},{3,11}... | collective-permute-start | bytes 393224 | tf_op jit(solution)/shard_map/ppermute | solution.py:330
  72.1 13.6 %collective-permute-start.25 = (bf16[4,64,256]{2,1,0:T(8,128)(2,1)S(1)}, bf16[4,64,256]{2,1,0:T(8,128)(2,1)S(1)}, u32[]{:S(2)}, u32[]{:S(2)}) collective-permute-start(bf16[4,64,256]{2,1,0:T(8,128)(2,1)S(1)} %get-tuple-element.59.refs_0_), channel_id=1, source_target_pairs={{0,8},{2,10},{4,12},{6,14},{8,0},{10,2},{12,4},{14,6},{1,9},{3,11}... | collective-permute-start | bytes 393224 | tf_op jit(solution)/shard_map/ppermute | solution.py:344
  72.8 15.3 %collective-permute-start.12 = (bf16[4,64,256]{2,1,0:T(8,128)(2,1)S(1)}, bf16[4,64,256]{2,1,0:T(8,128)(2,1)S(1)}, u32[]{:S(2)}, u32[]{:S(2)}) collective-permute-start(bf16[4,64,256]{2,1,0:T(8,128)(2,1)S(1)} %get-tuple-element.48.refs_0_), channel_id=1, source_target_pairs={{0,8},{2,10},{4,12},{6,14},{8,0},{10,2},{12,4},{14,6},{1,9},{3,11}... | collective-permute-start | bytes 393224 | tf_op jit(solution)/shard_map/ppermute | solution.py:344
  78.0 12.3 %collective-permute-start.30 = (bf16[4,64,256]{2,1,0:T(8,128)(2,1)S(1)}, bf16[4,64,256]{2,1,0:T(8,128)(2,1)S(1)}, u32[]{:S(2)}, u32[]{:S(2)}) collective-permute-start(bf16[4,64,256]{2,1,0:T(8,128)(2,1)S(1)} %collective-permute-done.29.refs_2_), channel_id=1, source_target_pairs={{0,6},{2,4},{4,2},{6,0},{8,14},{10,12},{12,10},{14,8},{1,7},{3,5},... | collective-permute-start | bytes 393224 | tf_op jit(solution)/shard_map/ppermute | solution.py:344
  78.1 26.3 %collective-permute-start.18 = (bf16[8,128,128]{2,1,0:T(8,128)(2,1)S(1)}, bf16[8,128,128]{2,1,0:T(8,128)(2,1)S(1)}, u32[]{:S(2)}, u32[]{:S(2)}) collective-permute-start(bf16[8,128,128]{2,1,0:T(8,128)(2,1)S(1)} %collective-permute-done.7.refs_4_), channel_id=1, source_target_pairs={{0,2},{2,0},{1,3},{3,1},{4,6},{6,4},{5,7},{7,5},{8,10},{10,8},{9,1... | collective-permute-start | bytes 786440 | tf_op jit(solution)/shard_map/ppermute | solution.py:416
  79.7 13.4 %collective-permute-start.24 = (bf16[4,64,256]{2,1,0:T(8,128)(2,1)S(1)}, bf16[4,64,256]{2,1,0:T(8,128)(2,1)S(1)}, u32[]{:S(2)}, u32[]{:S(2)}) collective-permute-start(bf16[4,64,256]{2,1,0:T(8,128)(2,1)S(1)} %get-tuple-element.59.refs_0_), channel_id=1, source_target_pairs={{0,6},{2,4},{4,2},{6,0},{8,14},{10,12},{12,10},{14,8},{1,7},{3,5},... | collective-permute-start | bytes 393224 | tf_op jit(solution)/shard_map/ppermute | solution.py:344
  88.0 13.7 %collective-permute-start.11 = (bf16[4,64,256]{2,1,0:T(8,128)(2,1)S(1)}, bf16[4,64,256]{2,1,0:T(8,128)(2,1)S(1)}, u32[]{:S(2)}, u32[]{:S(2)}) collective-permute-start(bf16[4,64,256]{2,1,0:T(8,128)(2,1)S(1)} %get-tuple-element.48.refs_0_), channel_id=1, source_target_pairs={{0,6},{2,4},{4,2},{6,0},{8,14},{10,12},{12,10},{14,8},{1,7},{3,5},... | collective-permute-start | bytes 393224 | tf_op jit(solution)/shard_map/ppermute | solution.py:344
  97.6 14.0 %collective-permute-start.19 = (bf16[8,128,128]{2,1,0:T(8,128)(2,1)S(1)}, bf16[8,128,128]{2,1,0:T(8,128)(2,1)S(1)}, u32[]{:S(2)}, u32[]{:S(2)}) collective-permute-start(bf16[8,128,128]{2,1,0:T(8,128)(2,1)S(1)} %copy-done.4), channel_id=1, source_target_pairs={{0,2},{2,0},{1,3},{3,1},{4,6},{6,4},{5,7},{7,5},{8,10},{10,8},{9,1... | collective-permute-start | bytes 786440 | tf_op jit(solution)/shard_map/ppermute | solution.py:416
  101.8 15.5 %collective-permute-start.31 = (bf16[2,256,256]{2,1,0:T(8,128)(2,1)S(1)}, bf16[2,256,256]{2,1,0:T(8,128)(2,1)S(1)}, u32[]{:S(2)}, u32[]{:S(2)}) collective-permute-start(bf16[2,256,256]{2,1,0:T(8,128)(2,1)S(1)} %get-tuple-element.64.refs_1_), channel_id=1, source_target_pairs={{0,2},{2,0},{1,3},{3,1},{4,6},{6,4},{5,7},{7,5},{8,10},{10,8},{9,1... | collective-permute-start | bytes 786440 | tf_op jit(solution)/shard_map/ppermute | solution.py:416
  101.8 21.0 %collective-permute-start.27 = (bf16[2,256,256]{2,1,0:T(8,128)(2,1)S(1)}, bf16[2,256,256]{2,1,0:T(8,128)(2,1)S(1)}, u32[]{:S(2)}, u32[]{:S(2)}) collective-permute-start(bf16[2,256,256]{2,1,0:T(8,128)(2,1)S(1)} %get-tuple-element.61.refs_1_), channel_id=1, source_target_pairs={{0,2},{2,0},{1,3},{3,1},{4,6},{6,4},{5,7},{7,5},{8,10},{10,8},{9,1... | collective-permute-start | bytes 786440 | tf_op jit(solution)/shard_map/ppermute | solution.py:416
  104.4 24.0 %collective-permute-start.14 = (bf16[2,256,256]{2,1,0:T(8,128)(2,1)S(1)}, bf16[2,256,256]{2,1,0:T(8,128)(2,1)S(1)}, u32[]{:S(2)}, u32[]{:S(2)}) collective-permute-start(bf16[2,256,256]{2,1,0:T(8,128)(2,1)S(1)} %get-tuple-element.50.refs_1_), channel_id=1, source_target_pairs={{0,2},{2,0},{1,3},{3,1},{4,6},{6,4},{5,7},{7,5},{8,10},{10,8},{9,1... | collective-permute-start | bytes 786440 | tf_op jit(solution)/shard_map/ppermute | solution.py:416
  124.8 32.2 %collective-permute-start.33 = (bf16[1,256,1024]{2,1,0:T(8,128)(2,1)S(1)}, bf16[1,256,1024]{2,1,0:T(8,128)(2,1)S(1)}, u32[]{:S(2)}, u32[]{:S(2)}) collective-permute-start(bf16[1,256,1024]{2,1,0:T(8,128)(2,1)S(1)} %get-tuple-element.68), channel_id=1, source_target_pairs={{0,1},{1,0},{2,3},{3,2},{4,5},{5,4},{6,7},{7,6},{8,9},{9,8},{10,11... | collective-permute-start | bytes 1572872 | tf_op jit(solution)/shard_map/ppermute | solution.py:463
  129.8 28.1 %collective-permute-start.20 = (bf16[1,256,1024]{2,1,0:T(8,128)(2,1)S(1)}, bf16[1,256,1024]{2,1,0:T(8,128)(2,1)S(1)}, u32[]{:S(2)}, u32[]{:S(2)}) collective-permute-start(bf16[1,256,1024]{2,1,0:T(8,128)(2,1)S(1)} %get-tuple-element.53), channel_id=1, source_target_pairs={{0,1},{1,0},{2,3},{3,2},{4,5},{5,4},{6,7},{7,6},{8,9},{9,8},{10,11... | collective-permute-start | bytes 1572872 | tf_op jit(solution)/shard_map/ppermute | solution.py:463
  131.8 13.8 %collective-permute-start.35 = (bf16[2,4,128,128]{3,2,1,0:T(8,128)(2,1)S(1)}, bf16[2,4,128,128]{3,2,1,0:T(8,128)(2,1)S(1)}, u32[]{:S(2)}, u32[]{:S(2)}) collective-permute-start(bf16[2,4,128,128]{3,2,1,0:T(8,128)(2,1)S(1)} %shard_map.137), channel_id=1, source_target_pairs={{0,0},{1,8},{2,4},{3,12},{4,5},{5,13},{6,1},{7,9},{8,2},{9,10},{10... | collective-permute-start | bytes 786440 | tf_op jit(solution)/shard_map/ppermute | solution.py:471
  137.8 12.9 %collective-permute-start.34 = (bf16[2,4,128,128]{3,2,1,0:T(8,128)(2,1)S(1)}, bf16[2,4,128,128]{3,2,1,0:T(8,128)(2,1)S(1)}, u32[]{:S(2)}, u32[]{:S(2)}) collective-permute-start(bf16[2,4,128,128]{3,2,1,0:T(8,128)(2,1)S(1)} %shard_map.135), channel_id=1, source_target_pairs={{0,0},{1,8},{2,4},{3,12},{4,5},{5,13},{6,1},{7,9},{8,2},{9,10},{10... | collective-permute-start | bytes 786440 | tf_op jit(solution)/shard_map/ppermute | solution.py:471
  142.8 13.5 %collective-permute-start.36 = (bf16[2,4,128,128]{3,2,1,0:T(8,128)(2,1)S(1)}, bf16[2,4,128,128]{3,2,1,0:T(8,128)(2,1)S(1)}, u32[]{:S(2)}, u32[]{:S(2)}) collective-permute-start(bf16[2,4,128,128]{3,2,1,0:T(8,128)(2,1)S(1)} %shard_map.139), channel_id=1, source_target_pairs={{0,0},{1,8},{2,4},{3,12},{4,5},{5,13},{6,1},{7,9},{8,2},{9,10},{10... | collective-permute-start | bytes 786440 | tf_op jit(solution)/shard_map/ppermute | solution.py:471
  (20 other events, 175.3 us)
